TPU v7x, 32 devices: a whole 2x2x4 slice. The times are simulated.
32 devices in a mesh: shard: 8 (over y, x, core), tensor: 4 (over z).
Axes of the slice: x: 2, y: 2, z: 4, core: 2. Of those that a mesh axis runs over, the one named last changes fastest.
Arguments:
- step: int32 [1], replicated, may hold values from 1 to 19
- lengths: int32 [80], replicated, may hold values from 1 to 262144, 2097152 in all
- grads: bfloat16 [8, 8, 4, 65536], P('shard', None, 'tensor'), may hold values from -2 to 2
- weights: float32 [2097152], P(('shard', 'tensor'))
- moment1: float32 [2097152], P(('shard', 'tensor')), may hold values from -0.4375 to 0.4375
- moment2: float32 [2097152], P(('shard', 'tensor')), may hold values from 0.0001 to 0.01
Outputs:
- new_weights: float32 [2097152], P(('shard', 'tensor'))
- new_moment1: float32 [2097152], P(('shard', 'tensor'))
- new_moment2: float32 [2097152], P(('shard', 'tensor'))
- train_weights: bfloat16 [8, 4, 65536], P(None, 'tensor')
Inputs may be any that keep to these rules, and one draw needn't show every extreme that they name: The lengths sum to 2097152, and one of them equals 262144.
All inputs are finite; a program needn't handle non-finite values.
Results may differ from a plain program's by a relative error of at most 0.0004.
Values may be sent and summed in bfloat16 or wider, within the bound.
No kernel may reach another device: no remote copies, remote signals or barrier semaphores. Data moves between devices by JAX's collectives and lax.ppermute only.
A program may use at most 128 MiB of HBM per device.

v0:
```python
import math

import jax
import jax.numpy as jnp
from jax import lax
from jax.sharding import PartitionSpec as P


def segment_squares(columns, base, starts, ends):
    width = columns.shape[1]
    block = math.gcd(width, 8192)
    blocks = width // block
    pieces = columns.reshape(columns.shape[0], blocks, block).transpose(1, 0, 2)
    places = base + jnp.arange(width, dtype=jnp.int32).reshape(blocks, block)

    def add_block(total, item):
        piece, place = item
        member = ((place[None, :] >= starts[:, None]) & (place[None, :] < ends[:, None])).astype(
            jnp.float32
        )
        return (total + jnp.dot(member, piece.T, precision=lax.Precision.HIGHEST), None)

    init = jnp.zeros((starts.shape[0], columns.shape[0]), jnp.float32)
    total, unused = lax.scan(add_block, init, (pieces, places))
    return total


def spread_ratio(ratio, base, starts, ends, width):
    block = math.gcd(width, 8192)
    blocks = width // block
    places = base + jnp.arange(width, dtype=jnp.int32).reshape(blocks, block)

    def expand(carry, place):
        member = ((place[None, :] >= starts[:, None]) & (place[None, :] < ends[:, None])).astype(
            jnp.float32
        )
        return (carry, jnp.dot(ratio[None, :], member, precision=lax.Precision.HIGHEST)[0])

    unused, rows = lax.scan(expand, jnp.float32(0.0), places)
    return rows.reshape(width)


def local(step, lengths, grads, weights, moment1, moment2):
    width = weights.shape[0]
    base = (lax.axis_index("shard") * lax.axis_size("tensor") + lax.axis_index("tensor")) * width
    ends = jnp.cumsum(lengths)
    starts = ends - lengths
    flat_grads = grads.reshape(-1)
    grad = lax.psum_scatter(
        flat_grads.astype(jnp.float32), "shard", scatter_dimension=0, tiled=True
    )
    count = step[0].astype(jnp.float32)
    first = 1.0 - jnp.power(jnp.float32(0.9), count)
    second = 1.0 - jnp.power(jnp.float32(0.999), count)
    new_moment1 = 0.9 * moment1 + 0.1 * grad
    new_moment2 = 0.999 * moment2 + 0.001 * grad * grad
    update = new_moment1 / first / (jnp.sqrt(new_moment2 / second) + 1e-06) + 0.1 * weights
    stacked = jnp.stack([weights * weights, update * update])
    partial_value = segment_squares(stacked, base, starts, ends)
    wsq, usq = lax.psum((partial_value[:, 0], partial_value[:, 1]), ("shard", "tensor"))
    ratio = jnp.sqrt(wsq) / jnp.maximum(jnp.sqrt(usq), 1.0)
    local_ratio = spread_ratio(ratio, base, starts, ends, width)
    new_weights = weights - 0.25 * local_ratio * update
    rounded = new_weights.astype(jnp.bfloat16).reshape(1, 1, width)
    train_weights = lax.all_gather(rounded, "shard", axis=0, tiled=True)
    return (new_weights, new_moment1, new_moment2, train_weights)


def solution(mesh):
    placed = (
        P(),
        P(),
        P("shard", None, "tensor", None),
        P(("shard", "tensor")),
        P(("shard", "tensor")),
        P(("shard", "tensor")),
    )
    return jax.shard_map(
        local,
        mesh=mesh,
        in_specs=placed,
        out_specs=(
            P(("shard", "tensor")),
            P(("shard", "tensor")),
            P(("shard", "tensor")),
            P(None, "tensor", None),
        ),
        check_vma=False,
    )
```

profile of v0, /device:TPU:0, one launch (start us, length us, event | category | flops | bytes accessed | tf_op | source)
XLA Modules:
  0.0 172.9 jit_solution(6423546391148193087)
XLA Ops:
  7.2 0.0 all-reduce.4.cloned.1.call-start
  7.2 1.4 convert_bitcast_fusion
  8.6 1.7 copy.13
  10.3 0.0 copy-start.4
  10.3 0.0 all-reduce.4.cloned.1.call-update
  10.3 0.0 all-gather.3.cloned.1.call-start
  11.2 0.0 copy-done.5
  11.2 0.1 copy.12
  11.3 0.1 reduce-window.9
  11.4 0.1 reduce
  11.6 0.6 dynamic-slice
  12.9 62.5 %all-reduce.4.cloned.1.call-done = f32[524288]{0:T(1024)} async-done(((f32[524288]{0:T(1024)}), f32[524288]{0:T(1024)}) %all-reduce.4.cloned.1.call-update) | async-done | bytes 2097168
  75.4 1.2 fusion.14
  76.5 0.0 copy-start.1
  76.6 0.0 copy-start.2
  76.6 0.5 maximum_bitcast_fusion
  77.0 12.3 %while.22 = (s32[]{:T(128)}, f32[80,2]{0,1:T(2,128)S(1)}, s32[8,8192]{1,0:T(8,128)S(1)}, s32[80]{0:T(128)S(1)}, s32[80]{0:T(128)S(1)}, /*index=5*/f32[8,2,8192]{2,1,0:T(2,128)S(1)}, s32[]{:T(128)}, s32[]{:T(128)}) while((s32[]{:T(128)}, f32[80,2]{0,1:T(2,128)S(1)}, s32[8,8192]{1,0:T(8,128)S(1)}, s32[80]{0:T(128)S(1)}, ...), condition=%wide.region_3.4_spmd.clone, body=%wide.region_2.3_spmd.clone.sunk | while | flops 17695044 | bytes 166631 | solution.py:24
  77.1 1.5 fusion.24
  78.6 1.5 fusion.24
  80.2 1.5 fusion.24
  81.7 1.5 fusion.24
  83.2 1.5 fusion.24
  84.8 1.5 fusion.24
  86.3 1.5 fusion.24
  87.9 1.5 fusion.24
  89.4 39.4 %all-reduce.1 = (f32[80]{0:T(128)S(1)}, f32[80]{0:T(128)S(1)}) all-reduce(f32[80]{0:T(128)S(1)} %get-tuple-element.124, f32[80]{0:T(128)S(1)} %get-tuple-element.123), channel_id=1, replica_groups=mesh['shard'=8,'tensor'=4] {'shard','tensor'}, use_global_device_ids=true, to_apply=%region_5.6 | all-reduce | flops 160 | bytes 1280 | tf_op jit(solution)/shard_map/psum | solution.py:60
  128.7 10.2 %while.21 = (s32[]{:T(128)}, f32[8,8192]{1,0:T(8,128)S(1)}, s32[8,8192]{1,0:T(8,128)S(1)}, s32[80]{0:T(128)S(1)}, s32[80]{0:T(128)S(1)}, /*index=5*/f32[80]{0:T(128)S(1)}, s32[]{:T(128)}, s32[]{:T(128)}) while((s32[]{:T(128)}, f32[8,8192]{1,0:T(8,128)S(1)}, s32[8,8192]{1,0:T(8,128)S(1)}, s32[80]{0:T(128)S(1)}, s32[80]{0:T(128)S(1)}, ...), condition=%wide.region_7.8_spmd, body=%wide.region_6.7_spmd.sunk | while | flops 9830402 | bytes 197661 | solution.py:39
  128.8 1.1 fusion.22
  129.9 0.1 dynamic_update_slice.5
  130.1 1.1 fusion.22
  131.1 0.1 dynamic_update_slice.5
  131.3 1.1 fusion.22
  132.4 0.1 dynamic_update_slice.5
  132.6 1.1 fusion.22
  133.7 0.1 dynamic_update_slice.5
  133.9 1.1 fusion.22
  134.9 0.1 dynamic_update_slice.5
  135.1 1.1 fusion.22
  136.2 0.1 dynamic_update_slice.5
  136.4 1.1 fusion.22
  137.5 0.1 dynamic_update_slice.5
  137.7 1.1 fusion.22
  138.7 0.1 dynamic_update_slice.5
  138.9 0.1 copy.14
  139.0 0.9 fusion.15
  139.9 0.0 all-gather.3.cloned.1.call-update
  140.0 23.5 %all-gather.3.cloned.1.call-done = bf16[524288]{0:T(1024)(128)(2,1)} async-done(((bf16[65536]{0:T(1024)(128)(2,1)}), bf16[524288]{0:T(1024)(128)(2,1)}) %all-gather.3.cloned.1.call-update) | async-done | bytes 1048592 | tf_op jit(solution)/shard_map/all_gather | solution.py:65
  163.5 2.6 %reshape.79 = bf16[8,1,65536]{2,0,1:T(8,128)(2,1)} reshape(bf16[524288]{0:T(1024)(128)(2,1)} %all-gather.3.cloned.1.call-done) | data formatting | bytes 2097152 | tf_op jit(solution)/shard_map/all_gather | solution.py:65
  (33 shorter events, 0.5 us)
Async XLA Ops:
  7.2 68.2 %all-reduce.4.cloned.1.call-start = ((), (), s32[]{:S(2)}) async-start(), calls=%async_computation.1 | async-start | bytes 4194304
  10.3 0.9 copy-start.5
  10.3 1.3 copy-start.6
  10.3 65.1 %copy-start = (f32[65536]{0:T(1024)S(1)}, f32[65536]{0:T(1024)}, u32[]{:S(2)}) copy-start(f32[65536]{0:T(1024)} %param.13) | copy-start | bytes 786436
  10.3 65.1 %copy-start.3 = (f32[65536]{0:T(1024)S(1)}, f32[65536]{0:T(1024)}, u32[]{:S(2)}) copy-start(f32[65536]{0:T(1024)} %param.15) | copy-start | bytes 786436
  10.3 65.1 %copy-start.4 = (f32[65536]{0:T(1024)S(1)}, f32[65536]{0:T(1024)}, u32[]{:S(2)}) copy-start(f32[65536]{0:T(1024)} %param.14) | copy-start | bytes 786436
  10.3 153.2 %all-gather.3.cloned.1.call-start = ((), (), s32[]{:S(2)}) async-start(), calls=%async_computation | async-start | bytes 1179648 | tf_op jit(solution)/shard_map/all_gather | solution.py:65
  76.5 62.5 %copy-start.1 = (f32[65536]{0:T(1024)}, f32[65536]{0:T(1024)S(1)}, u32[]{:S(2)}) copy-start(f32[65536]{0:T(1024)S(1)} %get-tuple-element.120) | copy-start | bytes 786436
  76.6 62.5 %copy-start.2 = (f32[65536]{0:T(1024)}, f32[65536]{0:T(1024)S(1)}, u32[]{:S(2)}) copy-start(f32[65536]{0:T(1024)S(1)} %get-tuple-element.121) | copy-start | bytes 786436
Sparse Core Ops, SparseCore 0:
  11.2 64.0 all-reduce.3
  140.1 23.3 all-gather.2
where the time goes:
time: 173 us
  waiting for transfers between devices  86.1 us (50%)
  blocking collectives  39.4 us (23%)
  matrix products  20.4 us (12%)
  between operations  15.7 us (9%)
  local copies, waits for them, and re-layouts  6.7 us (4%)
  other arithmetic  4.19 us (2%)
    unnamed x3, waiting for transfers between devices  62.5 us
    psum x1, blocking collectives, local(): lax.psum((partial_value[:, 0], partial_value[:, 1]), ('shard', 'tensor'))  39.4 us
    all_gather x1, waiting for transfers between devices, local(): train_weights = lax.all_gather(rounded, 'shard', axis=0, tiled=True)  23.5 us
    dot_general x8, matrix products, add_block(): jnp.dot(member, piece.T, precision=lax.Precision.HIGHEST)  11.8 us
    dot_general x8, matrix products, expand(): jnp.dot(ratio[None, :], member, precision=lax.Precision.HIGHEST)[0]  8.56 us
  transfers between devices with their start and end apart: 2, of which 2 were waited for; matrix products, arithmetic and copies ran while one was open for 1% of the time, Pallas kernels for 0%

commit v1 on v0

v1 whole, which is shorter than its diff:
```python
import functools

import jax
import jax.numpy as jnp
from jax import lax
from jax.experimental import pallas as pl
from jax.experimental.pallas import tpu as pltpu
from jax.sharding import PartitionSpec as P

LANES = 128
VMEM = pl.BlockSpec(memory_space=pltpu.VMEM)
SMEM = pl.BlockSpec(memory_space=pltpu.SMEM)
BIG = pltpu.CompilerParams(vmem_limit_bytes=48 << 20)


def split_kernel(n, chunks, grads_ref, *rest):
    outs, wide = rest[:n], rest[n]
    me = lax.axis_index("shard")
    wide[...] = grads_ref[...].astype(jnp.float32).reshape(wide.shape)
    for k in range(n):
        row = me ^ k
        first = (row // 8) * (chunks * 8) + row % 8
        outs[k][...] = wide[pl.ds(first, chunks, stride=8), :].astype(jnp.bfloat16)


def join_kernel(n, chunks, *rest):
    ins, out_ref, wide = rest[:n], rest[n], rest[n + 1]
    me = lax.axis_index("shard")
    for k in range(n):
        row = me ^ k
        first = (row // 8) * (chunks * 8) + row % 8
        wide[pl.ds(first, chunks, stride=8), :] = ins[k][...].astype(jnp.float32)
    out_ref[...] = wide[...].reshape(out_ref.shape).astype(jnp.bfloat16)


def segment_rows(squares, table, bounds):
    tile = lax.broadcasted_iota(jnp.int32, (8, LANES), 0) * LANES
    tile = tile + lax.broadcasted_iota(jnp.int32, (8, LANES), 1)
    table[...] = jnp.zeros_like(table)
    count = bounds.shape[0] - 3

    def segment(k, carry):
        low, high = bounds[k], bounds[k + 1]

        def step(t, total):
            place = tile + t * (8 * LANES)
            piece = squares[pl.ds(pl.multiple_of(t * 8, 8), 8), :]
            return total + jnp.where((place >= low) & (place < high), piece, 0.0)

        total = lax.fori_loop(
            low // (8 * LANES),
            (high + (8 * LANES - 1)) // (8 * LANES),
            step,
            jnp.zeros((8, LANES), jnp.float32),
        )
        table[pl.ds(k, 1), :] = jnp.sum(total, axis=0, keepdims=True)
        return carry

    lax.fori_loop(bounds[count + 1], bounds[count + 2], segment, 0)


def weights_kernel(lengths_ref, weights_ref, sums_ref, bounds_ref, squares, table):
    chunks = weights_ref.shape[0]
    width = chunks * LANES
    count = lengths_ref.shape[0]
    index = lax.axis_index("shard") * lax.axis_size("tensor") + lax.axis_index("tensor")
    base = index * width

    def walk(k, carry):
        at, first, last = carry
        bounds_ref[k] = jnp.clip(at, 0, width)
        then = at + lengths_ref[k]
        first = jnp.where(then <= 0, k + 1, first)
        last = jnp.where(at < width, k + 1, last)
        return (then, first, last)

    at, first, last = lax.fori_loop(
        0, count, walk, (-base, jnp.int32(0), jnp.int32(0))
    )
    bounds_ref[count] = jnp.clip(at, 0, width)
    bounds_ref[count + 1] = first
    bounds_ref[count + 2] = last
    squares[...] = weights_ref[...] * weights_ref[...]
    segment_rows(squares, table, bounds_ref)
    sums_ref[...] = jnp.sum(table[...].T, axis=0, keepdims=True)


def update_kernel(n, step_ref, bounds_ref, sums_ref, weights_ref, moment1_ref, moment2_ref, *rest):
    pieces = rest[:n]
    new1_ref, new2_ref, update_ref, send_ref = rest[n : n + 4]
    squares, table = rest[n + 4 :]

    def power(base):
        return lax.fori_loop(
            0, step_ref[0], lambda i, p: p * base, jnp.full((8, LANES), 1.0, jnp.float32)
        )

    scale1 = (1.0 / (1.0 - power(jnp.float32(0.9))))[0:1, :]
    scale2 = (1.0 / (1.0 - power(jnp.float32(0.999))))[0:1, :]
    grad = pieces[0][...].astype(jnp.float32)
    for piece in pieces[1:]:
        grad = grad + piece[...].astype(jnp.float32)
    new1 = 0.9 * moment1_ref[...] + 0.1 * grad
    new2 = 0.999 * moment2_ref[...] + 0.001 * grad * grad
    new1_ref[...] = new1
    new2_ref[...] = new2
    update = (new1 * scale1) / (jnp.sqrt(new2 * scale2) + 1e-06) + 0.1 * weights_ref[...]
    update_ref[...] = update
    squares[...] = update * update
    segment_rows(squares, table, bounds_ref)
    mine = jnp.sum(table[...].T, axis=0, keepdims=True)
    which = lax.broadcasted_iota(jnp.int32, (8, LANES), 0)
    both = jnp.where(which == 0, sums_ref[...], jnp.where(which == 1, mine, 0.0))
    send_ref[...] = jnp.broadcast_to(both[None], send_ref.shape)


def weights_out_kernel(
    bounds_ref, sums_ref, weights_ref, update_ref, new_ref, narrow_ref, table, spread
):
    chunks = weights_ref.shape[0]
    count = bounds_ref.shape[0] - 3
    both = jnp.sum(sums_ref[...], axis=0)
    ratio = 0.25 * (jnp.sqrt(both[0:1, :]) / jnp.maximum(jnp.sqrt(both[1:2, :]), 1.0))
    table[...] = jnp.broadcast_to(ratio, (LANES, LANES)).T
    place = lax.broadcasted_iota(jnp.int32, (chunks, LANES), 0) * LANES
    place = place + lax.broadcasted_iota(jnp.int32, (chunks, LANES), 1)
    first = bounds_ref[count + 1]
    spread[...] = jnp.broadcast_to(table[pl.ds(first, 1), :], spread.shape)

    def segment(k, carry):
        spread[...] = jnp.where(place >= bounds_ref[k], table[pl.ds(k, 1), :], spread[...])
        return carry

    lax.fori_loop(first + 1, bounds_ref[count + 2], segment, 0)
    new = weights_ref[...] - spread[...] * update_ref[...]
    new_ref[...] = new
    narrow_ref[...] = new.astype(jnp.bfloat16)


def swap(value, axis, size, k):
    return lax.ppermute(value, axis, [(i, i ^ k) for i in range(size)])


def local(step, lengths, grads, weights, moment1, moment2):
    n = lax.axis_size("shard")
    everyone = n * lax.axis_size("tensor")
    width = weights.shape[0]
    chunks = width // LANES
    count = lengths.shape[0]
    flat = lambda dtype: jax.ShapeDtypeStruct((chunks, LANES), dtype)
    rows = grads.reshape(n // 8, 8, chunks, LANES).transpose(0, 2, 1, 3)
    pieces = pl.pallas_call(
        functools.partial(split_kernel, n, chunks),
        out_shape=[flat(jnp.bfloat16)] * n,
        in_specs=[VMEM],
        out_specs=[VMEM] * n,
        scratch_shapes=[pltpu.VMEM((n * chunks, LANES), jnp.float32)],
        compiler_params=BIG,
        name="split",
    )(rows)
    pieces = [pieces[0]] + [swap(pieces[k], "shard", n, k) for k in range(1, n)]
    weights = weights.reshape(chunks, LANES)
    moment1 = moment1.reshape(chunks, LANES)
    moment2 = moment2.reshape(chunks, LANES)
    square_table = [
        pltpu.VMEM((chunks, LANES), jnp.float32),
        pltpu.VMEM((LANES, LANES), jnp.float32),
    ]
    sums, bounds = pl.pallas_call(
        weights_kernel,
        out_shape=[
            jax.ShapeDtypeStruct((1, LANES), jnp.float32),
            jax.ShapeDtypeStruct((count + 3,), jnp.int32),
        ],
        in_specs=[SMEM, VMEM],
        out_specs=[VMEM, SMEM],
        scratch_shapes=square_table,
        compiler_params=BIG,
        cost_estimate=pl.CostEstimate(flops=8 * width, bytes_accessed=4 * width, transcendentals=0),
        name="weight_squares",
    )(lengths, weights)
    new1, new2, update, send = pl.pallas_call(
        functools.partial(update_kernel, n),
        out_shape=[flat(jnp.float32)] * 3
        + [jax.ShapeDtypeStruct((everyone, 8, LANES), jnp.float32)],
        in_specs=[SMEM, SMEM] + [VMEM] * (4 + n),
        out_specs=[VMEM] * 4,
        scratch_shapes=square_table,
        compiler_params=BIG,
        name="update",
    )(step, bounds, sums, weights, moment1, moment2, *pieces)
    sums = lax.all_to_all(send, ("shard", "tensor"), 0, 0, tiled=True)
    new, narrow = pl.pallas_call(
        weights_out_kernel,
        out_shape=[flat(jnp.float32), flat(jnp.bfloat16)],
        in_specs=[SMEM, VMEM, VMEM, VMEM],
        out_specs=[VMEM] * 2,
        scratch_shapes=[
            pltpu.VMEM((LANES, LANES), jnp.float32),
            pltpu.VMEM((chunks, LANES), jnp.float32),
        ],
        compiler_params=BIG,
        name="new_weights",
    )(bounds, sums, weights, update)
    gathered = {0: narrow}
    for k in range(2, n, 2):
        gathered[k] = swap(narrow, "shard", n, k)
    for k in range(0, n, 2):
        gathered[k + 1] = swap(gathered[k], "shard", n, 1)
    joined = pl.pallas_call(
        functools.partial(join_kernel, n, chunks),
        out_shape=jax.ShapeDtypeStruct((n // 8, chunks, 8, LANES), jnp.bfloat16),
        in_specs=[VMEM] * n,
        out_specs=VMEM,
        scratch_shapes=[pltpu.VMEM((n * chunks, LANES), jnp.float32)],
        compiler_params=BIG,
        name="join",
    )(*[gathered[k] for k in range(n)])
    train = joined.transpose(0, 2, 1, 3).reshape(n, 1, width)
    return (new.reshape(width), new1.reshape(width), new2.reshape(width), train)


def solution(mesh):
    whole = P(("shard", "tensor"))
    return jax.shard_map(
        local,
        mesh=mesh,
        in_specs=(P(), P(), P("shard", None, "tensor", None), whole, whole, whole),
        out_specs=(whole, whole, whole, P(None, "tensor", None)),
        check_vma=False,
    )
```

time: 173 us -> 48.9 us (0.28)
  waiting for transfers between devices: 86.1 us -> 9.91 us
  blocking collectives: 39.4 us -> 14.4 us
  matrix products: 20.4 us -> 0 us
  between operations: 15.7 us -> 1.37 us
  starting transfers between devices: 0.08 us -> 13.1 us
  Pallas kernels: 0 us -> 8.6 us
  local copies, waits for them, and re-layouts: 6.7 us -> 1.24 us
  other arithmetic: 4.19 us -> 0 us
    unnamed x3 -> x0, waiting for transfers between devices: 62.5 us -> none
    psum x1 -> x0, blocking collectives: 39.4 us -> none  [local(): lax.psum((partial_value[:, 0], partial_value[:, 1]), ('shard', 'tensor'))]
    all_gather x1 -> x0, waiting for transfers between devices: 23.5 us -> none  [local(): train_weights = lax.all_gather(rounded, 'shard', axis=0, tiled=True)]
    dot_general x16 -> x0, matrix products: 20.4 us -> none  [the longest x8 11.8 us: add_block(): jnp.dot(member, piece.T, precision=lax.Precision.HIGHEST)]
    all_to_all x0 -> x1, blocking collectives: none -> 14.4 us  [local(): sums = lax.all_to_all(send, ('shard', 'tensor'), 0, 0, tiled=True)]
    ppermute x0 -> x14, starting transfers between devices: none -> 13.1 us  [swap(): return lax.ppermute(value, axis, [(i, i ^ k) for i in range(size)])]
    ppermute x0 -> x14, waiting for transfers between devices: none -> 9.91 us  [swap(): return lax.ppermute(value, axis, [(i, i ^ k) for i in range(size)])]
    pallas_call x0 -> x5, Pallas kernels: none -> 8.6 us  [the longest x1 2.34 us: local(): pl.pallas_call(weights_kernel, out_shape=[jax.ShapeDtypeStruct((1, LANES)...]
  transfers between devices with their start and end apart: 2 -> 14, of which waited for: 2 -> 5; matrix products, arithmetic and copies ran while one was open for 1% -> 0% of each run, Pallas kernels for 0% -> 5%
where the time goes in v1:
time: 48.9 us; the launch traced here: 48.6 us
  blocking collectives  14.4 us (29%)
  starting transfers between devices  13.1 us (27%)
  waiting for transfers between devices  9.91 us (20%)
  Pallas kernels  8.6 us (18%)
  between operations  1.37 us (3%)
  local copies, waits for them, and re-layouts  1.24 us (3%)
    all_to_all x1, blocking collectives, local(): sums = lax.all_to_all(send, ('shard', 'tensor'), 0, 0, tiled=True)  14.4 us
    ppermute x14, starting transfers between devices, swap(): return lax.ppermute(value, axis, [(i, i ^ k) for i in range(size)])  13.1 us
    ppermute x14, waiting for transfers between devices, swap(): return lax.ppermute(value, axis, [(i, i ^ k) for i in range(size)])  9.91 us
    pallas_call x1, Pallas kernels, local(): pl.pallas_call(weights_kernel, out_shape=[jax.ShapeDtypeStruct((1, LANES)...  2.34 us
    pallas_call x1, Pallas kernels, local(): pl.pallas_call(functools.partial(update_kernel, n), out_shape=[flat(jnp.f...  2.28 us
    pallas_call x1, Pallas kernels, local(): pl.pallas_call(functools.partial(join_kernel, n, chunks), out_shape=jax.S...  1.65 us
    pallas_call x1, Pallas kernels, local(): pl.pallas_call(weights_out_kernel, out_shape=[flat(jnp.float32), flat(jnp...  1.65 us
    unnamed x10, local copies, waits for them, and re-layouts  1.24 us
  transfers between devices with their start and end apart: 14, of which 5 were waited for; matrix products, arithmetic and copies ran while one was open for 0% of the time, Pallas kernels for 5%

profile of v1, /device:TPU:0, one launch (start us, length us, event | category | flops | bytes accessed | tf_op | source)
XLA Modules:
  0.0 48.6 jit_solution(5862290695398600154)
XLA Ops:
  0.6 0.0 copy-start.1
  0.6 1.2 %copy-done.1 = bf16[1,8,1,65536]{3,1,2,0:T(8,128)(2,1)S(1)} copy-done((bf16[1,8,1,65536]{3,1,2,0:T(8,128)(2,1)S(1)}, bf16[1,8,1,65536]{3,1,2,0:T(8,128)(2,1)}, u32[]{:S(2)}) %copy-start.1) | copy-done | bytes 1048600
  1.9 0.0 copy-start
  1.9 0.0 copy-start.4
  1.9 0.0 copy-start.3
  1.9 0.7 %split.1 = (bf16[512,128]{1,0:T(8,128)(2,1)S(1)}, bf16[512,128]{1,0:T(8,128)(2,1)S(1)}, bf16[512,128]{1,0:T(8,128)(2,1)S(1)}, bf16[512,128]{1,0:T(8,128)(2,1)S(1...) custom-call(bf16[1,512,8,128]{3,2,1,0:T(8,128)(2,1)S(1)} %bitcast.15), custom_call_target="tpu_custom_call" | custom-call | tf_op jit(solution)/shard_map/split/pallas_call | solution.py:152
  2.6 0.0 copy-start.2
  2.6 0.5 %collective-permute-start = (bf16[512,128]{1,0:T(8,128)(2,1)S(1)}, bf16[512,128]{1,0:T(8,128)(2,1)S(1)}, u32[]{:S(2)}, u32[]{:S(2)}) collective-permute-start(bf16[512,128]{1,0:T(8,128)(2,1)S(1)} %get-tuple-element.23), channel_id=1, source_target_pairs={{0,4},{4,0},{8,12},{12,8},{16,20},{20,16},{24,28},{28,24},{1,5},{5... | collective-permute-start | bytes 393224 | tf_op jit(solution)/shard_map/ppermute | solution.py:141
  3.1 2.6 %collective-permute-start.1 = (bf16[512,128]{1,0:T(8,128)(2,1)S(1)}, bf16[512,128]{1,0:T(8,128)(2,1)S(1)}, u32[]{:S(2)}, u32[]{:S(2)}) collective-permute-start(bf16[512,128]{1,0:T(8,128)(2,1)S(1)} %get-tuple-element.24), channel_id=1, source_target_pairs={{0,8},{4,12},{8,0},{12,4},{16,24},{20,28},{24,16},{28,20},{1,9},{5... | collective-permute-start | bytes 393224 | tf_op jit(solution)/shard_map/ppermute | solution.py:141
  5.7 0.1 collective-permute-start.2
  5.7 1.8 %collective-permute-start.3 = (bf16[512,128]{1,0:T(8,128)(2,1)S(1)}, bf16[512,128]{1,0:T(8,128)(2,1)S(1)}, u32[]{:S(2)}, u32[]{:S(2)}) collective-permute-start(bf16[512,128]{1,0:T(8,128)(2,1)S(1)} %get-tuple-element.26), channel_id=1, source_target_pairs={{0,16},{4,20},{8,24},{12,28},{16,0},{20,4},{24,8},{28,12},{1,17},{... | collective-permute-start | bytes 393224 | tf_op jit(solution)/shard_map/ppermute | solution.py:141
  7.5 0.0 collective-permute-start.4
  7.5 0.0 collective-permute-done.rest_1_
  7.5 2.6 %collective-permute-start.5 = (bf16[512,128]{1,0:T(8,128)(2,1)S(1)}, bf16[512,128]{1,0:T(8,128)(2,1)S(1)}, u32[]{:S(2)}, u32[]{:S(2)}) collective-permute-start(bf16[512,128]{1,0:T(8,128)(2,1)S(1)} %get-tuple-element.28), channel_id=1, source_target_pairs={{0,24},{4,28},{8,16},{12,20},{16,8},{20,12},{24,0},{28,4},{1,25},{... | collective-permute-start | bytes 393224 | tf_op jit(solution)/shard_map/ppermute | solution.py:141
  10.1 0.0 collective-permute-done.1.rest_2_
  10.1 1.6 %collective-permute-start.6 = (bf16[512,128]{1,0:T(8,128)(2,1)S(1)}, bf16[512,128]{1,0:T(8,128)(2,1)S(1)}, u32[]{:S(2)}, u32[]{:S(2)}) collective-permute-start(bf16[512,128]{1,0:T(8,128)(2,1)S(1)} %get-tuple-element.29), channel_id=1, source_target_pairs={{0,28},{4,24},{8,20},{12,16},{16,12},{20,8},{24,4},{28,0},{1,29},{... | collective-permute-start | bytes 393224 | tf_op jit(solution)/shard_map/ppermute | solution.py:141
  12.4 0.0 copy-done
  12.4 0.0 copy-done.4
  12.4 2.3 %weight_squares.1 = (f32[1,128]{1,0:T(1,128)S(1)}, s32[83]{0:T(128)S(1)}) custom-call(s32[80]{0:T(128)S(1)} %copy-done.4, f32[512,128]{1,0:T(8,128)S(1)} %bitcast.12), custom_call_target="tpu_custom_call" | custom-call | flops 524288 | bytes 262144 | tf_op jit(solution)/shard_map/weight_squares/pallas_call | solution.py:169
  14.7 0.0 collective-permute-done.2.rest_3_
  14.8 0.0 collective-permute-done.3.rest_4_
  14.8 4.4 %collective-permute-done.4.rest_5_ = bf16[512,128]{1,0:T(8,128)(2,1)S(1)} collective-permute-done((bf16[512,128]{1,0:T(8,128)(2,1)S(1)}, bf16[512,128]{1,0:T(8,128)(2,1)S(1)}, u32[]{:S(2)}, u32[]{:S(2)}) %collective-permute-start.4) | collective-permute-done | bytes 131104 | tf_op jit(solution)/shard_map/ppermute | solution.py:141
  19.2 0.0 collective-permute-done.5.rest_6_
  19.2 0.0 collective-permute-done.6.rest_7_
  19.2 0.0 copy-done.3
  19.2 0.0 copy-done.2
  19.2 2.3 %update.1 = (f32[512,128]{1,0:T(8,128)}, f32[512,128]{1,0:T(8,128)}, f32[512,128]{1,0:T(8,128)S(1)}, f32[32,8,128]{2,1,0:T(8,128)S(1)}) custom-call(s32[1]{0:T(128)S(6)} %copy.10.step_ref, s32[83]{0:T(128)S(1)} %get-tuple-element.20.bounds_ref, f32[1,128]{1,0:T(1,128)S(1)} %get-tuple-element.21.sums_ref, f32[512,128]{1,0:T(8,128)S(1)} %bitcast.13, ...), custom_call_target="tpu_custom_call" | custom-call | tf_op jit(solution)/shard_map/update/pallas_call | solution.py:182
  21.5 14.4 %all_to_all.5.sums_ref = f32[32,8,128]{2,1,0:T(8,128)S(1)} all-to-all(f32[32,8,128]{2,1,0:T(8,128)S(1)} %get-tuple-element.30), channel_id=1, replica_groups=mesh['shard'=8,'tensor'=4] {'shard','tensor'}, dimensions={0} | all-to-all | bytes 262144 | tf_op jit(solution)/shard_map/all_to_all | solution.py:192
  35.8 1.6 %new_weights.1 = (f32[512,128]{1,0:T(8,128)}, bf16[512,128]{1,0:T(8,128)(2,1)S(1)}) custom-call(s32[83]{0:T(128)S(1)} %get-tuple-element.20.bounds_ref, f32[32,8,128]{2,1,0:T(8,128)S(1)} %all_to_all.5.sums_ref, f32[512,128]{1,0:T(8,128)S(1)} %bitcast.14, f32[512,128]{1,0:T(8,128)S(1)} %get-tuple-element.31.update_ref), custom_call_target="tpu_custom_call" | custom-call | tf_op jit(solution)/shard_map/new_weights/pallas_call | solution.py:193
  37.5 0.7 %collective-permute-start.12 = (bf16[512,128]{1,0:T(8,128)(2,1)S(1)}, bf16[512,128]{1,0:T(8,128)(2,1)S(1)}, u32[]{:S(2)}, u32[]{:S(2)}) collective-permute-start(bf16[512,128]{1,0:T(8,128)(2,1)S(1)} %get-tuple-element.35.rest_0_), channel_id=1, source_target_pairs={{0,24},{4,28},{8,16},{12,20},{16,8},{20,12},{24,0},{28,4},{1,25},{... | collective-permute-start | bytes 393224 | tf_op jit(solution)/shard_map/ppermute | solution.py:141
  38.1 1.5 %collective-permute-start.10 = (bf16[512,128]{1,0:T(8,128)(2,1)S(1)}, bf16[512,128]{1,0:T(8,128)(2,1)S(1)}, u32[]{:S(2)}, u32[]{:S(2)}) collective-permute-start(bf16[512,128]{1,0:T(8,128)(2,1)S(1)} %get-tuple-element.35.rest_0_), channel_id=1, source_target_pairs={{0,16},{4,20},{8,24},{12,28},{16,0},{20,4},{24,8},{28,12},{1,17},{... | collective-permute-start | bytes 393224 | tf_op jit(solution)/shard_map/ppermute | solution.py:141
  39.7 1.3 %collective-permute-start.8 = (bf16[512,128]{1,0:T(8,128)(2,1)S(1)}, bf16[512,128]{1,0:T(8,128)(2,1)S(1)}, u32[]{:S(2)}, u32[]{:S(2)}) collective-permute-start(bf16[512,128]{1,0:T(8,128)(2,1)S(1)} %get-tuple-element.35.rest_0_), channel_id=1, source_target_pairs={{0,8},{4,12},{8,0},{12,4},{16,24},{20,28},{24,16},{28,20},{1,9},{5... | collective-permute-start | bytes 393224 | tf_op jit(solution)/shard_map/ppermute | solution.py:141
  41.0 0.0 collective-permute-start.7
  41.0 3.4 %collective-permute-done.12.rest_6_ = bf16[512,128]{1,0:T(8,128)(2,1)S(1)} collective-permute-done((bf16[512,128]{1,0:T(8,128)(2,1)S(1)}, bf16[512,128]{1,0:T(8,128)(2,1)S(1)}, u32[]{:S(2)}, u32[]{:S(2)}) %collective-permute-start.12) | collective-permute-done | bytes 131104 | tf_op jit(solution)/shard_map/ppermute | solution.py:141
  44.3 0.0 collective-permute-start.13
  44.3 1.1 %collective-permute-done.10.rest_4_ = bf16[512,128]{1,0:T(8,128)(2,1)S(1)} collective-permute-done((bf16[512,128]{1,0:T(8,128)(2,1)S(1)}, bf16[512,128]{1,0:T(8,128)(2,1)S(1)}, u32[]{:S(2)}, u32[]{:S(2)}) %collective-permute-start.10) | collective-permute-done | bytes 131104 | tf_op jit(solution)/shard_map/ppermute | solution.py:141
  45.4 0.0 collective-permute-start.11
  45.4 0.0 collective-permute-done.8.rest_2_
  45.4 0.5 %collective-permute-start.9 = (bf16[512,128]{1,0:T(8,128)(2,1)S(1)}, bf16[512,128]{1,0:T(8,128)(2,1)S(1)}, u32[]{:S(2)}, u32[]{:S(2)}) collective-permute-start(bf16[512,128]{1,0:T(8,128)(2,1)S(1)} %collective-permute-done.8.rest_2_), channel_id=1, source_target_pairs={{0,4},{4,0},{8,12},{12,8},{16,20},{20,16},{24,28},{28,24},{1,5},{5... | collective-permute-start | bytes 393224 | tf_op jit(solution)/shard_map/ppermute | solution.py:141
  45.9 0.0 collective-permute-done.7.rest_1_
  45.9 0.0 collective-permute-done.13.rest_7_
  46.0 0.8 %collective-permute-done.11.rest_5_ = bf16[512,128]{1,0:T(8,128)(2,1)S(1)} collective-permute-done((bf16[512,128]{1,0:T(8,128)(2,1)S(1)}, bf16[512,128]{1,0:T(8,128)(2,1)S(1)}, u32[]{:S(2)}, u32[]{:S(2)}) %collective-permute-start.11) | collective-permute-done | bytes 131104 | tf_op jit(solution)/shard_map/ppermute | solution.py:141
  46.8 0.2 collective-permute-done.9.rest_3_
  47.0 1.6 %join.1 = bf16[1,512,8,128]{3,2,1,0:T(8,128)(2,1)} custom-call(bf16[512,128]{1,0:T(8,128)(2,1)S(1)} %get-tuple-element.35.rest_0_, bf16[512,128]{1,0:T(8,128)(2,1)S(1)} %collective-permute-done.7.rest_1_, bf16[512,128]{1,0:T(8,128)(2,1)S(1)} %collective-permute-done.8.rest_2_, bf16[512,128]{1,0:T(8,128)(2,1)S(1)} %collective-permute-done.9.rest_3_, ...), custom_call_target="tpu_custom_call" | custom-call | tf_op jit(solution)/shard_map/join/pallas_call | solution.py:210
Async XLA Ops:
  0.6 1.2 %copy-start.1 = (bf16[1,8,1,65536]{3,1,2,0:T(8,128)(2,1)S(1)}, bf16[1,8,1,65536]{3,1,2,0:T(8,128)(2,1)}, u32[]{:S(2)}) copy-start(bf16[1,8,1,65536]{3,1,2,0:T(8,128)(2,1)} %param.8) | copy-start | bytes 3145732
  1.9 10.5 %copy-start = (f32[65536]{0:T(1024)S(1)}, f32[65536]{0:T(1024)}, u32[]{:S(2)}) copy-start(f32[65536]{0:T(1024)} %param.9) | copy-start | bytes 786436
  1.9 10.5 %copy-start.4 = (s32[80]{0:T(128)S(1)}, s32[80]{0:T(128)}, u32[]{:S(2)}) copy-start(s32[80]{0:T(128)} %lengths_ref.1) | copy-start | bytes 964
  1.9 17.3 %copy-start.3 = (f32[65536]{0:T(1024)S(1)}, f32[65536]{0:T(1024)}, u32[]{:S(2)}) copy-start(f32[65536]{0:T(1024)} %param.11) | copy-start | bytes 786436
  2.6 16.6 %copy-start.2 = (f32[65536]{0:T(1024)S(1)}, f32[65536]{0:T(1024)}, u32[]{:S(2)}) copy-start(f32[65536]{0:T(1024)} %param.10) | copy-start | bytes 786436
  2.6 4.9 %collective-permute-start = (bf16[512,128]{1,0:T(8,128)(2,1)S(1)}, bf16[512,128]{1,0:T(8,128)(2,1)S(1)}, u32[]{:S(2)}, u32[]{:S(2)}) collective-permute-start(bf16[512,128]{1,0:T(8,128)(2,1)S(1)} %get-tuple-element.23), channel_id=1, source_target_pairs={{0,4},{4,0},{8,12},{12,8},{16,20},{20,16},{24,28},{28,24},{1,5},{5... | collective-permute-start | bytes 393224 | tf_op jit(solution)/shard_map/ppermute | solution.py:141
  3.1 7.0 %collective-permute-start.1 = (bf16[512,128]{1,0:T(8,128)(2,1)S(1)}, bf16[512,128]{1,0:T(8,128)(2,1)S(1)}, u32[]{:S(2)}, u32[]{:S(2)}) collective-permute-start(bf16[512,128]{1,0:T(8,128)(2,1)S(1)} %get-tuple-element.24), channel_id=1, source_target_pairs={{0,8},{4,12},{8,0},{12,4},{16,24},{20,28},{24,16},{28,20},{1,9},{5... | collective-permute-start | bytes 393224 | tf_op jit(solution)/shard_map/ppermute | solution.py:141
  5.7 9.1 %collective-permute-start.2 = (bf16[512,128]{1,0:T(8,128)(2,1)S(1)}, bf16[512,128]{1,0:T(8,128)(2,1)S(1)}, u32[]{:S(2)}, u32[]{:S(2)}) collective-permute-start(bf16[512,128]{1,0:T(8,128)(2,1)S(1)} %get-tuple-element.25), channel_id=1, source_target_pairs={{0,12},{4,8},{8,4},{12,0},{16,28},{20,24},{24,20},{28,16},{1,13},{... | collective-permute-start | bytes 393224 | tf_op jit(solution)/shard_map/ppermute | solution.py:141
  5.7 9.0 %collective-permute-start.3 = (bf16[512,128]{1,0:T(8,128)(2,1)S(1)}, bf16[512,128]{1,0:T(8,128)(2,1)S(1)}, u32[]{:S(2)}, u32[]{:S(2)}) collective-permute-start(bf16[512,128]{1,0:T(8,128)(2,1)S(1)} %get-tuple-element.26), channel_id=1, source_target_pairs={{0,16},{4,20},{8,24},{12,28},{16,0},{20,4},{24,8},{28,12},{1,17},{... | collective-permute-start | bytes 393224 | tf_op jit(solution)/shard_map/ppermute | solution.py:141
  7.5 11.7 %collective-permute-start.4 = (bf16[512,128]{1,0:T(8,128)(2,1)S(1)}, bf16[512,128]{1,0:T(8,128)(2,1)S(1)}, u32[]{:S(2)}, u32[]{:S(2)}) collective-permute-start(bf16[512,128]{1,0:T(8,128)(2,1)S(1)} %get-tuple-element.27), channel_id=1, source_target_pairs={{0,20},{4,16},{8,28},{12,24},{16,4},{20,0},{24,12},{28,8},{1,21},{... | collective-permute-start | bytes 393224 | tf_op jit(solution)/shard_map/ppermute | solution.py:141
  7.5 11.7 %collective-permute-start.5 = (bf16[512,128]{1,0:T(8,128)(2,1)S(1)}, bf16[512,128]{1,0:T(8,128)(2,1)S(1)}, u32[]{:S(2)}, u32[]{:S(2)}) collective-permute-start(bf16[512,128]{1,0:T(8,128)(2,1)S(1)} %get-tuple-element.28), channel_id=1, source_target_pairs={{0,24},{4,28},{8,16},{12,20},{16,8},{20,12},{24,0},{28,4},{1,25},{... | collective-permute-start | bytes 393224 | tf_op jit(solution)/shard_map/ppermute | solution.py:141
  10.1 9.1 %collective-permute-start.6 = (bf16[512,128]{1,0:T(8,128)(2,1)S(1)}, bf16[512,128]{1,0:T(8,128)(2,1)S(1)}, u32[]{:S(2)}, u32[]{:S(2)}) collective-permute-start(bf16[512,128]{1,0:T(8,128)(2,1)S(1)} %get-tuple-element.29), channel_id=1, source_target_pairs={{0,28},{4,24},{8,20},{12,16},{16,12},{20,8},{24,4},{28,0},{1,29},{... | collective-permute-start | bytes 393224 | tf_op jit(solution)/shard_map/ppermute | solution.py:141
  37.5 6.9 %collective-permute-start.12 = (bf16[512,128]{1,0:T(8,128)(2,1)S(1)}, bf16[512,128]{1,0:T(8,128)(2,1)S(1)}, u32[]{:S(2)}, u32[]{:S(2)}) collective-permute-start(bf16[512,128]{1,0:T(8,128)(2,1)S(1)} %get-tuple-element.35.rest_0_), channel_id=1, source_target_pairs={{0,24},{4,28},{8,16},{12,20},{16,8},{20,12},{24,0},{28,4},{1,25},{... | collective-permute-start | bytes 393224 | tf_op jit(solution)/shard_map/ppermute | solution.py:141
  38.1 7.3 %collective-permute-start.10 = (bf16[512,128]{1,0:T(8,128)(2,1)S(1)}, bf16[512,128]{1,0:T(8,128)(2,1)S(1)}, u32[]{:S(2)}, u32[]{:S(2)}) collective-permute-start(bf16[512,128]{1,0:T(8,128)(2,1)S(1)} %get-tuple-element.35.rest_0_), channel_id=1, source_target_pairs={{0,16},{4,20},{8,24},{12,28},{16,0},{20,4},{24,8},{28,12},{1,17},{... | collective-permute-start | bytes 393224 | tf_op jit(solution)/shard_map/ppermute | solution.py:141
  39.7 5.8 %collective-permute-start.8 = (bf16[512,128]{1,0:T(8,128)(2,1)S(1)}, bf16[512,128]{1,0:T(8,128)(2,1)S(1)}, u32[]{:S(2)}, u32[]{:S(2)}) collective-permute-start(bf16[512,128]{1,0:T(8,128)(2,1)S(1)} %get-tuple-element.35.rest_0_), channel_id=1, source_target_pairs={{0,8},{4,12},{8,0},{12,4},{16,24},{20,28},{24,16},{28,20},{1,9},{5... | collective-permute-start | bytes 393224 | tf_op jit(solution)/shard_map/ppermute | solution.py:141
  41.0 5.0 %collective-permute-start.7 = (bf16[512,128]{1,0:T(8,128)(2,1)S(1)}, bf16[512,128]{1,0:T(8,128)(2,1)S(1)}, u32[]{:S(2)}, u32[]{:S(2)}) collective-permute-start(bf16[512,128]{1,0:T(8,128)(2,1)S(1)} %get-tuple-element.35.rest_0_), channel_id=1, source_target_pairs={{0,4},{4,0},{8,12},{12,8},{16,20},{20,16},{24,28},{28,24},{1,5},{5... | collective-permute-start | bytes 393224 | tf_op jit(solution)/shard_map/ppermute | solution.py:141
  44.3 1.6 %collective-permute-start.13 = (bf16[512,128]{1,0:T(8,128)(2,1)S(1)}, bf16[512,128]{1,0:T(8,128)(2,1)S(1)}, u32[]{:S(2)}, u32[]{:S(2)}) collective-permute-start(bf16[512,128]{1,0:T(8,128)(2,1)S(1)} %collective-permute-done.12.rest_6_), channel_id=1, source_target_pairs={{0,4},{4,0},{8,12},{12,8},{16,20},{20,16},{24,28},{28,24},{1,5},{5... | collective-permute-start | bytes 393224 | tf_op jit(solution)/shard_map/ppermute | solution.py:141
  45.4 1.3 %collective-permute-start.11 = (bf16[512,128]{1,0:T(8,128)(2,1)S(1)}, bf16[512,128]{1,0:T(8,128)(2,1)S(1)}, u32[]{:S(2)}, u32[]{:S(2)}) collective-permute-start(bf16[512,128]{1,0:T(8,128)(2,1)S(1)} %collective-permute-done.10.rest_4_), channel_id=1, source_target_pairs={{0,4},{4,0},{8,12},{12,8},{16,20},{20,16},{24,28},{28,24},{1,5},{5... | collective-permute-start | bytes 393224 | tf_op jit(solution)/shard_map/ppermute | solution.py:141
  45.4 1.5 %collective-permute-start.9 = (bf16[512,128]{1,0:T(8,128)(2,1)S(1)}, bf16[512,128]{1,0:T(8,128)(2,1)S(1)}, u32[]{:S(2)}, u32[]{:S(2)}) collective-permute-start(bf16[512,128]{1,0:T(8,128)(2,1)S(1)} %collective-permute-done.8.rest_2_), channel_id=1, source_target_pairs={{0,4},{4,0},{8,12},{12,8},{16,20},{20,16},{24,28},{28,24},{1,5},{5... | collective-permute-start | bytes 393224 | tf_op jit(solution)/shard_map/ppermute | solution.py:141

commit v2 on v1

--- a/solution.py
+++ b/solution.py
@@ -1,4 +1,5 @@
 import functools
+import math
 
 import jax
 import jax.numpy as jnp
@@ -8,34 +9,70 @@
 from jax.sharding import PartitionSpec as P
 
 LANES = 128
+TILE = 64
+PARTS = 4
 VMEM = pl.BlockSpec(memory_space=pltpu.VMEM)
 SMEM = pl.BlockSpec(memory_space=pltpu.SMEM)
+HBM = pl.BlockSpec(memory_space=pltpu.HBM)
 BIG = pltpu.CompilerParams(vmem_limit_bytes=48 << 20)
 
 
 def split_kernel(n, chunks, grads_ref, *rest):
-    outs, wide = rest[:n], rest[n]
+    outs, (held, wide, sems) = rest[:n], rest[n:]
     me = lax.axis_index("shard")
-    wide[...] = grads_ref[...].astype(jnp.float32).reshape(wide.shape)
-    for k in range(n):
-        row = me ^ k
-        first = (row // 8) * (chunks * 8) + row % 8
-        outs[k][...] = wide[pl.ds(first, chunks, stride=8), :].astype(jnp.bfloat16)
+    parts, depth = held.shape[0], held.shape[2]
+    copies = []
+    for part in range(parts):
+        source = grads_ref.at[:, pl.ds(part * depth, depth)]
+        copies.append(pltpu.make_async_copy(source, held.at[part], sems.at[part]))
+        copies[-1].start()
+    for part in range(parts):
+        copies[part].wait()
+        wide[part] = held[part].astype(jnp.float32).reshape(wide.shape[1:])
+        for k in range(n):
+            row = me ^ k
+            first = (row // 8) * (depth * 8) + row % 8
+            taken = wide[part, pl.ds(first, depth, stride=8), :]
+            outs[k][part * depth : (part + 1) * depth, :] = taken.astype(jnp.bfloat16)
 
 
 def join_kernel(n, chunks, *rest):
-    ins, out_ref, wide = rest[:n], rest[n], rest[n + 1]
+    ins, out_ref, (held, wide, sems) = rest[:n], rest[n], rest[n + 1 :]
     me = lax.axis_index("shard")
-    for k in range(n):
-        row = me ^ k
-        first = (row // 8) * (chunks * 8) + row % 8
-        wide[pl.ds(first, chunks, stride=8), :] = ins[k][...].astype(jnp.float32)
-    out_ref[...] = wide[...].reshape(out_ref.shape).astype(jnp.bfloat16)
+    parts, depth = held.shape[0], held.shape[2]
+    copies = []
+    for part in range(parts):
+        for k in range(n):
+            row = me ^ k
+            first = (row // 8) * (depth * 8) + row % 8
+            taken = ins[k][part * depth : (part + 1) * depth, :]
+            wide[part, pl.ds(first, depth, stride=8), :] = taken.astype(jnp.float32)
+        held[part] = wide[part].reshape(held.shape[1:]).astype(jnp.bfloat16)
+        target = out_ref.at[:, pl.ds(part * depth, depth)]
+        copies.append(pltpu.make_async_copy(held.at[part], target, sems.at[part]))
+        copies[-1].start()
+    for copy in copies:
+        copy.wait()
+
+
+def store_kernel(new1_ref, new2_ref, new_ref, out1_ref, out2_ref, out_ref, sems):
+    pairs = ((new1_ref, out1_ref), (new2_ref, out2_ref), (new_ref, out_ref))
+    copies = [pltpu.make_async_copy(*pair, sems.at[i]) for i, pair in enumerate(pairs)]
+    for copy in copies:
+        copy.start()
+    for copy in copies:
+        copy.wait()
+
+
+def places(rows):
+    place = lax.broadcasted_iota(jnp.int32, (rows, LANES), 0) * LANES
+    return place + lax.broadcasted_iota(jnp.int32, (rows, LANES), 1)
 
 
 def segment_rows(squares, table, bounds):
-    tile = lax.broadcasted_iota(jnp.int32, (8, LANES), 0) * LANES
-    tile = tile + lax.broadcasted_iota(jnp.int32, (8, LANES), 1)
+    rows = math.gcd(squares.shape[0], TILE)
+    size = rows * LANES
+    place = places(rows)
     table[...] = jnp.zeros_like(table)
     count = bounds.shape[0] - 3
 
@@ -43,15 +80,16 @@
         low, high = bounds[k], bounds[k + 1]
 
         def step(t, total):
-            place = tile + t * (8 * LANES)
-            piece = squares[pl.ds(pl.multiple_of(t * 8, 8), 8), :]
-            return total + jnp.where((place >= low) & (place < high), piece, 0.0)
+            piece = squares[pl.ds(pl.multiple_of(t * rows, rows), rows), :]
+            at = t * size
+            inside = (place >= low - at) & (place < high - at)
+            return total + jnp.where(inside, piece, 0.0)
 
         total = lax.fori_loop(
-            low // (8 * LANES),
-            (high + (8 * LANES - 1)) // (8 * LANES),
+            low // size,
+            (high + (size - 1)) // size,
             step,
-            jnp.zeros((8, LANES), jnp.float32),
+            jnp.zeros((rows, LANES), jnp.float32),
         )
         table[pl.ds(k, 1), :] = jnp.sum(total, axis=0, keepdims=True)
         return carry
@@ -97,44 +135,59 @@
 
     scale1 = (1.0 / (1.0 - power(jnp.float32(0.9))))[0:1, :]
     scale2 = (1.0 / (1.0 - power(jnp.float32(0.999))))[0:1, :]
-    grad = pieces[0][...].astype(jnp.float32)
-    for piece in pieces[1:]:
-        grad = grad + piece[...].astype(jnp.float32)
-    new1 = 0.9 * moment1_ref[...] + 0.1 * grad
-    new2 = 0.999 * moment2_ref[...] + 0.001 * grad * grad
-    new1_ref[...] = new1
-    new2_ref[...] = new2
-    update = (new1 * scale1) / (jnp.sqrt(new2 * scale2) + 1e-06) + 0.1 * weights_ref[...]
-    update_ref[...] = update
-    squares[...] = update * update
+    chunks = weights_ref.shape[0]
+    rows = math.gcd(chunks, TILE)
+
+    def block(t, carry):
+        part = pl.ds(pl.multiple_of(t * rows, rows), rows)
+        grad = pieces[0][part, :].astype(jnp.float32)
+        for piece in pieces[1:]:
+            grad = grad + piece[part, :].astype(jnp.float32)
+        new1 = 0.9 * moment1_ref[part, :] + 0.1 * grad
+        new2 = 0.999 * moment2_ref[part, :] + 0.001 * grad * grad
+        new1_ref[part, :] = new1
+        new2_ref[part, :] = new2
+        update = (new1 * scale1) / (jnp.sqrt(new2 * scale2) + 1e-06)
+        update = update + 0.1 * weights_ref[part, :]
+        update_ref[part, :] = update
+        squares[part, :] = update * update
+        return carry
+
+    lax.fori_loop(0, chunks // rows, block, 0, unroll=2)
     segment_rows(squares, table, bounds_ref)
     mine = jnp.sum(table[...].T, axis=0, keepdims=True)
-    which = lax.broadcasted_iota(jnp.int32, (8, LANES), 0)
-    both = jnp.where(which == 0, sums_ref[...], jnp.where(which == 1, mine, 0.0))
+    which = lax.broadcasted_iota(jnp.int32, (2, LANES), 0)
+    both = jnp.where(which == 0, sums_ref[...], mine)
     send_ref[...] = jnp.broadcast_to(both[None], send_ref.shape)
 
 
 def weights_out_kernel(
-    bounds_ref, sums_ref, weights_ref, update_ref, new_ref, narrow_ref, table, spread
+    bounds_ref, sums_ref, weights_ref, update_ref, new_ref, narrow_ref, table
 ):
     chunks = weights_ref.shape[0]
+    rows = math.gcd(chunks, TILE)
+    size = rows * LANES
+    place = places(rows)
     count = bounds_ref.shape[0] - 3
     both = jnp.sum(sums_ref[...], axis=0)
     ratio = 0.25 * (jnp.sqrt(both[0:1, :]) / jnp.maximum(jnp.sqrt(both[1:2, :]), 1.0))
     table[...] = jnp.broadcast_to(ratio, (LANES, LANES)).T
-    place = lax.broadcasted_iota(jnp.int32, (chunks, LANES), 0) * LANES
-    place = place + lax.broadcasted_iota(jnp.int32, (chunks, LANES), 1)
-    first = bounds_ref[count + 1]
-    spread[...] = jnp.broadcast_to(table[pl.ds(first, 1), :], spread.shape)
 
     def segment(k, carry):
-        spread[...] = jnp.where(place >= bounds_ref[k], table[pl.ds(k, 1), :], spread[...])
-        return carry
-
-    lax.fori_loop(first + 1, bounds_ref[count + 2], segment, 0)
-    new = weights_ref[...] - spread[...] * update_ref[...]
-    new_ref[...] = new
-    narrow_ref[...] = new.astype(jnp.bfloat16)
+        low, high = bounds_ref[k], bounds_ref[k + 1]
+        scale = table[pl.ds(k, 1), :]
+
+        def step(t, carry):
+            part = pl.ds(pl.multiple_of(t * rows, rows), rows)
+            new = weights_ref[part, :] - scale * update_ref[part, :]
+            new = jnp.where(place >= low - t * size, new, new_ref[part, :])
+            new_ref[part, :] = new
+            narrow_ref[part, :] = new.astype(jnp.bfloat16)
+            return carry
+
+        return lax.fori_loop(low // size, (high + (size - 1)) // size, step, carry)
+
+    lax.fori_loop(bounds_ref[count + 1], bounds_ref[count + 2], segment, 0)
 
 
 def swap(value, axis, size, k):
@@ -149,15 +202,22 @@
     count = lengths.shape[0]
     flat = lambda dtype: jax.ShapeDtypeStruct((chunks, LANES), dtype)
     rows = grads.reshape(n // 8, 8, chunks, LANES).transpose(0, 2, 1, 3)
+    parts = math.gcd(PARTS, chunks // 16)
+    depth = chunks // parts
+    staging = [
+        pltpu.VMEM((parts, n // 8, depth, 8, LANES), jnp.bfloat16),
+        pltpu.VMEM((parts, n * depth, LANES), jnp.float32),
+        pltpu.SemaphoreType.DMA((parts,)),
+    ]
     pieces = pl.pallas_call(
         functools.partial(split_kernel, n, chunks),
         out_shape=[flat(jnp.bfloat16)] * n,
-        in_specs=[VMEM],
+        in_specs=[HBM],
         out_specs=[VMEM] * n,
-        scratch_shapes=[pltpu.VMEM((n * chunks, LANES), jnp.float32)],
+        scratch_shapes=staging,
         compiler_params=BIG,
         name="split",
-    )(rows)
+    )(pltpu.with_memory_space_constraint(rows, pltpu.HBM))
     pieces = [pieces[0]] + [swap(pieces[k], "shard", n, k) for k in range(1, n)]
     weights = weights.reshape(chunks, LANES)
     moment1 = moment1.reshape(chunks, LANES)
@@ -182,7 +242,7 @@
     new1, new2, update, send = pl.pallas_call(
         functools.partial(update_kernel, n),
         out_shape=[flat(jnp.float32)] * 3
-        + [jax.ShapeDtypeStruct((everyone, 8, LANES), jnp.float32)],
+        + [jax.ShapeDtypeStruct((everyone, 2, LANES), jnp.float32)],
         in_specs=[SMEM, SMEM] + [VMEM] * (4 + n),
         out_specs=[VMEM] * 4,
         scratch_shapes=square_table,
@@ -195,10 +255,7 @@
         out_shape=[flat(jnp.float32), flat(jnp.bfloat16)],
         in_specs=[SMEM, VMEM, VMEM, VMEM],
         out_specs=[VMEM] * 2,
-        scratch_shapes=[
-            pltpu.VMEM((LANES, LANES), jnp.float32),
-            pltpu.VMEM((chunks, LANES), jnp.float32),
-        ],
+        scratch_shapes=[pltpu.VMEM((LANES, LANES), jnp.float32)],
         compiler_params=BIG,
         name="new_weights",
     )(bounds, sums, weights, update)
@@ -207,12 +264,22 @@
         gathered[k] = swap(narrow, "shard", n, k)
     for k in range(0, n, 2):
         gathered[k + 1] = swap(gathered[k], "shard", n, 1)
+    new1, new2, new = pl.pallas_call(
+        store_kernel,
+        out_shape=[flat(jnp.float32)] * 3,
+        in_specs=[VMEM] * 3,
+        out_specs=[HBM] * 3,
+        scratch_shapes=[pltpu.SemaphoreType.DMA((3,))],
+        compiler_params=BIG,
+        cost_estimate=pl.CostEstimate(flops=0, bytes_accessed=12 * width, transcendentals=0),
+        name="store",
+    )(new1, new2, new)
     joined = pl.pallas_call(
         functools.partial(join_kernel, n, chunks),
         out_shape=jax.ShapeDtypeStruct((n // 8, chunks, 8, LANES), jnp.bfloat16),
         in_specs=[VMEM] * n,
-        out_specs=VMEM,
-        scratch_shapes=[pltpu.VMEM((n * chunks, LANES), jnp.float32)],
+        out_specs=HBM,
+        scratch_shapes=staging,
         compiler_params=BIG,
         name="join",
     )(*[gathered[k] for k in range(n)])

time: 48.9 us -> 46.3 us (0.947)
  local copies, waits for them, and re-layouts: 1.24 us -> 0.02 us
  blocking collectives: 14.4 us -> 13.3 us
    unnamed x10 -> x8, local copies, waits for them, and re-layouts: 1.24 us -> 0.02 us
    all_to_all x1, blocking collectives: 14.4 us -> 13.3 us  [local(): sums = lax.all_to_all(send, ('shard', 'tensor'), 0, 0, tiled=True)]
    pallas_call x1, Pallas kernels: 0.69 us -> 1.74 us  [local(): pl.pallas_call(functools.partial(split_kernel, n, chunks), out_shape=[fla...]
    pallas_call x1, Pallas kernels: 2.28 us -> 1.31 us  [local(): pl.pallas_call(functools.partial(update_kernel, n), out_shape=[flat(jnp.f...]
    pallas_call x0 -> x1, Pallas kernels: none -> 0.9 us  [local(): pl.pallas_call(store_kernel, out_shape=[flat(jnp.float32)] * 3, in_specs=...]
    pallas_call x1, Pallas kernels: 1.65 us -> 0.92 us  [local(): pl.pallas_call(weights_out_kernel, out_shape=[flat(jnp.float32), flat(jnp...]
  transfers between devices with their start and end apart: 14 -> 14, of which waited for: 5 -> 4; matrix products, arithmetic and copies ran while one was open for 0% -> 0% of each run, Pallas kernels for 5% -> 6%
where the time goes in v2:
time: 46.3 us; the launch traced here: 46.1 us
  blocking collectives  13.3 us (29%)
  starting transfers between devices  13.2 us (29%)
  waiting for transfers between devices  9.83 us (21%)
  Pallas kernels  8.28 us (18%)
  between operations  1.43 us (3%)
    all_to_all x1, blocking collectives, local(): sums = lax.all_to_all(send, ('shard', 'tensor'), 0, 0, tiled=True)  13.3 us
    ppermute x14, starting transfers between devices, swap(): return lax.ppermute(value, axis, [(i, i ^ k) for i in range(size)])  13.2 us
    ppermute x14, waiting for transfers between devices, swap(): return lax.ppermute(value, axis, [(i, i ^ k) for i in range(size)])  9.83 us
    pallas_call x1, Pallas kernels, local(): pl.pallas_call(weights_kernel, out_shape=[jax.ShapeDtypeStruct((1, LANES)...  2.02 us
    pallas_call x1, Pallas kernels, local(): pl.pallas_call(functools.partial(split_kernel, n, chunks), out_shape=[fla...  1.74 us
    pallas_call x1, Pallas kernels, local(): pl.pallas_call(functools.partial(join_kernel, n, chunks), out_shape=jax.S...  1.4 us
    pallas_call x1, Pallas kernels, local(): pl.pallas_call(functools.partial(update_kernel, n), out_shape=[flat(jnp.f...  1.31 us
  transfers between devices with their start and end apart: 14, of which 4 were waited for; matrix products, arithmetic and copies ran while one was open for 0% of the time, Pallas kernels for 6%

profile of v2, /device:TPU:0, one launch (start us, length us, event | category | flops | bytes accessed | tf_op | source)
XLA Modules:
  0.0 46.1 jit_solution(11780630608549003477)
XLA Ops:
  0.6 0.0 copy-start
  0.6 0.0 copy-start.3
  0.7 0.0 copy-start.2
  0.7 1.7 %split.1 = (bf16[512,128]{1,0:T(8,128)(2,1)S(1)}, bf16[512,128]{1,0:T(8,128)(2,1)S(1)}, bf16[512,128]{1,0:T(8,128)(2,1)S(1)}, bf16[512,128]{1,0:T(8,128)(2,1)S(1...) custom-call(bf16[1,512,8,128]{3,2,1,0:T(8,128)(2,1)} %bitcast.17), custom_call_target="tpu_custom_call" | custom-call | tf_op jit(solution)/shard_map/split/pallas_call | solution.py:212
  2.4 0.0 copy-start.1
  2.4 0.5 %collective-permute-start = (bf16[512,128]{1,0:T(8,128)(2,1)S(1)}, bf16[512,128]{1,0:T(8,128)(2,1)S(1)}, u32[]{:S(2)}, u32[]{:S(2)}) collective-permute-start(bf16[512,128]{1,0:T(8,128)(2,1)S(1)} %get-tuple-element.26), channel_id=1, source_target_pairs={{0,4},{4,0},{8,12},{12,8},{16,20},{20,16},{24,28},{28,24},{1,5},{5... | collective-permute-start | bytes 393224 | tf_op jit(solution)/shard_map/ppermute | solution.py:194
  2.9 2.6 %collective-permute-start.1 = (bf16[512,128]{1,0:T(8,128)(2,1)S(1)}, bf16[512,128]{1,0:T(8,128)(2,1)S(1)}, u32[]{:S(2)}, u32[]{:S(2)}) collective-permute-start(bf16[512,128]{1,0:T(8,128)(2,1)S(1)} %get-tuple-element.27), channel_id=1, source_target_pairs={{0,8},{4,12},{8,0},{12,4},{16,24},{20,28},{24,16},{28,20},{1,9},{5... | collective-permute-start | bytes 393224 | tf_op jit(solution)/shard_map/ppermute | solution.py:194
  5.5 0.1 collective-permute-start.2
  5.6 1.8 %collective-permute-start.3 = (bf16[512,128]{1,0:T(8,128)(2,1)S(1)}, bf16[512,128]{1,0:T(8,128)(2,1)S(1)}, u32[]{:S(2)}, u32[]{:S(2)}) collective-permute-start(bf16[512,128]{1,0:T(8,128)(2,1)S(1)} %get-tuple-element.29), channel_id=1, source_target_pairs={{0,16},{4,20},{8,24},{12,28},{16,0},{20,4},{24,8},{28,12},{1,17},{... | collective-permute-start | bytes 393224 | tf_op jit(solution)/shard_map/ppermute | solution.py:194
  7.3 0.0 collective-permute-start.4
  7.3 0.0 collective-permute-done.rest_1_
  7.3 2.6 %collective-permute-start.5 = (bf16[512,128]{1,0:T(8,128)(2,1)S(1)}, bf16[512,128]{1,0:T(8,128)(2,1)S(1)}, u32[]{:S(2)}, u32[]{:S(2)}) collective-permute-start(bf16[512,128]{1,0:T(8,128)(2,1)S(1)} %get-tuple-element.31), channel_id=1, source_target_pairs={{0,24},{4,28},{8,16},{12,20},{16,8},{20,12},{24,0},{28,4},{1,25},{... | collective-permute-start | bytes 393224 | tf_op jit(solution)/shard_map/ppermute | solution.py:194
  10.0 0.0 collective-permute-done.1.rest_2_
  10.0 1.6 %collective-permute-start.6 = (bf16[512,128]{1,0:T(8,128)(2,1)S(1)}, bf16[512,128]{1,0:T(8,128)(2,1)S(1)}, u32[]{:S(2)}, u32[]{:S(2)}) collective-permute-start(bf16[512,128]{1,0:T(8,128)(2,1)S(1)} %get-tuple-element.32), channel_id=1, source_target_pairs={{0,28},{4,24},{8,20},{12,16},{16,12},{20,8},{24,4},{28,0},{1,29},{... | collective-permute-start | bytes 393224 | tf_op jit(solution)/shard_map/ppermute | solution.py:194
  12.2 0.0 copy-done
  12.2 0.0 copy-done.3
  12.2 2.0 %weight_squares.1 = (f32[1,128]{1,0:T(1,128)S(1)}, s32[83]{0:T(128)S(1)}) custom-call(s32[80]{0:T(128)S(1)} %copy-done.3, f32[512,128]{1,0:T(8,128)S(1)} %bitcast.12), custom_call_target="tpu_custom_call" | custom-call | flops 524288 | bytes 262144 | tf_op jit(solution)/shard_map/weight_squares/pallas_call | solution.py:229
  14.3 0.0 collective-permute-done.2.rest_3_
  14.3 0.0 collective-permute-done.3.rest_4_
  14.3 4.7 %collective-permute-done.4.rest_5_ = bf16[512,128]{1,0:T(8,128)(2,1)S(1)} collective-permute-done((bf16[512,128]{1,0:T(8,128)(2,1)S(1)}, bf16[512,128]{1,0:T(8,128)(2,1)S(1)}, u32[]{:S(2)}, u32[]{:S(2)}) %collective-permute-start.4) | collective-permute-done | bytes 131104 | tf_op jit(solution)/shard_map/ppermute | solution.py:194
  19.0 0.0 collective-permute-done.5.rest_6_
  19.0 0.0 collective-permute-done.6.rest_7_
  19.0 0.0 copy-done.2
  19.0 0.0 copy-done.1
  19.0 1.3 %update.1 = (f32[512,128]{1,0:T(8,128)S(1)}, f32[512,128]{1,0:T(8,128)S(1)}, f32[512,128]{1,0:T(8,128)S(1)}, f32[32,2,128]{2,1,0:T(2,128)S(1)}) custom-call(s32[1]{0:T(128)S(6)} %copy.10.step_ref, s32[83]{0:T(128)S(1)} %get-tuple-element.23.bounds_ref, f32[1,128]{1,0:T(1,128)S(1)} %get-tuple-element.24.sums_ref, f32[512,128]{1,0:T(8,128)S(1)} %bitcast.13, ...), custom_call_target="tpu_custom_call" | custom-call | tf_op jit(solution)/shard_map/update/pallas_call | solution.py:242
  20.4 13.3 %all_to_all.5.sums_ref = f32[32,2,128]{2,1,0:T(2,128)S(1)} all-to-all(f32[32,2,128]{2,1,0:T(2,128)S(1)} %get-tuple-element.35), channel_id=1, replica_groups=mesh['shard'=8,'tensor'=4] {'shard','tensor'}, dimensions={0} | all-to-all | bytes 65536 | tf_op jit(solution)/shard_map/all_to_all | solution.py:252
  33.7 0.9 %new_weights.1 = (f32[512,128]{1,0:T(8,128)S(1)}, bf16[512,128]{1,0:T(8,128)(2,1)S(1)}) custom-call(s32[83]{0:T(128)S(1)} %get-tuple-element.23.bounds_ref, f32[32,2,128]{2,1,0:T(2,128)S(1)} %all_to_all.5.sums_ref, f32[512,128]{1,0:T(8,128)S(1)} %bitcast.14, f32[512,128]{1,0:T(8,128)S(1)} %get-tuple-element.36.update_ref), custom_call_target="tpu_custom_call" | custom-call | tf_op jit(solution)/shard_map/new_weights/pallas_call | solution.py:253
  34.6 0.6 %collective-permute-start.12 = (bf16[512,128]{1,0:T(8,128)(2,1)S(1)}, bf16[512,128]{1,0:T(8,128)(2,1)S(1)}, u32[]{:S(2)}, u32[]{:S(2)}) collective-permute-start(bf16[512,128]{1,0:T(8,128)(2,1)S(1)} %get-tuple-element.41.rest_0_), channel_id=1, source_target_pairs={{0,24},{4,28},{8,16},{12,20},{16,8},{20,12},{24,0},{28,4},{1,25},{... | collective-permute-start | bytes 393224 | tf_op jit(solution)/shard_map/ppermute | solution.py:194
  35.2 1.4 %collective-permute-start.10 = (bf16[512,128]{1,0:T(8,128)(2,1)S(1)}, bf16[512,128]{1,0:T(8,128)(2,1)S(1)}, u32[]{:S(2)}, u32[]{:S(2)}) collective-permute-start(bf16[512,128]{1,0:T(8,128)(2,1)S(1)} %get-tuple-element.41.rest_0_), channel_id=1, source_target_pairs={{0,16},{4,20},{8,24},{12,28},{16,0},{20,4},{24,8},{28,12},{1,17},{... | collective-permute-start | bytes 393224 | tf_op jit(solution)/shard_map/ppermute | solution.py:194
  36.7 1.5 %collective-permute-start.8 = (bf16[512,128]{1,0:T(8,128)(2,1)S(1)}, bf16[512,128]{1,0:T(8,128)(2,1)S(1)}, u32[]{:S(2)}, u32[]{:S(2)}) collective-permute-start(bf16[512,128]{1,0:T(8,128)(2,1)S(1)} %get-tuple-element.41.rest_0_), channel_id=1, source_target_pairs={{0,8},{4,12},{8,0},{12,4},{16,24},{20,28},{24,16},{28,20},{1,9},{5... | collective-permute-start | bytes 393224 | tf_op jit(solution)/shard_map/ppermute | solution.py:194
  38.1 0.0 collective-permute-start.7
  38.2 3.8 %collective-permute-done.12.rest_6_ = bf16[512,128]{1,0:T(8,128)(2,1)S(1)} collective-permute-done((bf16[512,128]{1,0:T(8,128)(2,1)S(1)}, bf16[512,128]{1,0:T(8,128)(2,1)S(1)}, u32[]{:S(2)}, u32[]{:S(2)}) %collective-permute-start.12) | collective-permute-done | bytes 131104 | tf_op jit(solution)/shard_map/ppermute | solution.py:194
  42.0 0.0 collective-permute-start.13
  42.0 1.2 %collective-permute-done.10.rest_4_ = bf16[512,128]{1,0:T(8,128)(2,1)S(1)} collective-permute-done((bf16[512,128]{1,0:T(8,128)(2,1)S(1)}, bf16[512,128]{1,0:T(8,128)(2,1)S(1)}, u32[]{:S(2)}, u32[]{:S(2)}) %collective-permute-start.10) | collective-permute-done | bytes 131104 | tf_op jit(solution)/shard_map/ppermute | solution.py:194
  43.1 0.0 collective-permute-start.11
  43.2 0.0 collective-permute-done.8.rest_2_
  43.2 0.5 %collective-permute-start.9 = (bf16[512,128]{1,0:T(8,128)(2,1)S(1)}, bf16[512,128]{1,0:T(8,128)(2,1)S(1)}, u32[]{:S(2)}, u32[]{:S(2)}) collective-permute-start(bf16[512,128]{1,0:T(8,128)(2,1)S(1)} %collective-permute-done.8.rest_2_), channel_id=1, source_target_pairs={{0,4},{4,0},{8,12},{12,8},{16,20},{20,16},{24,28},{28,24},{1,5},{5... | collective-permute-start | bytes 393224 | tf_op jit(solution)/shard_map/ppermute | solution.py:194
  43.7 0.9 %store.1 = (f32[512,128]{1,0:T(8,128)}, f32[512,128]{1,0:T(8,128)}, f32[512,128]{1,0:T(8,128)}) custom-call(f32[512,128]{1,0:T(8,128)S(1)} %get-tuple-element.33.new1_ref, f32[512,128]{1,0:T(8,128)S(1)} %get-tuple-element.34.new2_ref, f32[512,128]{1,0:T(8,128)S(1)} %get-tuple-element.37.new_ref), custom_call_target="tpu_custom_call" | custom-call | bytes 786432 | tf_op jit(solution)/shard_map/store/pallas_call | solution.py:267
  44.6 0.0 collective-permute-done.7.rest_1_
  44.6 0.0 collective-permute-done.13.rest_7_
  44.6 0.0 collective-permute-done.11.rest_5_
  44.6 0.1 collective-permute-done.9.rest_3_
  44.7 1.4 %join.1 = bf16[1,512,8,128]{3,2,1,0:T(8,128)(2,1)} custom-call(bf16[512,128]{1,0:T(8,128)(2,1)S(1)} %get-tuple-element.41.rest_0_, bf16[512,128]{1,0:T(8,128)(2,1)S(1)} %collective-permute-done.7.rest_1_, bf16[512,128]{1,0:T(8,128)(2,1)S(1)} %collective-permute-done.8.rest_2_, bf16[512,128]{1,0:T(8,128)(2,1)S(1)} %collective-permute-done.9.rest_3_, ...), custom_call_target="tpu_custom_call" | custom-call | tf_op jit(solution)/shard_map/join/pallas_call | solution.py:277
Async XLA Ops:
  0.6 11.6 %copy-start = (f32[65536]{0:T(1024)S(1)}, f32[65536]{0:T(1024)}, u32[]{:S(2)}) copy-start(f32[65536]{0:T(1024)} %param.9) | copy-start | bytes 786436
  0.6 11.6 %copy-start.3 = (s32[80]{0:T(128)S(1)}, s32[80]{0:T(128)}, u32[]{:S(2)}) copy-start(s32[80]{0:T(128)} %lengths_ref.1) | copy-start | bytes 964
  0.7 18.4 %copy-start.2 = (f32[65536]{0:T(1024)S(1)}, f32[65536]{0:T(1024)}, u32[]{:S(2)}) copy-start(f32[65536]{0:T(1024)} %param.11) | copy-start | bytes 786436
  2.4 16.6 %copy-start.1 = (f32[65536]{0:T(1024)S(1)}, f32[65536]{0:T(1024)}, u32[]{:S(2)}) copy-start(f32[65536]{0:T(1024)} %param.10) | copy-start | bytes 786436
  2.4 4.9 %collective-permute-start = (bf16[512,128]{1,0:T(8,128)(2,1)S(1)}, bf16[512,128]{1,0:T(8,128)(2,1)S(1)}, u32[]{:S(2)}, u32[]{:S(2)}) collective-permute-start(bf16[512,128]{1,0:T(8,128)(2,1)S(1)} %get-tuple-element.26), channel_id=1, source_target_pairs={{0,4},{4,0},{8,12},{12,8},{16,20},{20,16},{24,28},{28,24},{1,5},{5... | collective-permute-start | bytes 393224 | tf_op jit(solution)/shard_map/ppermute | solution.py:194
  2.9 7.0 %collective-permute-start.1 = (bf16[512,128]{1,0:T(8,128)(2,1)S(1)}, bf16[512,128]{1,0:T(8,128)(2,1)S(1)}, u32[]{:S(2)}, u32[]{:S(2)}) collective-permute-start(bf16[512,128]{1,0:T(8,128)(2,1)S(1)} %get-tuple-element.27), channel_id=1, source_target_pairs={{0,8},{4,12},{8,0},{12,4},{16,24},{20,28},{24,16},{28,20},{1,9},{5... | collective-permute-start | bytes 393224 | tf_op jit(solution)/shard_map/ppermute | solution.py:194
  5.5 8.8 %collective-permute-start.2 = (bf16[512,128]{1,0:T(8,128)(2,1)S(1)}, bf16[512,128]{1,0:T(8,128)(2,1)S(1)}, u32[]{:S(2)}, u32[]{:S(2)}) collective-permute-start(bf16[512,128]{1,0:T(8,128)(2,1)S(1)} %get-tuple-element.28), channel_id=1, source_target_pairs={{0,12},{4,8},{8,4},{12,0},{16,28},{20,24},{24,20},{28,16},{1,13},{... | collective-permute-start | bytes 393224 | tf_op jit(solution)/shard_map/ppermute | solution.py:194
  5.6 8.7 %collective-permute-start.3 = (bf16[512,128]{1,0:T(8,128)(2,1)S(1)}, bf16[512,128]{1,0:T(8,128)(2,1)S(1)}, u32[]{:S(2)}, u32[]{:S(2)}) collective-permute-start(bf16[512,128]{1,0:T(8,128)(2,1)S(1)} %get-tuple-element.29), channel_id=1, source_target_pairs={{0,16},{4,20},{8,24},{12,28},{16,0},{20,4},{24,8},{28,12},{1,17},{... | collective-permute-start | bytes 393224 | tf_op jit(solution)/shard_map/ppermute | solution.py:194
  7.3 11.7 %collective-permute-start.4 = (bf16[512,128]{1,0:T(8,128)(2,1)S(1)}, bf16[512,128]{1,0:T(8,128)(2,1)S(1)}, u32[]{:S(2)}, u32[]{:S(2)}) collective-permute-start(bf16[512,128]{1,0:T(8,128)(2,1)S(1)} %get-tuple-element.30), channel_id=1, source_target_pairs={{0,20},{4,16},{8,28},{12,24},{16,4},{20,0},{24,12},{28,8},{1,21},{... | collective-permute-start | bytes 393224 | tf_op jit(solution)/shard_map/ppermute | solution.py:194
  7.3 11.7 %collective-permute-start.5 = (bf16[512,128]{1,0:T(8,128)(2,1)S(1)}, bf16[512,128]{1,0:T(8,128)(2,1)S(1)}, u32[]{:S(2)}, u32[]{:S(2)}) collective-permute-start(bf16[512,128]{1,0:T(8,128)(2,1)S(1)} %get-tuple-element.31), channel_id=1, source_target_pairs={{0,24},{4,28},{8,16},{12,20},{16,8},{20,12},{24,0},{28,4},{1,25},{... | collective-permute-start | bytes 393224 | tf_op jit(solution)/shard_map/ppermute | solution.py:194
  10.0 9.1 %collective-permute-start.6 = (bf16[512,128]{1,0:T(8,128)(2,1)S(1)}, bf16[512,128]{1,0:T(8,128)(2,1)S(1)}, u32[]{:S(2)}, u32[]{:S(2)}) collective-permute-start(bf16[512,128]{1,0:T(8,128)(2,1)S(1)} %get-tuple-element.32), channel_id=1, source_target_pairs={{0,28},{4,24},{8,20},{12,16},{16,12},{20,8},{24,4},{28,0},{1,29},{... | collective-permute-start | bytes 393224 | tf_op jit(solution)/shard_map/ppermute | solution.py:194
  34.6 7.4 %collective-permute-start.12 = (bf16[512,128]{1,0:T(8,128)(2,1)S(1)}, bf16[512,128]{1,0:T(8,128)(2,1)S(1)}, u32[]{:S(2)}, u32[]{:S(2)}) collective-permute-start(bf16[512,128]{1,0:T(8,128)(2,1)S(1)} %get-tuple-element.41.rest_0_), channel_id=1, source_target_pairs={{0,24},{4,28},{8,16},{12,20},{16,8},{20,12},{24,0},{28,4},{1,25},{... | collective-permute-start | bytes 393224 | tf_op jit(solution)/shard_map/ppermute | solution.py:194
  35.2 7.9 %collective-permute-start.10 = (bf16[512,128]{1,0:T(8,128)(2,1)S(1)}, bf16[512,128]{1,0:T(8,128)(2,1)S(1)}, u32[]{:S(2)}, u32[]{:S(2)}) collective-permute-start(bf16[512,128]{1,0:T(8,128)(2,1)S(1)} %get-tuple-element.41.rest_0_), channel_id=1, source_target_pairs={{0,16},{4,20},{8,24},{12,28},{16,0},{20,4},{24,8},{28,12},{1,17},{... | collective-permute-start | bytes 393224 | tf_op jit(solution)/shard_map/ppermute | solution.py:194
  36.7 6.5 %collective-permute-start.8 = (bf16[512,128]{1,0:T(8,128)(2,1)S(1)}, bf16[512,128]{1,0:T(8,128)(2,1)S(1)}, u32[]{:S(2)}, u32[]{:S(2)}) collective-permute-start(bf16[512,128]{1,0:T(8,128)(2,1)S(1)} %get-tuple-element.41.rest_0_), channel_id=1, source_target_pairs={{0,8},{4,12},{8,0},{12,4},{16,24},{20,28},{24,16},{28,20},{1,9},{5... | collective-permute-start | bytes 393224 | tf_op jit(solution)/shard_map/ppermute | solution.py:194
  38.1 6.4 %collective-permute-start.7 = (bf16[512,128]{1,0:T(8,128)(2,1)S(1)}, bf16[512,128]{1,0:T(8,128)(2,1)S(1)}, u32[]{:S(2)}, u32[]{:S(2)}) collective-permute-start(bf16[512,128]{1,0:T(8,128)(2,1)S(1)} %get-tuple-element.41.rest_0_), channel_id=1, source_target_pairs={{0,4},{4,0},{8,12},{12,8},{16,20},{20,16},{24,28},{28,24},{1,5},{5... | collective-permute-start | bytes 393224 | tf_op jit(solution)/shard_map/ppermute | solution.py:194
  42.0 2.6 %collective-permute-start.13 = (bf16[512,128]{1,0:T(8,128)(2,1)S(1)}, bf16[512,128]{1,0:T(8,128)(2,1)S(1)}, u32[]{:S(2)}, u32[]{:S(2)}) collective-permute-start(bf16[512,128]{1,0:T(8,128)(2,1)S(1)} %collective-permute-done.12.rest_6_), channel_id=1, source_target_pairs={{0,4},{4,0},{8,12},{12,8},{16,20},{20,16},{24,28},{28,24},{1,5},{5... | collective-permute-start | bytes 393224 | tf_op jit(solution)/shard_map/ppermute | solution.py:194
  43.1 1.4 %collective-permute-start.11 = (bf16[512,128]{1,0:T(8,128)(2,1)S(1)}, bf16[512,128]{1,0:T(8,128)(2,1)S(1)}, u32[]{:S(2)}, u32[]{:S(2)}) collective-permute-start(bf16[512,128]{1,0:T(8,128)(2,1)S(1)} %collective-permute-done.10.rest_4_), channel_id=1, source_target_pairs={{0,4},{4,0},{8,12},{12,8},{16,20},{20,16},{24,28},{28,24},{1,5},{5... | collective-permute-start | bytes 393224 | tf_op jit(solution)/shard_map/ppermute | solution.py:194
  43.2 1.5 %collective-permute-start.9 = (bf16[512,128]{1,0:T(8,128)(2,1)S(1)}, bf16[512,128]{1,0:T(8,128)(2,1)S(1)}, u32[]{:S(2)}, u32[]{:S(2)}) collective-permute-start(bf16[512,128]{1,0:T(8,128)(2,1)S(1)} %collective-permute-done.8.rest_2_), channel_id=1, source_target_pairs={{0,4},{4,0},{8,12},{12,8},{16,20},{20,16},{24,28},{28,24},{1,5},{5... | collective-permute-start | bytes 393224 | tf_op jit(solution)/shard_map/ppermute | solution.py:194

commit v3 on v2

--- a/solution.py
+++ b/solution.py
@@ -11,6 +11,8 @@
 LANES = 128
 TILE = 64
 PARTS = 4
+ORDER = (2, 4, 3, 5, 6, 7, 1)
+EARLY = 3
 VMEM = pl.BlockSpec(memory_space=pltpu.VMEM)
 SMEM = pl.BlockSpec(memory_space=pltpu.SMEM)
 HBM = pl.BlockSpec(memory_space=pltpu.HBM)
@@ -69,6 +71,13 @@
     return place + lax.broadcasted_iota(jnp.int32, (rows, LANES), 1)
 
 
+def total_of(pieces, part):
+    total = pieces[0][part, :].astype(jnp.float32)
+    for piece in pieces[1:]:
+        total = total + piece[part, :].astype(jnp.float32)
+    return total
+
+
 def segment_rows(squares, table, bounds):
     rows = math.gcd(squares.shape[0], TILE)
     size = rows * LANES
@@ -97,8 +106,15 @@
     lax.fori_loop(bounds[count + 1], bounds[count + 2], segment, 0)
 
 
-def weights_kernel(lengths_ref, weights_ref, sums_ref, bounds_ref, squares, table):
+def early_kernel(n, lengths_ref, weights_hbm, moment1_hbm, moment2_hbm, *rest):
+    pieces = rest[:n]
+    weights_ref, moment1_ref, moment2_ref, partial_ref, sums_ref, bounds_ref = rest[n : n + 6]
+    squares, table, sems = rest[n + 6 :]
     chunks = weights_ref.shape[0]
+    pairs = ((weights_hbm, weights_ref), (moment1_hbm, moment1_ref), (moment2_hbm, moment2_ref))
+    copies = [pltpu.make_async_copy(*pair, sems.at[i]) for i, pair in enumerate(pairs)]
+    for copy in copies:
+        copy.start()
     width = chunks * LANES
     count = lengths_ref.shape[0]
     index = lax.axis_index("shard") * lax.axis_size("tensor") + lax.axis_index("tensor")
@@ -118,13 +134,24 @@
     bounds_ref[count] = jnp.clip(at, 0, width)
     bounds_ref[count + 1] = first
     bounds_ref[count + 2] = last
+    rows = math.gcd(chunks, TILE)
+
+    def add(t, carry):
+        part = pl.ds(pl.multiple_of(t * rows, rows), rows)
+        partial_ref[part, :] = total_of(pieces, part)
+        return carry
+
+    lax.fori_loop(0, chunks // rows, add, 0)
+    for copy in copies:
+        copy.wait()
     squares[...] = weights_ref[...] * weights_ref[...]
     segment_rows(squares, table, bounds_ref)
     sums_ref[...] = jnp.sum(table[...].T, axis=0, keepdims=True)
 
 
 def update_kernel(n, step_ref, bounds_ref, sums_ref, weights_ref, moment1_ref, moment2_ref, *rest):
-    pieces = rest[:n]
+    partial_ref, pieces = rest[0], rest[1 : n + 1]
+    rest = rest[1:]
     new1_ref, new2_ref, update_ref, send_ref = rest[n : n + 4]
     squares, table = rest[n + 4 :]
 
@@ -140,9 +167,7 @@
 
     def block(t, carry):
         part = pl.ds(pl.multiple_of(t * rows, rows), rows)
-        grad = pieces[0][part, :].astype(jnp.float32)
-        for piece in pieces[1:]:
-            grad = grad + piece[part, :].astype(jnp.float32)
+        grad = partial_ref[part, :] + total_of(pieces, part)
         new1 = 0.9 * moment1_ref[part, :] + 0.1 * grad
         new2 = 0.999 * moment2_ref[part, :] + 0.001 * grad * grad
         new1_ref[part, :] = new1
@@ -188,6 +213,11 @@
         return lax.fori_loop(low // size, (high + (size - 1)) // size, step, carry)
 
     lax.fori_loop(bounds_ref[count + 1], bounds_ref[count + 2], segment, 0)
+
+
+def exchange_order(n):
+    first = [k for k in ORDER if k < n]
+    return first + [k for k in range(1, n) if k not in first]
 
 
 def swap(value, axis, size, k):
@@ -218,37 +248,43 @@
         compiler_params=BIG,
         name="split",
     )(pltpu.with_memory_space_constraint(rows, pltpu.HBM))
-    pieces = [pieces[0]] + [swap(pieces[k], "shard", n, k) for k in range(1, n)]
-    weights = weights.reshape(chunks, LANES)
-    moment1 = moment1.reshape(chunks, LANES)
-    moment2 = moment2.reshape(chunks, LANES)
+    order = exchange_order(n)
+    pieces = [pieces[0]] + [swap(pieces[k], "shard", n, k) for k in order]
+    early, late = pieces[: EARLY + 1], pieces[EARLY + 1 :]
     square_table = [
         pltpu.VMEM((chunks, LANES), jnp.float32),
         pltpu.VMEM((LANES, LANES), jnp.float32),
     ]
-    sums, bounds = pl.pallas_call(
-        weights_kernel,
-        out_shape=[
+    stored = [
+        pltpu.with_memory_space_constraint(value.reshape(chunks, LANES), pltpu.HBM)
+        for value in (weights, moment1, moment2)
+    ]
+    weights, moment1, moment2, partial, sums, bounds = pl.pallas_call(
+        functools.partial(early_kernel, len(early)),
+        out_shape=[flat(jnp.float32)] * 4
+        + [
             jax.ShapeDtypeStruct((1, LANES), jnp.float32),
             jax.ShapeDtypeStruct((count + 3,), jnp.int32),
         ],
-        in_specs=[SMEM, VMEM],
-        out_specs=[VMEM, SMEM],
-        scratch_shapes=square_table,
-        compiler_params=BIG,
-        cost_estimate=pl.CostEstimate(flops=8 * width, bytes_accessed=4 * width, transcendentals=0),
-        name="weight_squares",
-    )(lengths, weights)
+        in_specs=[SMEM] + [HBM] * 3 + [VMEM] * len(early),
+        out_specs=[VMEM] * 5 + [SMEM],
+        scratch_shapes=square_table + [pltpu.SemaphoreType.DMA((3,))],
+        compiler_params=BIG,
+        cost_estimate=pl.CostEstimate(
+            flops=8 * width, bytes_accessed=24 * width, transcendentals=0
+        ),
+        name="early",
+    )(lengths, *stored, *early)
     new1, new2, update, send = pl.pallas_call(
-        functools.partial(update_kernel, n),
+        functools.partial(update_kernel, len(late)),
         out_shape=[flat(jnp.float32)] * 3
         + [jax.ShapeDtypeStruct((everyone, 2, LANES), jnp.float32)],
-        in_specs=[SMEM, SMEM] + [VMEM] * (4 + n),
+        in_specs=[SMEM, SMEM] + [VMEM] * (5 + len(late)),
         out_specs=[VMEM] * 4,
         scratch_shapes=square_table,
         compiler_params=BIG,
         name="update",
-    )(step, bounds, sums, weights, moment1, moment2, *pieces)
+    )(step, bounds, sums, weights, moment1, moment2, partial, *late)
     sums = lax.all_to_all(send, ("shard", "tensor"), 0, 0, tiled=True)
     new, narrow = pl.pallas_call(
         weights_out_kernel,
@@ -262,8 +298,6 @@
     gathered = {0: narrow}
     for k in range(2, n, 2):
         gathered[k] = swap(narrow, "shard", n, k)
-    for k in range(0, n, 2):
-        gathered[k + 1] = swap(gathered[k], "shard", n, 1)
     new1, new2, new = pl.pallas_call(
         store_kernel,
         out_shape=[flat(jnp.float32)] * 3,
@@ -274,6 +308,8 @@
         cost_estimate=pl.CostEstimate(flops=0, bytes_accessed=12 * width, transcendentals=0),
         name="store",
     )(new1, new2, new)
+    for k in range(0, n, 2):
+        gathered[k + 1] = swap(gathered[k], "shard", n, 1)
     joined = pl.pallas_call(
         functools.partial(join_kernel, n, chunks),
         out_shape=jax.ShapeDtypeStruct((n // 8, chunks, 8, LANES), jnp.bfloat16),

time: 46.3 us -> 44 us (0.950)
  waiting for transfers between devices: 9.83 us -> 7.45 us
  blocking collectives: 13.3 us -> 11.8 us
  starting transfers between devices: 13.2 us -> 13.9 us
  local copies, waits for them, and re-layouts: 0.02 us -> 0.65 us
    ppermute x14, waiting for transfers between devices: 9.83 us -> 7.45 us  [swap(): return lax.ppermute(value, axis, [(i, i ^ k) for i in range(size)])]
    all_to_all x1, blocking collectives: 13.3 us -> 11.8 us  [local(): sums = lax.all_to_all(send, ('shard', 'tensor'), 0, 0, tiled=True)]
    ppermute x14, starting transfers between devices: 13.2 us -> 13.9 us  [swap(): return lax.ppermute(value, axis, [(i, i ^ k) for i in range(size)])]
    unnamed x8 -> x2, local copies, waits for them, and re-layouts: 0.02 us -> 0.65 us
    pallas_call x2, Pallas kernels: 3.32 us -> 3.82 us  [the longest x1 2.54 us: local(): pl.pallas_call(functools.partial(early_kernel, len(early)), out_shape=[fl...]
  transfers between devices with their start and end apart: 14 -> 14, of which waited for: 4 -> 6; matrix products, arithmetic and copies ran while one was open for 0% -> 0% of each run, Pallas kernels for 6% -> 8%
where the time goes in v3:
time: 44 us; the launch traced here: 43.9 us
  starting transfers between devices  13.9 us (32%)
  blocking collectives  11.8 us (27%)
  Pallas kernels  8.72 us (20%)
  waiting for transfers between devices  7.45 us (17%)
  between operations  1.37 us (3%)
  local copies, waits for them, and re-layouts  0.65 us (1%)
    ppermute x14, starting transfers between devices, swap(): return lax.ppermute(value, axis, [(i, i ^ k) for i in range(size)])  13.9 us
    all_to_all x1, blocking collectives, local(): sums = lax.all_to_all(send, ('shard', 'tensor'), 0, 0, tiled=True)  11.8 us
    ppermute x14, waiting for transfers between devices, swap(): return lax.ppermute(value, axis, [(i, i ^ k) for i in range(size)])  7.45 us
    pallas_call x1, Pallas kernels, local(): pl.pallas_call(functools.partial(early_kernel, len(early)), out_shape=[fl...  2.54 us
    pallas_call x1, Pallas kernels, local(): pl.pallas_call(functools.partial(split_kernel, n, chunks), out_shape=[fla...  1.68 us
    pallas_call x1, Pallas kernels, local(): pl.pallas_call(functools.partial(join_kernel, n, chunks), out_shape=jax.S...  1.39 us
    pallas_call x1, Pallas kernels, local(): pl.pallas_call(functools.partial(update_kernel, len(late)), out_shape=[fl...  1.28 us
    pallas_call x1, Pallas kernels, local(): pl.pallas_call(weights_out_kernel, out_shape=[flat(jnp.float32), flat(jnp...  0.92 us
  transfers between devices with their start and end apart: 14, of which 6 were waited for; matrix products, arithmetic and copies ran while one was open for 0% of the time, Pallas kernels for 8%

profile of v3, /device:TPU:0, one launch (start us, length us, event | category | flops | bytes accessed | tf_op | source)
XLA Modules:
  0.0 43.9 jit_solution(2731623809182362270)
XLA Ops:
  0.6 1.7 %split.1 = (bf16[512,128]{1,0:T(8,128)(2,1)S(1)}, bf16[512,128]{1,0:T(8,128)(2,1)S(1)}, bf16[512,128]{1,0:T(8,128)(2,1)S(1)}, bf16[512,128]{1,0:T(8,128)(2,1)S(1...) custom-call(bf16[1,512,8,128]{3,2,1,0:T(8,128)(2,1)} %bitcast.12), custom_call_target="tpu_custom_call" | custom-call | tf_op jit(solution)/shard_map/split/pallas_call | solution.py:242
  2.3 3.0 %collective-permute-start = (bf16[512,128]{1,0:T(8,128)(2,1)S(1)}, bf16[512,128]{1,0:T(8,128)(2,1)S(1)}, u32[]{:S(2)}, u32[]{:S(2)}) collective-permute-start(bf16[512,128]{1,0:T(8,128)(2,1)S(1)} %get-tuple-element.28), channel_id=1, source_target_pairs={{0,8},{4,12},{8,0},{12,4},{16,24},{20,28},{24,16},{28,20},{1,9},{5... | collective-permute-start | bytes 393224 | tf_op jit(solution)/shard_map/ppermute | solution.py:224
  5.3 1.5 %collective-permute-start.1 = (bf16[512,128]{1,0:T(8,128)(2,1)S(1)}, bf16[512,128]{1,0:T(8,128)(2,1)S(1)}, u32[]{:S(2)}, u32[]{:S(2)}) collective-permute-start(bf16[512,128]{1,0:T(8,128)(2,1)S(1)} %get-tuple-element.29), channel_id=1, source_target_pairs={{0,16},{4,20},{8,24},{12,28},{16,0},{20,4},{24,8},{28,12},{1,17},{... | collective-permute-start | bytes 393224 | tf_op jit(solution)/shard_map/ppermute | solution.py:224
  6.8 0.0 collective-permute-start.2
  6.8 0.3 collective-permute-start.3
  7.2 2.9 %collective-permute-start.4 = (bf16[512,128]{1,0:T(8,128)(2,1)S(1)}, bf16[512,128]{1,0:T(8,128)(2,1)S(1)}, u32[]{:S(2)}, u32[]{:S(2)}) collective-permute-start(bf16[512,128]{1,0:T(8,128)(2,1)S(1)} %get-tuple-element.38), channel_id=1, source_target_pairs={{0,24},{4,28},{8,16},{12,20},{16,8},{20,12},{24,0},{28,4},{1,25},{... | collective-permute-start | bytes 393224 | tf_op jit(solution)/shard_map/ppermute | solution.py:224
  10.1 0.0 collective-permute-done.rest_1_
  10.1 0.0 collective-permute-start.5
  10.1 0.7 %collective-permute-done.1.rest_2_ = bf16[512,128]{1,0:T(8,128)(2,1)S(1)} collective-permute-done((bf16[512,128]{1,0:T(8,128)(2,1)S(1)}, bf16[512,128]{1,0:T(8,128)(2,1)S(1)}, u32[]{:S(2)}, u32[]{:S(2)}) %collective-permute-start.1) | collective-permute-done | bytes 131104 | tf_op jit(solution)/shard_map/ppermute | solution.py:224
  10.8 2.0 %collective-permute-start.6 = (bf16[512,128]{1,0:T(8,128)(2,1)S(1)}, bf16[512,128]{1,0:T(8,128)(2,1)S(1)}, u32[]{:S(2)}, u32[]{:S(2)}) collective-permute-start(bf16[512,128]{1,0:T(8,128)(2,1)S(1)} %get-tuple-element.40), channel_id=1, source_target_pairs={{0,4},{4,0},{8,12},{12,8},{16,20},{20,16},{24,28},{28,24},{1,5},{5... | collective-permute-start | bytes 393224 | tf_op jit(solution)/shard_map/ppermute | solution.py:224
  13.4 0.0 collective-permute-done.2.rest_3_
  13.4 0.0 copy-start
  13.5 0.6 %copy-done = s32[80]{0:T(128)S(1)} copy-done((s32[80]{0:T(128)S(1)}, s32[80]{0:T(128)}, u32[]{:S(2)}) %copy-start) | copy-done | bytes 344
  14.1 2.5 %early.1 = (f32[512,128]{1,0:T(8,128)S(1)}, f32[512,128]{1,0:T(8,128)S(1)}, f32[512,128]{1,0:T(8,128)S(1)}, f32[512,128]{1,0:T(8,128)S(1)}, f32[1,128]{1,0:T(1,128)S(1)}, /*index=5*/s32[83]{0:T(128)S(1)}) custom-call(s32[80]{0:T(128)S(1)} %copy-done, f32[512,128]{1,0:T(8,128)} %bitcast.14, f32[512,128]{1,0:T(8,128)} %bitcast.15, f32[512,128]{1,0:T(8,128)} %bitcast.16, ...), custom_call_target="tpu_custom_call" | custom-call | flops 524288 | bytes 1572864 | tf_op jit(solution)/shard_map/early/pallas_call | solution.py:262
  16.7 1.1 %collective-permute-done.3.rest_1_ = bf16[512,128]{1,0:T(8,128)(2,1)S(1)} collective-permute-done((bf16[512,128]{1,0:T(8,128)(2,1)S(1)}, bf16[512,128]{1,0:T(8,128)(2,1)S(1)}, u32[]{:S(2)}, u32[]{:S(2)}) %collective-permute-start.3) | collective-permute-done | bytes 131104 | tf_op jit(solution)/shard_map/ppermute | solution.py:224
  17.7 0.0 collective-permute-done.4.rest_2_
  17.8 0.6 %collective-permute-done.5.rest_3_ = bf16[512,128]{1,0:T(8,128)(2,1)S(1)} collective-permute-done((bf16[512,128]{1,0:T(8,128)(2,1)S(1)}, bf16[512,128]{1,0:T(8,128)(2,1)S(1)}, u32[]{:S(2)}, u32[]{:S(2)}) %collective-permute-start.5) | collective-permute-done | bytes 131104 | tf_op jit(solution)/shard_map/ppermute | solution.py:224
  18.4 0.0 collective-permute-done.6.rest_4_
  18.4 1.3 %update.1 = (f32[512,128]{1,0:T(8,128)S(1)}, f32[512,128]{1,0:T(8,128)S(1)}, f32[512,128]{1,0:T(8,128)S(1)}, f32[32,2,128]{2,1,0:T(2,128)S(1)}) custom-call(s32[1]{0:T(128)S(6)} %copy.10.step_ref, s32[83]{0:T(128)S(1)} %get-tuple-element.31.bounds_ref, f32[1,128]{1,0:T(1,128)S(1)} %get-tuple-element.32.sums_ref, ...), custom_call_target="tpu_custom_call" | custom-call | tf_op jit(solution)/shard_map/update/pallas_call | solution.py:278
  19.6 11.8 %all_to_all.5.sums_ref = f32[32,2,128]{2,1,0:T(2,128)S(1)} all-to-all(f32[32,2,128]{2,1,0:T(2,128)S(1)} %get-tuple-element.43), channel_id=1, replica_groups=mesh['shard'=8,'tensor'=4] {'shard','tensor'}, dimensions={0} | all-to-all | bytes 65536 | tf_op jit(solution)/shard_map/all_to_all | solution.py:288
  31.4 0.9 %new_weights.1 = (f32[512,128]{1,0:T(8,128)S(1)}, bf16[512,128]{1,0:T(8,128)(2,1)S(1)}) custom-call(s32[83]{0:T(128)S(1)} %get-tuple-element.31.bounds_ref, f32[32,2,128]{2,1,0:T(2,128)S(1)} %all_to_all.5.sums_ref, f32[512,128]{1,0:T(8,128)S(1)} %get-tuple-element.33.weights_ref, f32[512,128]{1,0:T(8,128)S(1)} %get-tuple-element.44.update_ref), custom_call_target="tpu_custom_call" | custom-call | tf_op jit(solution)/shard_map/new_weights/pallas_call | solution.py:289
  32.4 0.6 %collective-permute-start.12 = (bf16[512,128]{1,0:T(8,128)(2,1)S(1)}, bf16[512,128]{1,0:T(8,128)(2,1)S(1)}, u32[]{:S(2)}, u32[]{:S(2)}) collective-permute-start(bf16[512,128]{1,0:T(8,128)(2,1)S(1)} %get-tuple-element.49.rest_0_), channel_id=1, source_target_pairs={{0,24},{4,28},{8,16},{12,20},{16,8},{20,12},{24,0},{28,4},{1,25},{... | collective-permute-start | bytes 393224 | tf_op jit(solution)/shard_map/ppermute | solution.py:224
  32.9 1.5 %collective-permute-start.10 = (bf16[512,128]{1,0:T(8,128)(2,1)S(1)}, bf16[512,128]{1,0:T(8,128)(2,1)S(1)}, u32[]{:S(2)}, u32[]{:S(2)}) collective-permute-start(bf16[512,128]{1,0:T(8,128)(2,1)S(1)} %get-tuple-element.49.rest_0_), channel_id=1, source_target_pairs={{0,16},{4,20},{8,24},{12,28},{16,0},{20,4},{24,8},{28,12},{1,17},{... | collective-permute-start | bytes 393224 | tf_op jit(solution)/shard_map/ppermute | solution.py:224
  34.4 1.5 %collective-permute-start.8 = (bf16[512,128]{1,0:T(8,128)(2,1)S(1)}, bf16[512,128]{1,0:T(8,128)(2,1)S(1)}, u32[]{:S(2)}, u32[]{:S(2)}) collective-permute-start(bf16[512,128]{1,0:T(8,128)(2,1)S(1)} %get-tuple-element.49.rest_0_), channel_id=1, source_target_pairs={{0,8},{4,12},{8,0},{12,4},{16,24},{20,28},{24,16},{28,20},{1,9},{5... | collective-permute-start | bytes 393224 | tf_op jit(solution)/shard_map/ppermute | solution.py:224
  35.9 0.0 collective-permute-start.7
  35.9 3.8 %collective-permute-done.12.rest_6_ = bf16[512,128]{1,0:T(8,128)(2,1)S(1)} collective-permute-done((bf16[512,128]{1,0:T(8,128)(2,1)S(1)}, bf16[512,128]{1,0:T(8,128)(2,1)S(1)}, u32[]{:S(2)}, u32[]{:S(2)}) %collective-permute-start.12) | collective-permute-done | bytes 131104 | tf_op jit(solution)/shard_map/ppermute | solution.py:224
  39.7 0.0 collective-permute-start.13
  39.8 1.2 %collective-permute-done.10.rest_4_ = bf16[512,128]{1,0:T(8,128)(2,1)S(1)} collective-permute-done((bf16[512,128]{1,0:T(8,128)(2,1)S(1)}, bf16[512,128]{1,0:T(8,128)(2,1)S(1)}, u32[]{:S(2)}, u32[]{:S(2)}) %collective-permute-start.10) | collective-permute-done | bytes 131104 | tf_op jit(solution)/shard_map/ppermute | solution.py:224
  40.9 0.0 collective-permute-start.11
  40.9 0.0 collective-permute-done.8.rest_2_
  40.9 0.5 %collective-permute-start.9 = (bf16[512,128]{1,0:T(8,128)(2,1)S(1)}, bf16[512,128]{1,0:T(8,128)(2,1)S(1)}, u32[]{:S(2)}, u32[]{:S(2)}) collective-permute-start(bf16[512,128]{1,0:T(8,128)(2,1)S(1)} %collective-permute-done.8.rest_2_), channel_id=1, source_target_pairs={{0,4},{4,0},{8,12},{12,8},{16,20},{20,16},{24,28},{28,24},{1,5},{5... | collective-permute-start | bytes 393224 | tf_op jit(solution)/shard_map/ppermute | solution.py:224
  41.4 0.9 %store.1 = (f32[512,128]{1,0:T(8,128)}, f32[512,128]{1,0:T(8,128)}, f32[512,128]{1,0:T(8,128)}) custom-call(f32[512,128]{1,0:T(8,128)S(1)} %get-tuple-element.41.new1_ref, f32[512,128]{1,0:T(8,128)S(1)} %get-tuple-element.42.new2_ref, f32[512,128]{1,0:T(8,128)S(1)} %get-tuple-element.45.new_ref), custom_call_target="tpu_custom_call" | custom-call | bytes 786432 | tf_op jit(solution)/shard_map/store/pallas_call | solution.py:301
  42.3 0.0 collective-permute-done.7.rest_1_
  42.4 0.0 collective-permute-done.13.rest_7_
  42.4 0.0 collective-permute-done.11.rest_5_
  42.4 0.1 collective-permute-done.9.rest_3_
  42.5 1.4 %join.1 = bf16[1,512,8,128]{3,2,1,0:T(8,128)(2,1)} custom-call(bf16[512,128]{1,0:T(8,128)(2,1)S(1)} %get-tuple-element.49.rest_0_, bf16[512,128]{1,0:T(8,128)(2,1)S(1)} %collective-permute-done.7.rest_1_, bf16[512,128]{1,0:T(8,128)(2,1)S(1)} %collective-permute-done.8.rest_2_, bf16[512,128]{1,0:T(8,128)(2,1)S(1)} %collective-permute-done.9.rest_3_, ...), custom_call_target="tpu_custom_call" | custom-call | tf_op jit(solution)/shard_map/join/pallas_call | solution.py:313
Async XLA Ops:
  2.3 7.7 %collective-permute-start = (bf16[512,128]{1,0:T(8,128)(2,1)S(1)}, bf16[512,128]{1,0:T(8,128)(2,1)S(1)}, u32[]{:S(2)}, u32[]{:S(2)}) collective-permute-start(bf16[512,128]{1,0:T(8,128)(2,1)S(1)} %get-tuple-element.28), channel_id=1, source_target_pairs={{0,8},{4,12},{8,0},{12,4},{16,24},{20,28},{24,16},{28,20},{1,9},{5... | collective-permute-start | bytes 393224 | tf_op jit(solution)/shard_map/ppermute | solution.py:224
  5.3 5.4 %collective-permute-start.1 = (bf16[512,128]{1,0:T(8,128)(2,1)S(1)}, bf16[512,128]{1,0:T(8,128)(2,1)S(1)}, u32[]{:S(2)}, u32[]{:S(2)}) collective-permute-start(bf16[512,128]{1,0:T(8,128)(2,1)S(1)} %get-tuple-element.29), channel_id=1, source_target_pairs={{0,16},{4,20},{8,24},{12,28},{16,0},{20,4},{24,8},{28,12},{1,17},{... | collective-permute-start | bytes 393224 | tf_op jit(solution)/shard_map/ppermute | solution.py:224
  6.8 6.6 %collective-permute-start.2 = (bf16[512,128]{1,0:T(8,128)(2,1)S(1)}, bf16[512,128]{1,0:T(8,128)(2,1)S(1)}, u32[]{:S(2)}, u32[]{:S(2)}) collective-permute-start(bf16[512,128]{1,0:T(8,128)(2,1)S(1)} %get-tuple-element.30), channel_id=1, source_target_pairs={{0,12},{4,8},{8,4},{12,0},{16,28},{20,24},{24,20},{28,16},{1,13},{... | collective-permute-start | bytes 393224 | tf_op jit(solution)/shard_map/ppermute | solution.py:224
  6.8 10.9 %collective-permute-start.3 = (bf16[512,128]{1,0:T(8,128)(2,1)S(1)}, bf16[512,128]{1,0:T(8,128)(2,1)S(1)}, u32[]{:S(2)}, u32[]{:S(2)}) collective-permute-start(bf16[512,128]{1,0:T(8,128)(2,1)S(1)} %get-tuple-element.37), channel_id=1, source_target_pairs={{0,20},{4,16},{8,28},{12,24},{16,4},{20,0},{24,12},{28,8},{1,21},{... | collective-permute-start | bytes 393224 | tf_op jit(solution)/shard_map/ppermute | solution.py:224
  7.2 10.6 %collective-permute-start.4 = (bf16[512,128]{1,0:T(8,128)(2,1)S(1)}, bf16[512,128]{1,0:T(8,128)(2,1)S(1)}, u32[]{:S(2)}, u32[]{:S(2)}) collective-permute-start(bf16[512,128]{1,0:T(8,128)(2,1)S(1)} %get-tuple-element.38), channel_id=1, source_target_pairs={{0,24},{4,28},{8,16},{12,20},{16,8},{20,12},{24,0},{28,4},{1,25},{... | collective-permute-start | bytes 393224 | tf_op jit(solution)/shard_map/ppermute | solution.py:224
  10.1 8.3 %collective-permute-start.5 = (bf16[512,128]{1,0:T(8,128)(2,1)S(1)}, bf16[512,128]{1,0:T(8,128)(2,1)S(1)}, u32[]{:S(2)}, u32[]{:S(2)}) collective-permute-start(bf16[512,128]{1,0:T(8,128)(2,1)S(1)} %get-tuple-element.39), channel_id=1, source_target_pairs={{0,28},{4,24},{8,20},{12,16},{16,12},{20,8},{24,4},{28,0},{1,29},{... | collective-permute-start | bytes 393224 | tf_op jit(solution)/shard_map/ppermute | solution.py:224
  10.8 7.6 %collective-permute-start.6 = (bf16[512,128]{1,0:T(8,128)(2,1)S(1)}, bf16[512,128]{1,0:T(8,128)(2,1)S(1)}, u32[]{:S(2)}, u32[]{:S(2)}) collective-permute-start(bf16[512,128]{1,0:T(8,128)(2,1)S(1)} %get-tuple-element.40), channel_id=1, source_target_pairs={{0,4},{4,0},{8,12},{12,8},{16,20},{20,16},{24,28},{28,24},{1,5},{5... | collective-permute-start | bytes 393224 | tf_op jit(solution)/shard_map/ppermute | solution.py:224
  13.4 0.7 %copy-start = (s32[80]{0:T(128)S(1)}, s32[80]{0:T(128)}, u32[]{:S(2)}) copy-start(s32[80]{0:T(128)} %lengths_ref.1) | copy-start | bytes 964
  32.4 7.4 %collective-permute-start.12 = (bf16[512,128]{1,0:T(8,128)(2,1)S(1)}, bf16[512,128]{1,0:T(8,128)(2,1)S(1)}, u32[]{:S(2)}, u32[]{:S(2)}) collective-permute-start(bf16[512,128]{1,0:T(8,128)(2,1)S(1)} %get-tuple-element.49.rest_0_), channel_id=1, source_target_pairs={{0,24},{4,28},{8,16},{12,20},{16,8},{20,12},{24,0},{28,4},{1,25},{... | collective-permute-start | bytes 393224 | tf_op jit(solution)/shard_map/ppermute | solution.py:224
  32.9 8.0 %collective-permute-start.10 = (bf16[512,128]{1,0:T(8,128)(2,1)S(1)}, bf16[512,128]{1,0:T(8,128)(2,1)S(1)}, u32[]{:S(2)}, u32[]{:S(2)}) collective-permute-start(bf16[512,128]{1,0:T(8,128)(2,1)S(1)} %get-tuple-element.49.rest_0_), channel_id=1, source_target_pairs={{0,16},{4,20},{8,24},{12,28},{16,0},{20,4},{24,8},{28,12},{1,17},{... | collective-permute-start | bytes 393224 | tf_op jit(solution)/shard_map/ppermute | solution.py:224
  34.4 6.5 %collective-permute-start.8 = (bf16[512,128]{1,0:T(8,128)(2,1)S(1)}, bf16[512,128]{1,0:T(8,128)(2,1)S(1)}, u32[]{:S(2)}, u32[]{:S(2)}) collective-permute-start(bf16[512,128]{1,0:T(8,128)(2,1)S(1)} %get-tuple-element.49.rest_0_), channel_id=1, source_target_pairs={{0,8},{4,12},{8,0},{12,4},{16,24},{20,28},{24,16},{28,20},{1,9},{5... | collective-permute-start | bytes 393224 | tf_op jit(solution)/shard_map/ppermute | solution.py:224
  35.9 6.4 %collective-permute-start.7 = (bf16[512,128]{1,0:T(8,128)(2,1)S(1)}, bf16[512,128]{1,0:T(8,128)(2,1)S(1)}, u32[]{:S(2)}, u32[]{:S(2)}) collective-permute-start(bf16[512,128]{1,0:T(8,128)(2,1)S(1)} %get-tuple-element.49.rest_0_), channel_id=1, source_target_pairs={{0,4},{4,0},{8,12},{12,8},{16,20},{20,16},{24,28},{28,24},{1,5},{5... | collective-permute-start | bytes 393224 | tf_op jit(solution)/shard_map/ppermute | solution.py:224
  39.7 2.6 %collective-permute-start.13 = (bf16[512,128]{1,0:T(8,128)(2,1)S(1)}, bf16[512,128]{1,0:T(8,128)(2,1)S(1)}, u32[]{:S(2)}, u32[]{:S(2)}) collective-permute-start(bf16[512,128]{1,0:T(8,128)(2,1)S(1)} %collective-permute-done.12.rest_6_), channel_id=1, source_target_pairs={{0,4},{4,0},{8,12},{12,8},{16,20},{20,16},{24,28},{28,24},{1,5},{5... | collective-permute-start | bytes 393224 | tf_op jit(solution)/shard_map/ppermute | solution.py:224
  40.9 1.4 %collective-permute-start.11 = (bf16[512,128]{1,0:T(8,128)(2,1)S(1)}, bf16[512,128]{1,0:T(8,128)(2,1)S(1)}, u32[]{:S(2)}, u32[]{:S(2)}) collective-permute-start(bf16[512,128]{1,0:T(8,128)(2,1)S(1)} %collective-permute-done.10.rest_4_), channel_id=1, source_target_pairs={{0,4},{4,0},{8,12},{12,8},{16,20},{20,16},{24,28},{28,24},{1,5},{5... | collective-permute-start | bytes 393224 | tf_op jit(solution)/shard_map/ppermute | solution.py:224
  40.9 1.5 %collective-permute-start.9 = (bf16[512,128]{1,0:T(8,128)(2,1)S(1)}, bf16[512,128]{1,0:T(8,128)(2,1)S(1)}, u32[]{:S(2)}, u32[]{:S(2)}) collective-permute-start(bf16[512,128]{1,0:T(8,128)(2,1)S(1)} %collective-permute-done.8.rest_2_), channel_id=1, source_target_pairs={{0,4},{4,0},{8,12},{12,8},{16,20},{20,16},{24,28},{28,24},{1,5},{5... | collective-permute-start | bytes 393224 | tf_op jit(solution)/shard_map/ppermute | solution.py:224

commit v4 on v3

--- a/solution.py
+++ b/solution.py
@@ -38,17 +38,28 @@
             outs[k][part * depth : (part + 1) * depth, :] = taken.astype(jnp.bfloat16)
 
 
-def join_kernel(n, chunks, *rest):
-    ins, out_ref, (held, wide, sems) = rest[:n], rest[n], rest[n + 1 :]
+def lay(rows, wide, part, depth, ins):
     me = lax.axis_index("shard")
+    for k, value in zip(rows, ins):
+        row = me ^ k
+        first = (row // 8) * (depth * 8) + row % 8
+        taken = value[part * depth : (part + 1) * depth, :]
+        wide[part, pl.ds(first, depth, stride=8), :] = taken.astype(jnp.float32)
+
+
+def lay_kernel(rows, *rest):
+    ins, wide = rest[:-1], rest[-1]
+    parts = wide.shape[0]
+    for part in range(parts):
+        lay(rows, wide, part, ins[0].shape[0] // parts, ins)
+
+
+def join_kernel(rows, *rest):
+    ins, (out_ref, wide, held, sems) = rest[1:-4], rest[-4:]
     parts, depth = held.shape[0], held.shape[2]
     copies = []
     for part in range(parts):
-        for k in range(n):
-            row = me ^ k
-            first = (row // 8) * (depth * 8) + row % 8
-            taken = ins[k][part * depth : (part + 1) * depth, :]
-            wide[part, pl.ds(first, depth, stride=8), :] = taken.astype(jnp.float32)
+        lay(rows, wide, part, depth, ins)
         held[part] = wide[part].reshape(held.shape[1:]).astype(jnp.bfloat16)
         target = out_ref.at[:, pl.ds(part * depth, depth)]
         copies.append(pltpu.make_async_copy(held.at[part], target, sems.at[part]))
@@ -308,17 +319,33 @@
         cost_estimate=pl.CostEstimate(flops=0, bytes_accessed=12 * width, transcendentals=0),
         name="store",
     )(new1, new2, new)
-    for k in range(0, n, 2):
+    new1, new2, new, own = lax.optimization_barrier((new1, new2, new, narrow))
+    gathered[1] = swap(own, "shard", n, 1)
+    for k in range(2, n, 2):
         gathered[k + 1] = swap(gathered[k], "shard", n, 1)
-    joined = pl.pallas_call(
-        functools.partial(join_kernel, n, chunks),
-        out_shape=jax.ShapeDtypeStruct((n // 8, chunks, 8, LANES), jnp.bfloat16),
-        in_specs=[VMEM] * n,
-        out_specs=HBM,
-        scratch_shapes=staging,
+    soon, last = [0, 1, *range(2, n, 2)], list(range(3, n, 2))
+    wide = jax.ShapeDtypeStruct((parts, n * depth, LANES), jnp.float32)
+    laid = pl.pallas_call(
+        functools.partial(lay_kernel, soon),
+        out_shape=wide,
+        in_specs=[VMEM] * len(soon),
+        out_specs=VMEM,
+        compiler_params=BIG,
+        cost_estimate=pl.CostEstimate(
+            flops=0, bytes_accessed=6 * width * len(soon), transcendentals=0
+        ),
+        name="lay",
+    )(*[gathered[k] for k in soon])
+    joined, unused = pl.pallas_call(
+        functools.partial(join_kernel, last),
+        out_shape=[jax.ShapeDtypeStruct((n // 8, chunks, 8, LANES), jnp.bfloat16), wide],
+        in_specs=[VMEM] * (1 + len(last)),
+        out_specs=[HBM, VMEM],
+        input_output_aliases={0: 1},
+        scratch_shapes=[staging[0], staging[2]],
         compiler_params=BIG,
         name="join",
-    )(*[gathered[k] for k in range(n)])
+    )(laid, *[gathered[k] for k in last])
     train = joined.transpose(0, 2, 1, 3).reshape(n, 1, width)
     return (new.reshape(width), new1.reshape(width), new2.reshape(width), train)
 

time: 44 us -> 43.8 us (level)
    pallas_call x1 -> x2, Pallas kernels: 1.39 us -> 1.47 us  [the longest x1 1.12 us: local(): pl.pallas_call(functools.partial(join_kernel, last), out_shape=[jax.Shape...]
  transfers between devices with their start and end apart: 14 -> 14, of which waited for: 6 -> 7; matrix products, arithmetic and copies ran while one was open for 0% -> 0% of each run, Pallas kernels for 8% -> 9%
where the time goes in v4:
time: 43.8 us; the launch traced here: 43.6 us
  starting transfers between devices  13.9 us (32%)
  blocking collectives  11.8 us (27%)
  Pallas kernels  8.78 us (20%)
  waiting for transfers between devices  7.06 us (16%)
  between operations  1.38 us (3%)
  local copies, waits for them, and re-layouts  0.65 us (1%)
    ppermute x14, starting transfers between devices, swap(): return lax.ppermute(value, axis, [(i, i ^ k) for i in range(size)])  13.9 us
    all_to_all x1, blocking collectives, local(): sums = lax.all_to_all(send, ('shard', 'tensor'), 0, 0, tiled=True)  11.8 us
    ppermute x14, waiting for transfers between devices, swap(): return lax.ppermute(value, axis, [(i, i ^ k) for i in range(size)])  7.06 us
    pallas_call x1, Pallas kernels, local(): pl.pallas_call(functools.partial(early_kernel, len(early)), out_shape=[fl...  2.51 us
    pallas_call x1, Pallas kernels, local(): pl.pallas_call(functools.partial(split_kernel, n, chunks), out_shape=[fla...  1.68 us
    pallas_call x1, Pallas kernels, local(): pl.pallas_call(functools.partial(update_kernel, len(late)), out_shape=[fl...  1.32 us
    pallas_call x1, Pallas kernels, local(): pl.pallas_call(functools.partial(join_kernel, last), out_shape=[jax.Shape...  1.12 us
    pallas_call x1, Pallas kernels, local(): pl.pallas_call(store_kernel, out_shape=[flat(jnp.float32)] * 3, in_specs=...  0.9 us
  transfers between devices with their start and end apart: 14, of which 7 were waited for; matrix products, arithmetic and copies ran while one was open for 0% of the time, Pallas kernels for 9%

profile of v4, /device:TPU:0, one launch (start us, length us, event | category | flops | bytes accessed | tf_op | source)
XLA Modules:
  0.0 43.6 jit_solution(5638038440148148922)
XLA Ops:
  0.6 1.7 %split.1 = (bf16[512,128]{1,0:T(8,128)(2,1)S(1)}, bf16[512,128]{1,0:T(8,128)(2,1)S(1)}, bf16[512,128]{1,0:T(8,128)(2,1)S(1)}, bf16[512,128]{1,0:T(8,128)(2,1)S(1...) custom-call(bf16[1,512,8,128]{3,2,1,0:T(8,128)(2,1)} %bitcast.12), custom_call_target="tpu_custom_call" | custom-call | tf_op jit(solution)/shard_map/split/pallas_call | solution.py:253
  2.3 3.0 %collective-permute-start = (bf16[512,128]{1,0:T(8,128)(2,1)S(1)}, bf16[512,128]{1,0:T(8,128)(2,1)S(1)}, u32[]{:S(2)}, u32[]{:S(2)}) collective-permute-start(bf16[512,128]{1,0:T(8,128)(2,1)S(1)} %get-tuple-element.33), channel_id=1, source_target_pairs={{0,8},{4,12},{8,0},{12,4},{16,24},{20,28},{24,16},{28,20},{1,9},{5... | collective-permute-start | bytes 393224 | tf_op jit(solution)/shard_map/ppermute | solution.py:235
  5.3 1.5 %collective-permute-start.1 = (bf16[512,128]{1,0:T(8,128)(2,1)S(1)}, bf16[512,128]{1,0:T(8,128)(2,1)S(1)}, u32[]{:S(2)}, u32[]{:S(2)}) collective-permute-start(bf16[512,128]{1,0:T(8,128)(2,1)S(1)} %get-tuple-element.34), channel_id=1, source_target_pairs={{0,16},{4,20},{8,24},{12,28},{16,0},{20,4},{24,8},{28,12},{1,17},{... | collective-permute-start | bytes 393224 | tf_op jit(solution)/shard_map/ppermute | solution.py:235
  6.8 0.0 collective-permute-start.2
  6.8 0.3 collective-permute-start.3
  7.2 2.9 %collective-permute-start.4 = (bf16[512,128]{1,0:T(8,128)(2,1)S(1)}, bf16[512,128]{1,0:T(8,128)(2,1)S(1)}, u32[]{:S(2)}, u32[]{:S(2)}) collective-permute-start(bf16[512,128]{1,0:T(8,128)(2,1)S(1)} %get-tuple-element.43), channel_id=1, source_target_pairs={{0,24},{4,28},{8,16},{12,20},{16,8},{20,12},{24,0},{28,4},{1,25},{... | collective-permute-start | bytes 393224 | tf_op jit(solution)/shard_map/ppermute | solution.py:235
  10.1 0.0 collective-permute-done.rest_1_
  10.1 0.0 collective-permute-start.5
  10.1 0.7 %collective-permute-done.1.rest_2_ = bf16[512,128]{1,0:T(8,128)(2,1)S(1)} collective-permute-done((bf16[512,128]{1,0:T(8,128)(2,1)S(1)}, bf16[512,128]{1,0:T(8,128)(2,1)S(1)}, u32[]{:S(2)}, u32[]{:S(2)}) %collective-permute-start.1) | collective-permute-done | bytes 131104 | tf_op jit(solution)/shard_map/ppermute | solution.py:235
  10.8 2.0 %collective-permute-start.6 = (bf16[512,128]{1,0:T(8,128)(2,1)S(1)}, bf16[512,128]{1,0:T(8,128)(2,1)S(1)}, u32[]{:S(2)}, u32[]{:S(2)}) collective-permute-start(bf16[512,128]{1,0:T(8,128)(2,1)S(1)} %get-tuple-element.45), channel_id=1, source_target_pairs={{0,4},{4,0},{8,12},{12,8},{16,20},{20,16},{24,28},{28,24},{1,5},{5... | collective-permute-start | bytes 393224 | tf_op jit(solution)/shard_map/ppermute | solution.py:235
  13.4 0.0 collective-permute-done.2.rest_3_
  13.4 0.0 copy-start
  13.5 0.6 %copy-done = s32[80]{0:T(128)S(1)} copy-done((s32[80]{0:T(128)S(1)}, s32[80]{0:T(128)}, u32[]{:S(2)}) %copy-start) | copy-done | bytes 344
  14.1 2.5 %early.1 = (f32[512,128]{1,0:T(8,128)S(1)}, f32[512,128]{1,0:T(8,128)S(1)}, f32[512,128]{1,0:T(8,128)S(1)}, f32[512,128]{1,0:T(8,128)S(1)}, f32[1,128]{1,0:T(1,128)S(1)}, /*index=5*/s32[83]{0:T(128)S(1)}) custom-call(s32[80]{0:T(128)S(1)} %copy-done, f32[512,128]{1,0:T(8,128)} %bitcast.13, f32[512,128]{1,0:T(8,128)} %bitcast.14, f32[512,128]{1,0:T(8,128)} %bitcast.15, ...), custom_call_target="tpu_custom_call" | custom-call | flops 524288 | bytes 1572864 | tf_op jit(solution)/shard_map/early/pallas_call | solution.py:273
  16.6 1.1 %collective-permute-done.3.rest_1_ = bf16[512,128]{1,0:T(8,128)(2,1)S(1)} collective-permute-done((bf16[512,128]{1,0:T(8,128)(2,1)S(1)}, bf16[512,128]{1,0:T(8,128)(2,1)S(1)}, u32[]{:S(2)}, u32[]{:S(2)}) %collective-permute-start.3) | collective-permute-done | bytes 131104 | tf_op jit(solution)/shard_map/ppermute | solution.py:235
  17.7 0.0 collective-permute-done.4.rest_2_
  17.8 0.6 %collective-permute-done.5.rest_3_ = bf16[512,128]{1,0:T(8,128)(2,1)S(1)} collective-permute-done((bf16[512,128]{1,0:T(8,128)(2,1)S(1)}, bf16[512,128]{1,0:T(8,128)(2,1)S(1)}, u32[]{:S(2)}, u32[]{:S(2)}) %collective-permute-start.5) | collective-permute-done | bytes 131104 | tf_op jit(solution)/shard_map/ppermute | solution.py:235
  18.4 0.0 collective-permute-done.6.rest_4_
  18.4 1.3 %update.1 = (f32[512,128]{1,0:T(8,128)S(1)}, f32[512,128]{1,0:T(8,128)S(1)}, f32[512,128]{1,0:T(8,128)S(1)}, f32[32,2,128]{2,1,0:T(2,128)S(1)}) custom-call(s32[1]{0:T(128)S(6)} %copy.12.step_ref, s32[83]{0:T(128)S(1)} %get-tuple-element.36.bounds_ref, f32[1,128]{1,0:T(1,128)S(1)} %get-tuple-element.37.sums_ref, ...), custom_call_target="tpu_custom_call" | custom-call | tf_op jit(solution)/shard_map/update/pallas_call | solution.py:289
  19.7 11.8 %all_to_all.5.sums_ref = f32[32,2,128]{2,1,0:T(2,128)S(1)} all-to-all(f32[32,2,128]{2,1,0:T(2,128)S(1)} %get-tuple-element.48), channel_id=1, replica_groups=mesh['shard'=8,'tensor'=4] {'shard','tensor'}, dimensions={0} | all-to-all | bytes 65536 | tf_op jit(solution)/shard_map/all_to_all | solution.py:299
  31.5 0.9 %new_weights.1 = (f32[512,128]{1,0:T(8,128)S(1)}, bf16[512,128]{1,0:T(8,128)(2,1)S(1)}) custom-call(s32[83]{0:T(128)S(1)} %get-tuple-element.36.bounds_ref, f32[32,2,128]{2,1,0:T(2,128)S(1)} %all_to_all.5.sums_ref, f32[512,128]{1,0:T(8,128)S(1)} %get-tuple-element.38.weights_ref, f32[512,128]{1,0:T(8,128)S(1)} %get-tuple-element.49.update_ref), custom_call_target="tpu_custom_call" | custom-call | tf_op jit(solution)/shard_map/new_weights/pallas_call | solution.py:300
  32.4 0.6 %collective-permute-start.10 = (bf16[512,128]{1,0:T(8,128)(2,1)S(1)}, bf16[512,128]{1,0:T(8,128)(2,1)S(1)}, u32[]{:S(2)}, u32[]{:S(2)}) collective-permute-start(bf16[512,128]{1,0:T(8,128)(2,1)S(1)} %get-tuple-element.58.rest_0_), channel_id=1, source_target_pairs={{0,24},{4,28},{8,16},{12,20},{16,8},{20,12},{24,0},{28,4},{1,25},{... | collective-permute-start | bytes 393224 | tf_op jit(solution)/shard_map/ppermute | solution.py:235
  33.0 1.4 %collective-permute-start.9 = (bf16[512,128]{1,0:T(8,128)(2,1)S(1)}, bf16[512,128]{1,0:T(8,128)(2,1)S(1)}, u32[]{:S(2)}, u32[]{:S(2)}) collective-permute-start(bf16[512,128]{1,0:T(8,128)(2,1)S(1)} %get-tuple-element.58.rest_0_), channel_id=1, source_target_pairs={{0,16},{4,20},{8,24},{12,28},{16,0},{20,4},{24,8},{28,12},{1,17},{... | collective-permute-start | bytes 393224 | tf_op jit(solution)/shard_map/ppermute | solution.py:235
  34.4 1.5 %collective-permute-start.8 = (bf16[512,128]{1,0:T(8,128)(2,1)S(1)}, bf16[512,128]{1,0:T(8,128)(2,1)S(1)}, u32[]{:S(2)}, u32[]{:S(2)}) collective-permute-start(bf16[512,128]{1,0:T(8,128)(2,1)S(1)} %get-tuple-element.58.rest_0_), channel_id=1, source_target_pairs={{0,8},{4,12},{8,0},{12,4},{16,24},{20,28},{24,16},{28,20},{1,9},{5... | collective-permute-start | bytes 393224 | tf_op jit(solution)/shard_map/ppermute | solution.py:235
  35.9 0.9 %store.1 = (f32[512,128]{1,0:T(8,128)}, f32[512,128]{1,0:T(8,128)}, f32[512,128]{1,0:T(8,128)}) custom-call(f32[512,128]{1,0:T(8,128)S(1)} %get-tuple-element.46.new1_ref, f32[512,128]{1,0:T(8,128)S(1)} %get-tuple-element.47.new2_ref, f32[512,128]{1,0:T(8,128)S(1)} %get-tuple-element.50.new_ref), custom_call_target="tpu_custom_call" | custom-call | bytes 786432 | tf_op jit(solution)/shard_map/store/pallas_call | solution.py:312
  36.8 0.1 collective-permute-start.7
  36.9 2.8 %collective-permute-done.10.rest_4_ = bf16[512,128]{1,0:T(8,128)(2,1)S(1)} collective-permute-done((bf16[512,128]{1,0:T(8,128)(2,1)S(1)}, bf16[512,128]{1,0:T(8,128)(2,1)S(1)}, u32[]{:S(2)}, u32[]{:S(2)}) %collective-permute-start.10) | collective-permute-done | bytes 131104 | tf_op jit(solution)/shard_map/ppermute | solution.py:235
  39.8 0.0 collective-permute-start.13
  39.8 1.2 %collective-permute-done.9.rest_3_ = bf16[512,128]{1,0:T(8,128)(2,1)S(1)} collective-permute-done((bf16[512,128]{1,0:T(8,128)(2,1)S(1)}, bf16[512,128]{1,0:T(8,128)(2,1)S(1)}, u32[]{:S(2)}, u32[]{:S(2)}) %collective-permute-start.9) | collective-permute-done | bytes 131104 | tf_op jit(solution)/shard_map/ppermute | solution.py:235
  40.9 0.0 collective-permute-start.12
  40.9 0.0 collective-permute-done.8.rest_2_
  40.9 0.5 %collective-permute-start.11 = (bf16[512,128]{1,0:T(8,128)(2,1)S(1)}, bf16[512,128]{1,0:T(8,128)(2,1)S(1)}, u32[]{:S(2)}, u32[]{:S(2)}) collective-permute-start(bf16[512,128]{1,0:T(8,128)(2,1)S(1)} %collective-permute-done.8.rest_2_), channel_id=1, source_target_pairs={{0,4},{4,0},{8,12},{12,8},{16,20},{20,16},{24,28},{28,24},{1,5},{5... | collective-permute-start | bytes 393224 | tf_op jit(solution)/shard_map/ppermute | solution.py:235
  41.4 0.0 collective-permute-done.7.rest_1_
  41.5 0.4 lay.1.rest_0_
  41.8 0.0 collective-permute-done.13.rest_3_
  41.8 0.5 %collective-permute-done.12.rest_2_ = bf16[512,128]{1,0:T(8,128)(2,1)S(1)} collective-permute-done((bf16[512,128]{1,0:T(8,128)(2,1)S(1)}, bf16[512,128]{1,0:T(8,128)(2,1)S(1)}, u32[]{:S(2)}, u32[]{:S(2)}) %collective-permute-start.12) | collective-permute-done | bytes 131104 | tf_op jit(solution)/shard_map/ppermute | solution.py:235
  42.3 0.2 collective-permute-done.11.rest_1_
  42.5 1.1 %join.1 = (bf16[1,512,8,128]{3,2,1,0:T(8,128)(2,1)}, f32[4,1024,128]{2,1,0:T(8,128)S(1)}) custom-call(f32[4,1024,128]{2,1,0:T(8,128)S(1)} %lay.1.rest_0_, bf16[512,128]{1,0:T(8,128)(2,1)S(1)} %collective-permute-done.11.rest_1_, bf16[512,128]{1,0:T(8,128)(2,1)S(1)} %collective-permute-done.12.rest_2_, ...), custom_call_target="tpu_custom_call", output_to_operand_aliasing={{1}: (0, {})} | custom-call | tf_op jit(solution)/shard_map/join/pallas_call | solution.py:339
Async XLA Ops:
  2.3 7.7 %collective-permute-start = (bf16[512,128]{1,0:T(8,128)(2,1)S(1)}, bf16[512,128]{1,0:T(8,128)(2,1)S(1)}, u32[]{:S(2)}, u32[]{:S(2)}) collective-permute-start(bf16[512,128]{1,0:T(8,128)(2,1)S(1)} %get-tuple-element.33), channel_id=1, source_target_pairs={{0,8},{4,12},{8,0},{12,4},{16,24},{20,28},{24,16},{28,20},{1,9},{5... | collective-permute-start | bytes 393224 | tf_op jit(solution)/shard_map/ppermute | solution.py:235
  5.3 5.4 %collective-permute-start.1 = (bf16[512,128]{1,0:T(8,128)(2,1)S(1)}, bf16[512,128]{1,0:T(8,128)(2,1)S(1)}, u32[]{:S(2)}, u32[]{:S(2)}) collective-permute-start(bf16[512,128]{1,0:T(8,128)(2,1)S(1)} %get-tuple-element.34), channel_id=1, source_target_pairs={{0,16},{4,20},{8,24},{12,28},{16,0},{20,4},{24,8},{28,12},{1,17},{... | collective-permute-start | bytes 393224 | tf_op jit(solution)/shard_map/ppermute | solution.py:235
  6.8 6.6 %collective-permute-start.2 = (bf16[512,128]{1,0:T(8,128)(2,1)S(1)}, bf16[512,128]{1,0:T(8,128)(2,1)S(1)}, u32[]{:S(2)}, u32[]{:S(2)}) collective-permute-start(bf16[512,128]{1,0:T(8,128)(2,1)S(1)} %get-tuple-element.35), channel_id=1, source_target_pairs={{0,12},{4,8},{8,4},{12,0},{16,28},{20,24},{24,20},{28,16},{1,13},{... | collective-permute-start | bytes 393224 | tf_op jit(solution)/shard_map/ppermute | solution.py:235
  6.8 10.9 %collective-permute-start.3 = (bf16[512,128]{1,0:T(8,128)(2,1)S(1)}, bf16[512,128]{1,0:T(8,128)(2,1)S(1)}, u32[]{:S(2)}, u32[]{:S(2)}) collective-permute-start(bf16[512,128]{1,0:T(8,128)(2,1)S(1)} %get-tuple-element.42), channel_id=1, source_target_pairs={{0,20},{4,16},{8,28},{12,24},{16,4},{20,0},{24,12},{28,8},{1,21},{... | collective-permute-start | bytes 393224 | tf_op jit(solution)/shard_map/ppermute | solution.py:235
  7.2 10.6 %collective-permute-start.4 = (bf16[512,128]{1,0:T(8,128)(2,1)S(1)}, bf16[512,128]{1,0:T(8,128)(2,1)S(1)}, u32[]{:S(2)}, u32[]{:S(2)}) collective-permute-start(bf16[512,128]{1,0:T(8,128)(2,1)S(1)} %get-tuple-element.43), channel_id=1, source_target_pairs={{0,24},{4,28},{8,16},{12,20},{16,8},{20,12},{24,0},{28,4},{1,25},{... | collective-permute-start | bytes 393224 | tf_op jit(solution)/shard_map/ppermute | solution.py:235
  10.1 8.3 %collective-permute-start.5 = (bf16[512,128]{1,0:T(8,128)(2,1)S(1)}, bf16[512,128]{1,0:T(8,128)(2,1)S(1)}, u32[]{:S(2)}, u32[]{:S(2)}) collective-permute-start(bf16[512,128]{1,0:T(8,128)(2,1)S(1)} %get-tuple-element.44), channel_id=1, source_target_pairs={{0,28},{4,24},{8,20},{12,16},{16,12},{20,8},{24,4},{28,0},{1,29},{... | collective-permute-start | bytes 393224 | tf_op jit(solution)/shard_map/ppermute | solution.py:235
  10.8 7.6 %collective-permute-start.6 = (bf16[512,128]{1,0:T(8,128)(2,1)S(1)}, bf16[512,128]{1,0:T(8,128)(2,1)S(1)}, u32[]{:S(2)}, u32[]{:S(2)}) collective-permute-start(bf16[512,128]{1,0:T(8,128)(2,1)S(1)} %get-tuple-element.45), channel_id=1, source_target_pairs={{0,4},{4,0},{8,12},{12,8},{16,20},{20,16},{24,28},{28,24},{1,5},{5... | collective-permute-start | bytes 393224 | tf_op jit(solution)/shard_map/ppermute | solution.py:235
  13.4 0.7 %copy-start = (s32[80]{0:T(128)S(1)}, s32[80]{0:T(128)}, u32[]{:S(2)}) copy-start(s32[80]{0:T(128)} %lengths_ref.1) | copy-start | bytes 964
  32.4 7.4 %collective-permute-start.10 = (bf16[512,128]{1,0:T(8,128)(2,1)S(1)}, bf16[512,128]{1,0:T(8,128)(2,1)S(1)}, u32[]{:S(2)}, u32[]{:S(2)}) collective-permute-start(bf16[512,128]{1,0:T(8,128)(2,1)S(1)} %get-tuple-element.58.rest_0_), channel_id=1, source_target_pairs={{0,24},{4,28},{8,16},{12,20},{16,8},{20,12},{24,0},{28,4},{1,25},{... | collective-permute-start | bytes 393224 | tf_op jit(solution)/shard_map/ppermute | solution.py:235
  33.0 8.0 %collective-permute-start.9 = (bf16[512,128]{1,0:T(8,128)(2,1)S(1)}, bf16[512,128]{1,0:T(8,128)(2,1)S(1)}, u32[]{:S(2)}, u32[]{:S(2)}) collective-permute-start(bf16[512,128]{1,0:T(8,128)(2,1)S(1)} %get-tuple-element.58.rest_0_), channel_id=1, source_target_pairs={{0,16},{4,20},{8,24},{12,28},{16,0},{20,4},{24,8},{28,12},{1,17},{... | collective-permute-start | bytes 393224 | tf_op jit(solution)/shard_map/ppermute | solution.py:235
  34.4 6.5 %collective-permute-start.8 = (bf16[512,128]{1,0:T(8,128)(2,1)S(1)}, bf16[512,128]{1,0:T(8,128)(2,1)S(1)}, u32[]{:S(2)}, u32[]{:S(2)}) collective-permute-start(bf16[512,128]{1,0:T(8,128)(2,1)S(1)} %get-tuple-element.58.rest_0_), channel_id=1, source_target_pairs={{0,8},{4,12},{8,0},{12,4},{16,24},{20,28},{24,16},{28,20},{1,9},{5... | collective-permute-start | bytes 393224 | tf_op jit(solution)/shard_map/ppermute | solution.py:235
  36.8 4.6 %collective-permute-start.7 = (bf16[512,128]{1,0:T(8,128)(2,1)S(1)}, bf16[512,128]{1,0:T(8,128)(2,1)S(1)}, u32[]{:S(2)}, u32[]{:S(2)}) collective-permute-start(bf16[512,128]{1,0:T(8,128)(2,1)S(1)} %get-tuple-element.58.rest_0_), channel_id=1, source_target_pairs={{0,4},{4,0},{8,12},{12,8},{16,20},{20,16},{24,28},{28,24},{1,5},{5... | collective-permute-start | bytes 393224 | tf_op jit(solution)/shard_map/ppermute | solution.py:235
  39.8 2.1 %collective-permute-start.13 = (bf16[512,128]{1,0:T(8,128)(2,1)S(1)}, bf16[512,128]{1,0:T(8,128)(2,1)S(1)}, u32[]{:S(2)}, u32[]{:S(2)}) collective-permute-start(bf16[512,128]{1,0:T(8,128)(2,1)S(1)} %collective-permute-done.10.rest_4_), channel_id=1, source_target_pairs={{0,4},{4,0},{8,12},{12,8},{16,20},{20,16},{24,28},{28,24},{1,5},{5... | collective-permute-start | bytes 393224 | tf_op jit(solution)/shard_map/ppermute | solution.py:235
  40.9 1.3 %collective-permute-start.12 = (bf16[512,128]{1,0:T(8,128)(2,1)S(1)}, bf16[512,128]{1,0:T(8,128)(2,1)S(1)}, u32[]{:S(2)}, u32[]{:S(2)}) collective-permute-start(bf16[512,128]{1,0:T(8,128)(2,1)S(1)} %collective-permute-done.9.rest_3_), channel_id=1, source_target_pairs={{0,4},{4,0},{8,12},{12,8},{16,20},{20,16},{24,28},{28,24},{1,5},{5... | collective-permute-start | bytes 393224 | tf_op jit(solution)/shard_map/ppermute | solution.py:235
  40.9 1.5 %collective-permute-start.11 = (bf16[512,128]{1,0:T(8,128)(2,1)S(1)}, bf16[512,128]{1,0:T(8,128)(2,1)S(1)}, u32[]{:S(2)}, u32[]{:S(2)}) collective-permute-start(bf16[512,128]{1,0:T(8,128)(2,1)S(1)} %collective-permute-done.8.rest_2_), channel_id=1, source_target_pairs={{0,4},{4,0},{8,12},{12,8},{16,20},{20,16},{24,28},{28,24},{1,5},{5... | collective-permute-start | bytes 393224 | tf_op jit(solution)/shard_map/ppermute | solution.py:235

commit v5 on v4

--- a/solution.py
+++ b/solution.py
@@ -117,10 +117,10 @@
     lax.fori_loop(bounds[count + 1], bounds[count + 2], segment, 0)
 
 
-def early_kernel(n, lengths_ref, weights_hbm, moment1_hbm, moment2_hbm, *rest):
+def early_kernel(n, step_ref, lengths_ref, weights_hbm, moment1_hbm, moment2_hbm, *rest):
     pieces = rest[:n]
-    weights_ref, moment1_ref, moment2_ref, partial_ref, sums_ref, bounds_ref = rest[n : n + 6]
-    squares, table, sems = rest[n + 6 :]
+    weights_ref, moment1_ref, moment2_ref, partial_ref, sums_ref, scales_ref = rest[n : n + 6]
+    bounds_ref, squares, table, sems = rest[n + 6 :]
     chunks = weights_ref.shape[0]
     pairs = ((weights_hbm, weights_ref), (moment1_hbm, moment1_ref), (moment2_hbm, moment2_ref))
     copies = [pltpu.make_async_copy(*pair, sems.at[i]) for i, pair in enumerate(pairs)]
@@ -153,6 +153,14 @@
         return carry
 
     lax.fori_loop(0, chunks // rows, add, 0)
+
+    def power(base):
+        return lax.fori_loop(
+            0, step_ref[0], lambda i, p: p * base, jnp.full((1, LANES), 1.0, jnp.float32)
+        )
+
+    scales_ref[0:1, :] = 1.0 / (1.0 - power(jnp.float32(0.9)))
+    scales_ref[1:2, :] = 1.0 / (1.0 - power(jnp.float32(0.999)))
     for copy in copies:
         copy.wait()
     squares[...] = weights_ref[...] * weights_ref[...]
@@ -160,19 +168,13 @@
     sums_ref[...] = jnp.sum(table[...].T, axis=0, keepdims=True)
 
 
-def update_kernel(n, step_ref, bounds_ref, sums_ref, weights_ref, moment1_ref, moment2_ref, *rest):
+def update_kernel(n, bounds_ref, scales_ref, sums_ref, weights_ref, moment1_ref, moment2_ref, *rest):
     partial_ref, pieces = rest[0], rest[1 : n + 1]
     rest = rest[1:]
     new1_ref, new2_ref, update_ref, send_ref = rest[n : n + 4]
     squares, table = rest[n + 4 :]
 
-    def power(base):
-        return lax.fori_loop(
-            0, step_ref[0], lambda i, p: p * base, jnp.full((8, LANES), 1.0, jnp.float32)
-        )
-
-    scale1 = (1.0 / (1.0 - power(jnp.float32(0.9))))[0:1, :]
-    scale2 = (1.0 / (1.0 - power(jnp.float32(0.999))))[0:1, :]
+    scale1, scale2 = scales_ref[0:1, :], scales_ref[1:2, :]
     chunks = weights_ref.shape[0]
     rows = math.gcd(chunks, TILE)
 
@@ -192,9 +194,9 @@
     lax.fori_loop(0, chunks // rows, block, 0, unroll=2)
     segment_rows(squares, table, bounds_ref)
     mine = jnp.sum(table[...].T, axis=0, keepdims=True)
-    which = lax.broadcasted_iota(jnp.int32, (2, LANES), 0)
-    both = jnp.where(which == 0, sums_ref[...], mine)
-    send_ref[...] = jnp.broadcast_to(both[None], send_ref.shape)
+    half = (send_ref.shape[0], LANES)
+    send_ref[:, :LANES] = jnp.broadcast_to(sums_ref[...], half)
+    send_ref[:, LANES:] = jnp.broadcast_to(mine, half)
 
 
 def weights_out_kernel(
@@ -205,8 +207,9 @@
     size = rows * LANES
     place = places(rows)
     count = bounds_ref.shape[0] - 3
-    both = jnp.sum(sums_ref[...], axis=0)
-    ratio = 0.25 * (jnp.sqrt(both[0:1, :]) / jnp.maximum(jnp.sqrt(both[1:2, :]), 1.0))
+    both = jnp.sum(sums_ref[...], axis=0, keepdims=True)
+    ratio = jnp.sqrt(both[:, :LANES]) / jnp.maximum(jnp.sqrt(both[:, LANES:]), 1.0)
+    ratio = 0.25 * ratio
     table[...] = jnp.broadcast_to(ratio, (LANES, LANES)).T
 
     def segment(k, carry):
@@ -270,32 +273,33 @@
         pltpu.with_memory_space_constraint(value.reshape(chunks, LANES), pltpu.HBM)
         for value in (weights, moment1, moment2)
     ]
-    weights, moment1, moment2, partial, sums, bounds = pl.pallas_call(
+    weights, moment1, moment2, partial, sums, scales, bounds = pl.pallas_call(
         functools.partial(early_kernel, len(early)),
         out_shape=[flat(jnp.float32)] * 4
         + [
             jax.ShapeDtypeStruct((1, LANES), jnp.float32),
+            jax.ShapeDtypeStruct((2, LANES), jnp.float32),
             jax.ShapeDtypeStruct((count + 3,), jnp.int32),
         ],
-        in_specs=[SMEM] + [HBM] * 3 + [VMEM] * len(early),
-        out_specs=[VMEM] * 5 + [SMEM],
+        in_specs=[SMEM] * 2 + [HBM] * 3 + [VMEM] * len(early),
+        out_specs=[VMEM] * 6 + [SMEM],
         scratch_shapes=square_table + [pltpu.SemaphoreType.DMA((3,))],
         compiler_params=BIG,
         cost_estimate=pl.CostEstimate(
             flops=8 * width, bytes_accessed=24 * width, transcendentals=0
         ),
         name="early",
-    )(lengths, *stored, *early)
+    )(step, lengths, *stored, *early)
     new1, new2, update, send = pl.pallas_call(
         functools.partial(update_kernel, len(late)),
         out_shape=[flat(jnp.float32)] * 3
-        + [jax.ShapeDtypeStruct((everyone, 2, LANES), jnp.float32)],
-        in_specs=[SMEM, SMEM] + [VMEM] * (5 + len(late)),
+        + [jax.ShapeDtypeStruct((everyone, 2 * LANES), jnp.float32)],
+        in_specs=[SMEM] + [VMEM] * (6 + len(late)),
         out_specs=[VMEM] * 4,
         scratch_shapes=square_table,
         compiler_params=BIG,
         name="update",
-    )(step, bounds, sums, weights, moment1, moment2, partial, *late)
+    )(bounds, scales, sums, weights, moment1, moment2, partial, *late)
     sums = lax.all_to_all(send, ("shard", "tensor"), 0, 0, tiled=True)
     new, narrow = pl.pallas_call(
         weights_out_kernel,

time: 43.8 us -> 43.8 us (level)
  transfers between devices with their start and end apart: 14 -> 14, of which waited for: 7 -> 7; matrix products, arithmetic and copies ran while one was open for 0% -> 0% of each run, Pallas kernels for 9% -> 8%
where the time goes in v5:
time: 43.8 us; the launch traced here: 43.6 us
  starting transfers between devices  13.9 us (32%)
  blocking collectives  11.9 us (27%)
  Pallas kernels  8.42 us (19%)
  waiting for transfers between devices  7.25 us (17%)
  between operations  1.38 us (3%)
  local copies, waits for them, and re-layouts  0.69 us (2%)
    ppermute x14, starting transfers between devices, swap(): return lax.ppermute(value, axis, [(i, i ^ k) for i in range(size)])  13.9 us
    all_to_all x1, blocking collectives, local(): sums = lax.all_to_all(send, ('shard', 'tensor'), 0, 0, tiled=True)  11.9 us
    ppermute x14, waiting for transfers between devices, swap(): return lax.ppermute(value, axis, [(i, i ^ k) for i in range(size)])  7.25 us
    pallas_call x1, Pallas kernels, local(): pl.pallas_call(functools.partial(early_kernel, len(early)), out_shape=[fl...  2.44 us
    pallas_call x1, Pallas kernels, local(): pl.pallas_call(functools.partial(split_kernel, n, chunks), out_shape=[fla...  1.68 us
    pallas_call x1, Pallas kernels, local(): pl.pallas_call(functools.partial(join_kernel, last), out_shape=[jax.Shape...  1.12 us
    pallas_call x1, Pallas kernels, local(): pl.pallas_call(functools.partial(update_kernel, len(late)), out_shape=[fl...  1.1 us
    pallas_call x1, Pallas kernels, local(): pl.pallas_call(store_kernel, out_shape=[flat(jnp.float32)] * 3, in_specs=...  0.9 us
  transfers between devices with their start and end apart: 14, of which 7 were waited for; matrix products, arithmetic and copies ran while one was open for 0% of the time, Pallas kernels for 8%

profile of v5, /device:TPU:0, one launch (start us, length us, event | category | flops | bytes accessed | tf_op | source)
XLA Modules:
  0.0 43.6 jit_solution(5851793729991655201)
XLA Ops:
  0.6 1.7 %split.1 = (bf16[512,128]{1,0:T(8,128)(2,1)S(1)}, bf16[512,128]{1,0:T(8,128)(2,1)S(1)}, bf16[512,128]{1,0:T(8,128)(2,1)S(1)}, bf16[512,128]{1,0:T(8,128)(2,1)S(1...) custom-call(bf16[1,512,8,128]{3,2,1,0:T(8,128)(2,1)} %bitcast.18), custom_call_target="tpu_custom_call" | custom-call | tf_op jit(solution)/shard_map/split/pallas_call | solution.py:256
  2.3 3.0 %collective-permute-start = (bf16[512,128]{1,0:T(8,128)(2,1)S(1)}, bf16[512,128]{1,0:T(8,128)(2,1)S(1)}, u32[]{:S(2)}, u32[]{:S(2)}) collective-permute-start(bf16[512,128]{1,0:T(8,128)(2,1)S(1)} %get-tuple-element.34), channel_id=1, source_target_pairs={{0,8},{4,12},{8,0},{12,4},{16,24},{20,28},{24,16},{28,20},{1,9},{5... | collective-permute-start | bytes 393224 | tf_op jit(solution)/shard_map/ppermute | solution.py:238
  5.3 1.5 %collective-permute-start.1 = (bf16[512,128]{1,0:T(8,128)(2,1)S(1)}, bf16[512,128]{1,0:T(8,128)(2,1)S(1)}, u32[]{:S(2)}, u32[]{:S(2)}) collective-permute-start(bf16[512,128]{1,0:T(8,128)(2,1)S(1)} %get-tuple-element.35), channel_id=1, source_target_pairs={{0,16},{4,20},{8,24},{12,28},{16,0},{20,4},{24,8},{28,12},{1,17},{... | collective-permute-start | bytes 393224 | tf_op jit(solution)/shard_map/ppermute | solution.py:238
  6.8 0.0 collective-permute-start.2
  6.8 0.3 collective-permute-start.3
  7.2 2.9 %collective-permute-start.4 = (bf16[512,128]{1,0:T(8,128)(2,1)S(1)}, bf16[512,128]{1,0:T(8,128)(2,1)S(1)}, u32[]{:S(2)}, u32[]{:S(2)}) collective-permute-start(bf16[512,128]{1,0:T(8,128)(2,1)S(1)} %get-tuple-element.45), channel_id=1, source_target_pairs={{0,24},{4,28},{8,16},{12,20},{16,8},{20,12},{24,0},{28,4},{1,25},{... | collective-permute-start | bytes 393224 | tf_op jit(solution)/shard_map/ppermute | solution.py:238
  10.1 0.0 collective-permute-done.rest_1_
  10.1 0.0 collective-permute-start.5
  10.1 0.7 %collective-permute-done.1.rest_2_ = bf16[512,128]{1,0:T(8,128)(2,1)S(1)} collective-permute-done((bf16[512,128]{1,0:T(8,128)(2,1)S(1)}, bf16[512,128]{1,0:T(8,128)(2,1)S(1)}, u32[]{:S(2)}, u32[]{:S(2)}) %collective-permute-start.1) | collective-permute-done | bytes 131104 | tf_op jit(solution)/shard_map/ppermute | solution.py:238
  10.8 2.0 %collective-permute-start.6 = (bf16[512,128]{1,0:T(8,128)(2,1)S(1)}, bf16[512,128]{1,0:T(8,128)(2,1)S(1)}, u32[]{:S(2)}, u32[]{:S(2)}) collective-permute-start(bf16[512,128]{1,0:T(8,128)(2,1)S(1)} %get-tuple-element.47), channel_id=1, source_target_pairs={{0,4},{4,0},{8,12},{12,8},{16,20},{20,16},{24,28},{28,24},{1,5},{5... | collective-permute-start | bytes 393224 | tf_op jit(solution)/shard_map/ppermute | solution.py:238
  13.4 0.0 collective-permute-done.2.rest_3_
  13.4 0.0 copy-start
  13.5 0.6 %copy-done = s32[80]{0:T(128)S(1)} copy-done((s32[80]{0:T(128)S(1)}, s32[80]{0:T(128)}, u32[]{:S(2)}) %copy-start) | copy-done | bytes 344
  14.1 2.4 %early.1 = (f32[512,128]{1,0:T(8,128)S(1)}, f32[512,128]{1,0:T(8,128)S(1)}, f32[512,128]{1,0:T(8,128)S(1)}, f32[512,128]{1,0:T(8,128)S(1)}, f32[1,128]{1,0:T(1,1...) custom-call(s32[1]{0:T(128)S(6)} %copy.16.step_ref, s32[80]{0:T(128)S(1)} %copy-done, f32[512,128]{1,0:T(8,128)} %bitcast.19, ...), custom_call_target="tpu_custom_call" | custom-call | flops 524288 | bytes 1572864 | tf_op jit(solution)/shard_map/early/pallas_call | solution.py:276
  16.6 1.2 %collective-permute-done.3.rest_1_ = bf16[512,128]{1,0:T(8,128)(2,1)S(1)} collective-permute-done((bf16[512,128]{1,0:T(8,128)(2,1)S(1)}, bf16[512,128]{1,0:T(8,128)(2,1)S(1)}, u32[]{:S(2)}, u32[]{:S(2)}) %collective-permute-start.3) | collective-permute-done | bytes 131104 | tf_op jit(solution)/shard_map/ppermute | solution.py:238
  17.7 0.0 collective-permute-done.4.rest_2_
  17.8 0.6 %collective-permute-done.5.rest_3_ = bf16[512,128]{1,0:T(8,128)(2,1)S(1)} collective-permute-done((bf16[512,128]{1,0:T(8,128)(2,1)S(1)}, bf16[512,128]{1,0:T(8,128)(2,1)S(1)}, u32[]{:S(2)}, u32[]{:S(2)}) %collective-permute-start.5) | collective-permute-done | bytes 131104 | tf_op jit(solution)/shard_map/ppermute | solution.py:238
  18.4 0.0 collective-permute-done.6.rest_4_
  18.4 1.1 %update.1 = (f32[512,128]{1,0:T(8,128)S(1)}, f32[512,128]{1,0:T(8,128)S(1)}, f32[512,128]{1,0:T(8,128)S(1)}, f32[32,256]{1,0:T(8,128)S(1)}) custom-call(s32[83]{0:T(128)S(1)} %get-tuple-element.37.bounds_ref, f32[2,128]{1,0:T(2,128)S(1)} %get-tuple-element.38.scales_ref, f32[1,128]{1,0:T(1,128)S(1)} %get-tuple-element.39.sums_ref, ...), custom_call_target="tpu_custom_call" | custom-call | tf_op jit(solution)/shard_map/update/pallas_call | solution.py:293
  19.5 11.9 %all_to_all.11 = f32[32,1,256]{2,1,0:T(1,128)S(1)} all-to-all(f32[32,1,256]{2,1,0:T(1,128)S(1)} %copy.11), channel_id=1, replica_groups=mesh['shard'=8,'tensor'=4] {'shard','tensor'}, dimensions={0} | all-to-all | bytes 65536 | tf_op jit(solution)/shard_map/all_to_all | solution.py:303
  31.4 0.8 %new_weights.1 = (f32[512,128]{1,0:T(8,128)S(1)}, bf16[512,128]{1,0:T(8,128)(2,1)S(1)}) custom-call(s32[83]{0:T(128)S(1)} %get-tuple-element.37.bounds_ref, f32[32,256]{1,0:T(8,128)S(1)} %bitcast.16, f32[512,128]{1,0:T(8,128)S(1)} %get-tuple-element.40.weights_ref, f32[512,128]{1,0:T(8,128)S(1)} %get-tuple-element.51.update_ref), custom_call_target="tpu_custom_call" | custom-call | tf_op jit(solution)/shard_map/new_weights/pallas_call | solution.py:304
  32.2 0.6 %collective-permute-start.10 = (bf16[512,128]{1,0:T(8,128)(2,1)S(1)}, bf16[512,128]{1,0:T(8,128)(2,1)S(1)}, u32[]{:S(2)}, u32[]{:S(2)}) collective-permute-start(bf16[512,128]{1,0:T(8,128)(2,1)S(1)} %get-tuple-element.60.rest_0_), channel_id=1, source_target_pairs={{0,24},{4,28},{8,16},{12,20},{16,8},{20,12},{24,0},{28,4},{1,25},{... | collective-permute-start | bytes 393224 | tf_op jit(solution)/shard_map/ppermute | solution.py:238
  32.8 1.6 %collective-permute-start.9 = (bf16[512,128]{1,0:T(8,128)(2,1)S(1)}, bf16[512,128]{1,0:T(8,128)(2,1)S(1)}, u32[]{:S(2)}, u32[]{:S(2)}) collective-permute-start(bf16[512,128]{1,0:T(8,128)(2,1)S(1)} %get-tuple-element.60.rest_0_), channel_id=1, source_target_pairs={{0,16},{4,20},{8,24},{12,28},{16,0},{20,4},{24,8},{28,12},{1,17},{... | collective-permute-start | bytes 393224 | tf_op jit(solution)/shard_map/ppermute | solution.py:238
  34.4 1.4 %collective-permute-start.8 = (bf16[512,128]{1,0:T(8,128)(2,1)S(1)}, bf16[512,128]{1,0:T(8,128)(2,1)S(1)}, u32[]{:S(2)}, u32[]{:S(2)}) collective-permute-start(bf16[512,128]{1,0:T(8,128)(2,1)S(1)} %get-tuple-element.60.rest_0_), channel_id=1, source_target_pairs={{0,8},{4,12},{8,0},{12,4},{16,24},{20,28},{24,16},{28,20},{1,9},{5... | collective-permute-start | bytes 393224 | tf_op jit(solution)/shard_map/ppermute | solution.py:238
  35.8 0.9 %store.1 = (f32[512,128]{1,0:T(8,128)}, f32[512,128]{1,0:T(8,128)}, f32[512,128]{1,0:T(8,128)}) custom-call(f32[512,128]{1,0:T(8,128)S(1)} %get-tuple-element.48.new1_ref, f32[512,128]{1,0:T(8,128)S(1)} %get-tuple-element.49.new2_ref, f32[512,128]{1,0:T(8,128)S(1)} %get-tuple-element.52.new_ref), custom_call_target="tpu_custom_call" | custom-call | bytes 786432 | tf_op jit(solution)/shard_map/store/pallas_call | solution.py:316
  36.7 0.1 collective-permute-start.7
  36.8 2.8 %collective-permute-done.10.rest_4_ = bf16[512,128]{1,0:T(8,128)(2,1)S(1)} collective-permute-done((bf16[512,128]{1,0:T(8,128)(2,1)S(1)}, bf16[512,128]{1,0:T(8,128)(2,1)S(1)}, u32[]{:S(2)}, u32[]{:S(2)}) %collective-permute-start.10) | collective-permute-done | bytes 131104 | tf_op jit(solution)/shard_map/ppermute | solution.py:238
  39.6 0.0 collective-permute-start.13
  39.6 1.3 %collective-permute-done.9.rest_3_ = bf16[512,128]{1,0:T(8,128)(2,1)S(1)} collective-permute-done((bf16[512,128]{1,0:T(8,128)(2,1)S(1)}, bf16[512,128]{1,0:T(8,128)(2,1)S(1)}, u32[]{:S(2)}, u32[]{:S(2)}) %collective-permute-start.9) | collective-permute-done | bytes 131104 | tf_op jit(solution)/shard_map/ppermute | solution.py:238
  40.9 0.0 collective-permute-start.12
  40.9 0.0 collective-permute-done.8.rest_2_
  40.9 0.5 %collective-permute-start.11 = (bf16[512,128]{1,0:T(8,128)(2,1)S(1)}, bf16[512,128]{1,0:T(8,128)(2,1)S(1)}, u32[]{:S(2)}, u32[]{:S(2)}) collective-permute-start(bf16[512,128]{1,0:T(8,128)(2,1)S(1)} %collective-permute-done.8.rest_2_), channel_id=1, source_target_pairs={{0,4},{4,0},{8,12},{12,8},{16,20},{20,16},{24,28},{28,24},{1,5},{5... | collective-permute-start | bytes 393224 | tf_op jit(solution)/shard_map/ppermute | solution.py:238
  41.4 0.0 collective-permute-done.7.rest_1_
  41.4 0.4 lay.1.rest_0_
  41.8 0.0 collective-permute-done.13.rest_3_
  41.8 0.5 %collective-permute-done.12.rest_2_ = bf16[512,128]{1,0:T(8,128)(2,1)S(1)} collective-permute-done((bf16[512,128]{1,0:T(8,128)(2,1)S(1)}, bf16[512,128]{1,0:T(8,128)(2,1)S(1)}, u32[]{:S(2)}, u32[]{:S(2)}) %collective-permute-start.12) | collective-permute-done | bytes 131104 | tf_op jit(solution)/shard_map/ppermute | solution.py:238
  42.3 0.2 collective-permute-done.11.rest_1_
  42.4 1.1 %join.1 = (bf16[1,512,8,128]{3,2,1,0:T(8,128)(2,1)}, f32[4,1024,128]{2,1,0:T(8,128)S(1)}) custom-call(f32[4,1024,128]{2,1,0:T(8,128)S(1)} %lay.1.rest_0_, bf16[512,128]{1,0:T(8,128)(2,1)S(1)} %collective-permute-done.11.rest_1_, bf16[512,128]{1,0:T(8,128)(2,1)S(1)} %collective-permute-done.12.rest_2_, ...), custom_call_target="tpu_custom_call", output_to_operand_aliasing={{1}: (0, {})} | custom-call | tf_op jit(solution)/shard_map/join/pallas_call | solution.py:343
  (2 shorter events, 0.0 us)
Async XLA Ops:
  2.3 7.7 %collective-permute-start = (bf16[512,128]{1,0:T(8,128)(2,1)S(1)}, bf16[512,128]{1,0:T(8,128)(2,1)S(1)}, u32[]{:S(2)}, u32[]{:S(2)}) collective-permute-start(bf16[512,128]{1,0:T(8,128)(2,1)S(1)} %get-tuple-element.34), channel_id=1, source_target_pairs={{0,8},{4,12},{8,0},{12,4},{16,24},{20,28},{24,16},{28,20},{1,9},{5... | collective-permute-start | bytes 393224 | tf_op jit(solution)/shard_map/ppermute | solution.py:238
  5.3 5.4 %collective-permute-start.1 = (bf16[512,128]{1,0:T(8,128)(2,1)S(1)}, bf16[512,128]{1,0:T(8,128)(2,1)S(1)}, u32[]{:S(2)}, u32[]{:S(2)}) collective-permute-start(bf16[512,128]{1,0:T(8,128)(2,1)S(1)} %get-tuple-element.35), channel_id=1, source_target_pairs={{0,16},{4,20},{8,24},{12,28},{16,0},{20,4},{24,8},{28,12},{1,17},{... | collective-permute-start | bytes 393224 | tf_op jit(solution)/shard_map/ppermute | solution.py:238
  6.8 6.6 %collective-permute-start.2 = (bf16[512,128]{1,0:T(8,128)(2,1)S(1)}, bf16[512,128]{1,0:T(8,128)(2,1)S(1)}, u32[]{:S(2)}, u32[]{:S(2)}) collective-permute-start(bf16[512,128]{1,0:T(8,128)(2,1)S(1)} %get-tuple-element.36), channel_id=1, source_target_pairs={{0,12},{4,8},{8,4},{12,0},{16,28},{20,24},{24,20},{28,16},{1,13},{... | collective-permute-start | bytes 393224 | tf_op jit(solution)/shard_map/ppermute | solution.py:238
  6.8 10.9 %collective-permute-start.3 = (bf16[512,128]{1,0:T(8,128)(2,1)S(1)}, bf16[512,128]{1,0:T(8,128)(2,1)S(1)}, u32[]{:S(2)}, u32[]{:S(2)}) collective-permute-start(bf16[512,128]{1,0:T(8,128)(2,1)S(1)} %get-tuple-element.44), channel_id=1, source_target_pairs={{0,20},{4,16},{8,28},{12,24},{16,4},{20,0},{24,12},{28,8},{1,21},{... | collective-permute-start | bytes 393224 | tf_op jit(solution)/shard_map/ppermute | solution.py:238
  7.2 10.6 %collective-permute-start.4 = (bf16[512,128]{1,0:T(8,128)(2,1)S(1)}, bf16[512,128]{1,0:T(8,128)(2,1)S(1)}, u32[]{:S(2)}, u32[]{:S(2)}) collective-permute-start(bf16[512,128]{1,0:T(8,128)(2,1)S(1)} %get-tuple-element.45), channel_id=1, source_target_pairs={{0,24},{4,28},{8,16},{12,20},{16,8},{20,12},{24,0},{28,4},{1,25},{... | collective-permute-start | bytes 393224 | tf_op jit(solution)/shard_map/ppermute | solution.py:238
  10.1 8.3 %collective-permute-start.5 = (bf16[512,128]{1,0:T(8,128)(2,1)S(1)}, bf16[512,128]{1,0:T(8,128)(2,1)S(1)}, u32[]{:S(2)}, u32[]{:S(2)}) collective-permute-start(bf16[512,128]{1,0:T(8,128)(2,1)S(1)} %get-tuple-element.46), channel_id=1, source_target_pairs={{0,28},{4,24},{8,20},{12,16},{16,12},{20,8},{24,4},{28,0},{1,29},{... | collective-permute-start | bytes 393224 | tf_op jit(solution)/shard_map/ppermute | solution.py:238
  10.8 7.6 %collective-permute-start.6 = (bf16[512,128]{1,0:T(8,128)(2,1)S(1)}, bf16[512,128]{1,0:T(8,128)(2,1)S(1)}, u32[]{:S(2)}, u32[]{:S(2)}) collective-permute-start(bf16[512,128]{1,0:T(8,128)(2,1)S(1)} %get-tuple-element.47), channel_id=1, source_target_pairs={{0,4},{4,0},{8,12},{12,8},{16,20},{20,16},{24,28},{28,24},{1,5},{5... | collective-permute-start | bytes 393224 | tf_op jit(solution)/shard_map/ppermute | solution.py:238
  13.4 0.7 %copy-start = (s32[80]{0:T(128)S(1)}, s32[80]{0:T(128)}, u32[]{:S(2)}) copy-start(s32[80]{0:T(128)} %lengths_ref.1) | copy-start | bytes 964
  32.2 7.4 %collective-permute-start.10 = (bf16[512,128]{1,0:T(8,128)(2,1)S(1)}, bf16[512,128]{1,0:T(8,128)(2,1)S(1)}, u32[]{:S(2)}, u32[]{:S(2)}) collective-permute-start(bf16[512,128]{1,0:T(8,128)(2,1)S(1)} %get-tuple-element.60.rest_0_), channel_id=1, source_target_pairs={{0,24},{4,28},{8,16},{12,20},{16,8},{20,12},{24,0},{28,4},{1,25},{... | collective-permute-start | bytes 393224 | tf_op jit(solution)/shard_map/ppermute | solution.py:238
  32.8 8.1 %collective-permute-start.9 = (bf16[512,128]{1,0:T(8,128)(2,1)S(1)}, bf16[512,128]{1,0:T(8,128)(2,1)S(1)}, u32[]{:S(2)}, u32[]{:S(2)}) collective-permute-start(bf16[512,128]{1,0:T(8,128)(2,1)S(1)} %get-tuple-element.60.rest_0_), channel_id=1, source_target_pairs={{0,16},{4,20},{8,24},{12,28},{16,0},{20,4},{24,8},{28,12},{1,17},{... | collective-permute-start | bytes 393224 | tf_op jit(solution)/shard_map/ppermute | solution.py:238
  34.4 6.5 %collective-permute-start.8 = (bf16[512,128]{1,0:T(8,128)(2,1)S(1)}, bf16[512,128]{1,0:T(8,128)(2,1)S(1)}, u32[]{:S(2)}, u32[]{:S(2)}) collective-permute-start(bf16[512,128]{1,0:T(8,128)(2,1)S(1)} %get-tuple-element.60.rest_0_), channel_id=1, source_target_pairs={{0,8},{4,12},{8,0},{12,4},{16,24},{20,28},{24,16},{28,20},{1,9},{5... | collective-permute-start | bytes 393224 | tf_op jit(solution)/shard_map/ppermute | solution.py:238
  36.7 4.7 %collective-permute-start.7 = (bf16[512,128]{1,0:T(8,128)(2,1)S(1)}, bf16[512,128]{1,0:T(8,128)(2,1)S(1)}, u32[]{:S(2)}, u32[]{:S(2)}) collective-permute-start(bf16[512,128]{1,0:T(8,128)(2,1)S(1)} %get-tuple-element.60.rest_0_), channel_id=1, source_target_pairs={{0,4},{4,0},{8,12},{12,8},{16,20},{20,16},{24,28},{28,24},{1,5},{5... | collective-permute-start | bytes 393224 | tf_op jit(solution)/shard_map/ppermute | solution.py:238
  39.6 2.2 %collective-permute-start.13 = (bf16[512,128]{1,0:T(8,128)(2,1)S(1)}, bf16[512,128]{1,0:T(8,128)(2,1)S(1)}, u32[]{:S(2)}, u32[]{:S(2)}) collective-permute-start(bf16[512,128]{1,0:T(8,128)(2,1)S(1)} %collective-permute-done.10.rest_4_), channel_id=1, source_target_pairs={{0,4},{4,0},{8,12},{12,8},{16,20},{20,16},{24,28},{28,24},{1,5},{5... | collective-permute-start | bytes 393224 | tf_op jit(solution)/shard_map/ppermute | solution.py:238
  40.9 1.3 %collective-permute-start.12 = (bf16[512,128]{1,0:T(8,128)(2,1)S(1)}, bf16[512,128]{1,0:T(8,128)(2,1)S(1)}, u32[]{:S(2)}, u32[]{:S(2)}) collective-permute-start(bf16[512,128]{1,0:T(8,128)(2,1)S(1)} %collective-permute-done.9.rest_3_), channel_id=1, source_target_pairs={{0,4},{4,0},{8,12},{12,8},{16,20},{20,16},{24,28},{28,24},{1,5},{5... | collective-permute-start | bytes 393224 | tf_op jit(solution)/shard_map/ppermute | solution.py:238
  40.9 1.5 %collective-permute-start.11 = (bf16[512,128]{1,0:T(8,128)(2,1)S(1)}, bf16[512,128]{1,0:T(8,128)(2,1)S(1)}, u32[]{:S(2)}, u32[]{:S(2)}) collective-permute-start(bf16[512,128]{1,0:T(8,128)(2,1)S(1)} %collective-permute-done.8.rest_2_), channel_id=1, source_target_pairs={{0,4},{4,0},{8,12},{12,8},{16,20},{20,16},{24,28},{28,24},{1,5},{5... | collective-permute-start | bytes 393224 | tf_op jit(solution)/shard_map/ppermute | solution.py:238

commit v6 on v5

--- a/solution.py
+++ b/solution.py
@@ -10,7 +10,7 @@
 
 LANES = 128
 TILE = 64
-PARTS = 4
+PARTS = 8
 ORDER = (2, 4, 3, 5, 6, 7, 1)
 EARLY = 3
 VMEM = pl.BlockSpec(memory_space=pltpu.VMEM)
@@ -68,15 +68,6 @@
         copy.wait()
 
 
-def store_kernel(new1_ref, new2_ref, new_ref, out1_ref, out2_ref, out_ref, sems):
-    pairs = ((new1_ref, out1_ref), (new2_ref, out2_ref), (new_ref, out_ref))
-    copies = [pltpu.make_async_copy(*pair, sems.at[i]) for i, pair in enumerate(pairs)]
-    for copy in copies:
-        copy.start()
-    for copy in copies:
-        copy.wait()
-
-
 def places(rows):
     place = lax.broadcasted_iota(jnp.int32, (rows, LANES), 0) * LANES
     return place + lax.broadcasted_iota(jnp.int32, (rows, LANES), 1)
@@ -199,34 +190,55 @@
     send_ref[:, LANES:] = jnp.broadcast_to(mine, half)
 
 
-def weights_out_kernel(
-    bounds_ref, sums_ref, weights_ref, update_ref, new_ref, narrow_ref, table
-):
-    chunks = weights_ref.shape[0]
+def scaled(bounds, table, weights, update, write):
+    chunks = weights.shape[0]
     rows = math.gcd(chunks, TILE)
     size = rows * LANES
     place = places(rows)
-    count = bounds_ref.shape[0] - 3
+    count = bounds.shape[0] - 3
+
+    def segment(k, carry):
+        low, high = bounds[k], bounds[k + 1]
+        scale = table[pl.ds(k, 1), :]
+
+        def step(t, carry):
+            part = pl.ds(pl.multiple_of(t * rows, rows), rows)
+            new = weights[part, :] - scale * update[part, :]
+            write(part, place >= low - t * size, new)
+            return carry
+
+        return lax.fori_loop(low // size, (high + (size - 1)) // size, step, carry)
+
+    lax.fori_loop(bounds[count + 1], bounds[count + 2], segment, 0)
+
+
+def narrow_kernel(bounds_ref, sums_ref, weights_ref, update_ref, narrow_ref, table):
     both = jnp.sum(sums_ref[...], axis=0, keepdims=True)
     ratio = jnp.sqrt(both[:, :LANES]) / jnp.maximum(jnp.sqrt(both[:, LANES:]), 1.0)
     ratio = 0.25 * ratio
     table[...] = jnp.broadcast_to(ratio, (LANES, LANES)).T
 
-    def segment(k, carry):
-        low, high = bounds_ref[k], bounds_ref[k + 1]
-        scale = table[pl.ds(k, 1), :]
-
-        def step(t, carry):
-            part = pl.ds(pl.multiple_of(t * rows, rows), rows)
-            new = weights_ref[part, :] - scale * update_ref[part, :]
-            new = jnp.where(place >= low - t * size, new, new_ref[part, :])
-            new_ref[part, :] = new
-            narrow_ref[part, :] = new.astype(jnp.bfloat16)
-            return carry
-
-        return lax.fori_loop(low // size, (high + (size - 1)) // size, step, carry)
-
-    lax.fori_loop(bounds_ref[count + 1], bounds_ref[count + 2], segment, 0)
+    def write(part, mine, new):
+        new = jnp.where(mine, new, narrow_ref[part, :].astype(jnp.float32))
+        narrow_ref[part, :] = new.astype(jnp.bfloat16)
+
+    scaled(bounds_ref, table, weights_ref, update_ref, write)
+
+
+def store_kernel(bounds_ref, table, weights_ref, update_ref, new1_ref, new2_ref, *rest):
+    out1_ref, out2_ref, out_ref, new_ref, sems = rest
+    pairs = ((new1_ref, out1_ref), (new2_ref, out2_ref), (new_ref, out_ref))
+    copies = [pltpu.make_async_copy(*pair, sems.at[i]) for i, pair in enumerate(pairs)]
+    copies[0].start()
+    copies[1].start()
+
+    def write(part, mine, new):
+        new_ref[part, :] = jnp.where(mine, new, new_ref[part, :])
+
+    scaled(bounds_ref, table, weights_ref, update_ref, write)
+    copies[2].start()
+    for copy in copies:
+        copy.wait()
 
 
 def exchange_order(n):
@@ -301,14 +313,13 @@
         name="update",
     )(bounds, scales, sums, weights, moment1, moment2, partial, *late)
     sums = lax.all_to_all(send, ("shard", "tensor"), 0, 0, tiled=True)
-    new, narrow = pl.pallas_call(
-        weights_out_kernel,
-        out_shape=[flat(jnp.float32), flat(jnp.bfloat16)],
+    narrow, table = pl.pallas_call(
+        narrow_kernel,
+        out_shape=[flat(jnp.bfloat16), jax.ShapeDtypeStruct((LANES, LANES), jnp.float32)],
         in_specs=[SMEM, VMEM, VMEM, VMEM],
         out_specs=[VMEM] * 2,
-        scratch_shapes=[pltpu.VMEM((LANES, LANES), jnp.float32)],
-        compiler_params=BIG,
-        name="new_weights",
+        compiler_params=BIG,
+        name="narrow_weights",
     )(bounds, sums, weights, update)
     gathered = {0: narrow}
     for k in range(2, n, 2):
@@ -316,13 +327,18 @@
     new1, new2, new = pl.pallas_call(
         store_kernel,
         out_shape=[flat(jnp.float32)] * 3,
-        in_specs=[VMEM] * 3,
+        in_specs=[SMEM] + [VMEM] * 5,
         out_specs=[HBM] * 3,
-        scratch_shapes=[pltpu.SemaphoreType.DMA((3,))],
-        compiler_params=BIG,
-        cost_estimate=pl.CostEstimate(flops=0, bytes_accessed=12 * width, transcendentals=0),
+        scratch_shapes=[
+            pltpu.VMEM((chunks, LANES), jnp.float32),
+            pltpu.SemaphoreType.DMA((3,)),
+        ],
+        compiler_params=BIG,
+        cost_estimate=pl.CostEstimate(
+            flops=4 * width, bytes_accessed=20 * width, transcendentals=0
+        ),
         name="store",
-    )(new1, new2, new)
+    )(bounds, table, weights, update, new1, new2)
     new1, new2, new, own = lax.optimization_barrier((new1, new2, new, narrow))
     gathered[1] = swap(own, "shard", n, 1)
     for k in range(2, n, 2):

time: 43.8 us -> 43.6 us (level)
  waiting for transfers between devices: 7.25 us -> 6.56 us
  Pallas kernels: 8.42 us -> 8.99 us
    ppermute x14, waiting for transfers between devices: 7.25 us -> 6.56 us  [swap(): return lax.ppermute(value, axis, [(i, i ^ k) for i in range(size)])]
    pallas_call x1, Pallas kernels: 0.9 us -> 1.45 us  [local(): pl.pallas_call(store_kernel, out_shape=[flat(jnp.float32)] * 3, in_specs=...]
  transfers between devices with their start and end apart: 14 -> 14, of which waited for: 7 -> 7; matrix products, arithmetic and copies ran while one was open for 0% -> 0% of each run, Pallas kernels for 8% -> 10%
where the time goes in v6:
time: 43.6 us; the launch traced here: 43.4 us
  starting transfers between devices  13.9 us (32%)
  blocking collectives  11.9 us (27%)
  Pallas kernels  8.99 us (21%)
  waiting for transfers between devices  6.56 us (15%)
  between operations  1.38 us (3%)
  local copies, waits for them, and re-layouts  0.69 us (2%)
    ppermute x14, starting transfers between devices, swap(): return lax.ppermute(value, axis, [(i, i ^ k) for i in range(size)])  13.9 us
    all_to_all x1, blocking collectives, local(): sums = lax.all_to_all(send, ('shard', 'tensor'), 0, 0, tiled=True)  11.9 us
    ppermute x14, waiting for transfers between devices, swap(): return lax.ppermute(value, axis, [(i, i ^ k) for i in range(size)])  6.56 us
    pallas_call x1, Pallas kernels, local(): pl.pallas_call(functools.partial(early_kernel, len(early)), out_shape=[fl...  2.48 us
    pallas_call x1, Pallas kernels, local(): pl.pallas_call(functools.partial(split_kernel, n, chunks), out_shape=[fla...  1.7 us
    pallas_call x1, Pallas kernels, local(): pl.pallas_call(store_kernel, out_shape=[flat(jnp.float32)] * 3, in_specs=...  1.45 us
    pallas_call x1, Pallas kernels, local(): pl.pallas_call(functools.partial(update_kernel, len(late)), out_shape=[fl...  1.14 us
    pallas_call x1, Pallas kernels, local(): pl.pallas_call(functools.partial(join_kernel, last), out_shape=[jax.Shape...  1.08 us
  transfers between devices with their start and end apart: 14, of which 7 were waited for; matrix products, arithmetic and copies ran while one was open for 0% of the time, Pallas kernels for 10%

profile of v6, /device:TPU:0, one launch (start us, length us, event | category | flops | bytes accessed | tf_op | source)
XLA Modules:
  0.0 43.4 jit_solution(1124622202493575478)
XLA Ops:
  0.6 1.7 %split.1 = (bf16[512,128]{1,0:T(8,128)(2,1)S(1)}, bf16[512,128]{1,0:T(8,128)(2,1)S(1)}, bf16[512,128]{1,0:T(8,128)(2,1)S(1)}, bf16[512,128]{1,0:T(8,128)(2,1)S(1...) custom-call(bf16[1,512,8,128]{3,2,1,0:T(8,128)(2,1)} %bitcast.18), custom_call_target="tpu_custom_call" | custom-call | tf_op jit(solution)/shard_map/split/pallas_call | solution.py:268
  2.3 3.0 %collective-permute-start = (bf16[512,128]{1,0:T(8,128)(2,1)S(1)}, bf16[512,128]{1,0:T(8,128)(2,1)S(1)}, u32[]{:S(2)}, u32[]{:S(2)}) collective-permute-start(bf16[512,128]{1,0:T(8,128)(2,1)S(1)} %get-tuple-element.34), channel_id=1, source_target_pairs={{0,8},{4,12},{8,0},{12,4},{16,24},{20,28},{24,16},{28,20},{1,9},{5... | collective-permute-start | bytes 393224 | tf_op jit(solution)/shard_map/ppermute | solution.py:250
  5.3 1.5 %collective-permute-start.1 = (bf16[512,128]{1,0:T(8,128)(2,1)S(1)}, bf16[512,128]{1,0:T(8,128)(2,1)S(1)}, u32[]{:S(2)}, u32[]{:S(2)}) collective-permute-start(bf16[512,128]{1,0:T(8,128)(2,1)S(1)} %get-tuple-element.35), channel_id=1, source_target_pairs={{0,16},{4,20},{8,24},{12,28},{16,0},{20,4},{24,8},{28,12},{1,17},{... | collective-permute-start | bytes 393224 | tf_op jit(solution)/shard_map/ppermute | solution.py:250
  6.9 0.0 collective-permute-start.2
  6.9 0.3 collective-permute-start.3
  7.2 2.9 %collective-permute-start.4 = (bf16[512,128]{1,0:T(8,128)(2,1)S(1)}, bf16[512,128]{1,0:T(8,128)(2,1)S(1)}, u32[]{:S(2)}, u32[]{:S(2)}) collective-permute-start(bf16[512,128]{1,0:T(8,128)(2,1)S(1)} %get-tuple-element.45), channel_id=1, source_target_pairs={{0,24},{4,28},{8,16},{12,20},{16,8},{20,12},{24,0},{28,4},{1,25},{... | collective-permute-start | bytes 393224 | tf_op jit(solution)/shard_map/ppermute | solution.py:250
  10.1 0.0 collective-permute-done.rest_1_
  10.1 0.0 collective-permute-start.5
  10.1 0.7 %collective-permute-done.1.rest_2_ = bf16[512,128]{1,0:T(8,128)(2,1)S(1)} collective-permute-done((bf16[512,128]{1,0:T(8,128)(2,1)S(1)}, bf16[512,128]{1,0:T(8,128)(2,1)S(1)}, u32[]{:S(2)}, u32[]{:S(2)}) %collective-permute-start.1) | collective-permute-done | bytes 131104 | tf_op jit(solution)/shard_map/ppermute | solution.py:250
  10.8 2.0 %collective-permute-start.6 = (bf16[512,128]{1,0:T(8,128)(2,1)S(1)}, bf16[512,128]{1,0:T(8,128)(2,1)S(1)}, u32[]{:S(2)}, u32[]{:S(2)}) collective-permute-start(bf16[512,128]{1,0:T(8,128)(2,1)S(1)} %get-tuple-element.47), channel_id=1, source_target_pairs={{0,4},{4,0},{8,12},{12,8},{16,20},{20,16},{24,28},{28,24},{1,5},{5... | collective-permute-start | bytes 393224 | tf_op jit(solution)/shard_map/ppermute | solution.py:250
  13.4 0.0 collective-permute-done.2.rest_3_
  13.5 0.0 copy-start
  13.5 0.6 %copy-done = s32[80]{0:T(128)S(1)} copy-done((s32[80]{0:T(128)S(1)}, s32[80]{0:T(128)}, u32[]{:S(2)}) %copy-start) | copy-done | bytes 344
  14.1 2.5 %early.1 = (f32[512,128]{1,0:T(8,128)S(1)}, f32[512,128]{1,0:T(8,128)S(1)}, f32[512,128]{1,0:T(8,128)S(1)}, f32[512,128]{1,0:T(8,128)S(1)}, f32[1,128]{1,0:T(1,1...) custom-call(s32[1]{0:T(128)S(6)} %copy.16.step_ref, s32[80]{0:T(128)S(1)} %copy-done, f32[512,128]{1,0:T(8,128)} %bitcast.19, ...), custom_call_target="tpu_custom_call" | custom-call | flops 524288 | bytes 1572864 | tf_op jit(solution)/shard_map/early/pallas_call | solution.py:288
  16.6 1.2 %collective-permute-done.3.rest_1_ = bf16[512,128]{1,0:T(8,128)(2,1)S(1)} collective-permute-done((bf16[512,128]{1,0:T(8,128)(2,1)S(1)}, bf16[512,128]{1,0:T(8,128)(2,1)S(1)}, u32[]{:S(2)}, u32[]{:S(2)}) %collective-permute-start.3) | collective-permute-done | bytes 131104 | tf_op jit(solution)/shard_map/ppermute | solution.py:250
  17.8 0.0 collective-permute-done.4.rest_2_
  17.8 0.6 %collective-permute-done.5.rest_3_ = bf16[512,128]{1,0:T(8,128)(2,1)S(1)} collective-permute-done((bf16[512,128]{1,0:T(8,128)(2,1)S(1)}, bf16[512,128]{1,0:T(8,128)(2,1)S(1)}, u32[]{:S(2)}, u32[]{:S(2)}) %collective-permute-start.5) | collective-permute-done | bytes 131104 | tf_op jit(solution)/shard_map/ppermute | solution.py:250
  18.4 0.0 collective-permute-done.6.rest_4_
  18.4 1.1 %update.1 = (f32[512,128]{1,0:T(8,128)S(1)}, f32[512,128]{1,0:T(8,128)S(1)}, f32[512,128]{1,0:T(8,128)S(1)}, f32[32,256]{1,0:T(8,128)S(1)}) custom-call(s32[83]{0:T(128)S(1)} %get-tuple-element.37.bounds_ref, f32[2,128]{1,0:T(2,128)S(1)} %get-tuple-element.38.scales_ref, f32[1,128]{1,0:T(1,128)S(1)} %get-tuple-element.39.sums_ref, ...), custom_call_target="tpu_custom_call" | custom-call | tf_op jit(solution)/shard_map/update/pallas_call | solution.py:305
  19.6 11.9 %all_to_all.11 = f32[32,1,256]{2,1,0:T(1,128)S(1)} all-to-all(f32[32,1,256]{2,1,0:T(1,128)S(1)} %copy.11), channel_id=1, replica_groups=mesh['shard'=8,'tensor'=4] {'shard','tensor'}, dimensions={0} | all-to-all | bytes 65536 | tf_op jit(solution)/shard_map/all_to_all | solution.py:315
  31.4 0.8 %narrow_weights.1 = (bf16[512,128]{1,0:T(8,128)(2,1)S(1)}, f32[128,128]{1,0:T(8,128)S(1)}) custom-call(s32[83]{0:T(128)S(1)} %get-tuple-element.37.bounds_ref, f32[32,256]{1,0:T(8,128)S(1)} %bitcast.16, f32[512,128]{1,0:T(8,128)S(1)} %get-tuple-element.40.weights_ref, f32[512,128]{1,0:T(8,128)S(1)} %get-tuple-element.49.update_ref), custom_call_target="tpu_custom_call" | custom-call | tf_op jit(solution)/shard_map/narrow_weights/pallas_call | solution.py:316
  32.3 0.7 %collective-permute-start.10 = (bf16[512,128]{1,0:T(8,128)(2,1)S(1)}, bf16[512,128]{1,0:T(8,128)(2,1)S(1)}, u32[]{:S(2)}, u32[]{:S(2)}) collective-permute-start(bf16[512,128]{1,0:T(8,128)(2,1)S(1)} %get-tuple-element.60.rest_0_), channel_id=1, source_target_pairs={{0,24},{4,28},{8,16},{12,20},{16,8},{20,12},{24,0},{28,4},{1,25},{... | collective-permute-start | bytes 393224 | tf_op jit(solution)/shard_map/ppermute | solution.py:250
  33.0 1.5 %collective-permute-start.9 = (bf16[512,128]{1,0:T(8,128)(2,1)S(1)}, bf16[512,128]{1,0:T(8,128)(2,1)S(1)}, u32[]{:S(2)}, u32[]{:S(2)}) collective-permute-start(bf16[512,128]{1,0:T(8,128)(2,1)S(1)} %get-tuple-element.60.rest_0_), channel_id=1, source_target_pairs={{0,16},{4,20},{8,24},{12,28},{16,0},{20,4},{24,8},{28,12},{1,17},{... | collective-permute-start | bytes 393224 | tf_op jit(solution)/shard_map/ppermute | solution.py:250
  34.4 1.4 %collective-permute-start.8 = (bf16[512,128]{1,0:T(8,128)(2,1)S(1)}, bf16[512,128]{1,0:T(8,128)(2,1)S(1)}, u32[]{:S(2)}, u32[]{:S(2)}) collective-permute-start(bf16[512,128]{1,0:T(8,128)(2,1)S(1)} %get-tuple-element.60.rest_0_), channel_id=1, source_target_pairs={{0,8},{4,12},{8,0},{12,4},{16,24},{20,28},{24,16},{28,20},{1,9},{5... | collective-permute-start | bytes 393224 | tf_op jit(solution)/shard_map/ppermute | solution.py:250
  35.8 1.5 %store.1 = (f32[512,128]{1,0:T(8,128)}, f32[512,128]{1,0:T(8,128)}, f32[512,128]{1,0:T(8,128)}) custom-call(s32[83]{0:T(128)S(1)} %get-tuple-element.37.bounds_ref, f32[128,128]{1,0:T(8,128)S(1)} %get-tuple-element.50.table, f32[512,128]{1,0:T(8,128)S(1)} %get-tuple-element.40.weights_ref, f32[512,128]{1,0:T(8,128)S(1)} %get-tuple-element.49.update_ref, ...), custom_call_target="tpu_custom_call" | custom-call | flops 262144 | bytes 1310720 | tf_op jit(solution)/shard_map/store/pallas_call | solution.py:327
  37.3 0.1 collective-permute-start.7
  37.4 2.3 %collective-permute-done.10.rest_4_ = bf16[512,128]{1,0:T(8,128)(2,1)S(1)} collective-permute-done((bf16[512,128]{1,0:T(8,128)(2,1)S(1)}, bf16[512,128]{1,0:T(8,128)(2,1)S(1)}, u32[]{:S(2)}, u32[]{:S(2)}) %collective-permute-start.10) | collective-permute-done | bytes 131104 | tf_op jit(solution)/shard_map/ppermute | solution.py:250
  39.6 0.0 collective-permute-start.13
  39.6 1.2 %collective-permute-done.9.rest_3_ = bf16[512,128]{1,0:T(8,128)(2,1)S(1)} collective-permute-done((bf16[512,128]{1,0:T(8,128)(2,1)S(1)}, bf16[512,128]{1,0:T(8,128)(2,1)S(1)}, u32[]{:S(2)}, u32[]{:S(2)}) %collective-permute-start.9) | collective-permute-done | bytes 131104 | tf_op jit(solution)/shard_map/ppermute | solution.py:250
  40.8 0.0 collective-permute-start.12
  40.8 0.0 collective-permute-done.8.rest_2_
  40.8 0.5 %collective-permute-start.11 = (bf16[512,128]{1,0:T(8,128)(2,1)S(1)}, bf16[512,128]{1,0:T(8,128)(2,1)S(1)}, u32[]{:S(2)}, u32[]{:S(2)}) collective-permute-start(bf16[512,128]{1,0:T(8,128)(2,1)S(1)} %collective-permute-done.8.rest_2_), channel_id=1, source_target_pairs={{0,4},{4,0},{8,12},{12,8},{16,20},{20,16},{24,28},{28,24},{1,5},{5... | collective-permute-start | bytes 393224 | tf_op jit(solution)/shard_map/ppermute | solution.py:250
  41.3 0.0 collective-permute-done.7.rest_1_
  41.3 0.3 lay.1.rest_0_
  41.6 0.0 collective-permute-done.13.rest_3_
  41.6 0.5 %collective-permute-done.12.rest_2_ = bf16[512,128]{1,0:T(8,128)(2,1)S(1)} collective-permute-done((bf16[512,128]{1,0:T(8,128)(2,1)S(1)}, bf16[512,128]{1,0:T(8,128)(2,1)S(1)}, u32[]{:S(2)}, u32[]{:S(2)}) %collective-permute-start.12) | collective-permute-done | bytes 131104 | tf_op jit(solution)/shard_map/ppermute | solution.py:250
  42.1 0.2 collective-permute-done.11.rest_1_
  42.3 1.1 %join.1 = (bf16[1,512,8,128]{3,2,1,0:T(8,128)(2,1)}, f32[8,512,128]{2,1,0:T(8,128)S(1)}) custom-call(f32[8,512,128]{2,1,0:T(8,128)S(1)} %lay.1.rest_0_, bf16[512,128]{1,0:T(8,128)(2,1)S(1)} %collective-permute-done.11.rest_1_, bf16[512,128]{1,0:T(8,128)(2,1)S(1)} %collective-permute-done.12.rest_2_, ...), custom_call_target="tpu_custom_call", output_to_operand_aliasing={{1}: (0, {})} | custom-call | tf_op jit(solution)/shard_map/join/pallas_call | solution.py:359
  (2 shorter events, 0.0 us)
Async XLA Ops:
  2.3 7.7 %collective-permute-start = (bf16[512,128]{1,0:T(8,128)(2,1)S(1)}, bf16[512,128]{1,0:T(8,128)(2,1)S(1)}, u32[]{:S(2)}, u32[]{:S(2)}) collective-permute-start(bf16[512,128]{1,0:T(8,128)(2,1)S(1)} %get-tuple-element.34), channel_id=1, source_target_pairs={{0,8},{4,12},{8,0},{12,4},{16,24},{20,28},{24,16},{28,20},{1,9},{5... | collective-permute-start | bytes 393224 | tf_op jit(solution)/shard_map/ppermute | solution.py:250
  5.3 5.4 %collective-permute-start.1 = (bf16[512,128]{1,0:T(8,128)(2,1)S(1)}, bf16[512,128]{1,0:T(8,128)(2,1)S(1)}, u32[]{:S(2)}, u32[]{:S(2)}) collective-permute-start(bf16[512,128]{1,0:T(8,128)(2,1)S(1)} %get-tuple-element.35), channel_id=1, source_target_pairs={{0,16},{4,20},{8,24},{12,28},{16,0},{20,4},{24,8},{28,12},{1,17},{... | collective-permute-start | bytes 393224 | tf_op jit(solution)/shard_map/ppermute | solution.py:250
  6.9 6.6 %collective-permute-start.2 = (bf16[512,128]{1,0:T(8,128)(2,1)S(1)}, bf16[512,128]{1,0:T(8,128)(2,1)S(1)}, u32[]{:S(2)}, u32[]{:S(2)}) collective-permute-start(bf16[512,128]{1,0:T(8,128)(2,1)S(1)} %get-tuple-element.36), channel_id=1, source_target_pairs={{0,12},{4,8},{8,4},{12,0},{16,28},{20,24},{24,20},{28,16},{1,13},{... | collective-permute-start | bytes 393224 | tf_op jit(solution)/shard_map/ppermute | solution.py:250
  6.9 10.9 %collective-permute-start.3 = (bf16[512,128]{1,0:T(8,128)(2,1)S(1)}, bf16[512,128]{1,0:T(8,128)(2,1)S(1)}, u32[]{:S(2)}, u32[]{:S(2)}) collective-permute-start(bf16[512,128]{1,0:T(8,128)(2,1)S(1)} %get-tuple-element.44), channel_id=1, source_target_pairs={{0,20},{4,16},{8,28},{12,24},{16,4},{20,0},{24,12},{28,8},{1,21},{... | collective-permute-start | bytes 393224 | tf_op jit(solution)/shard_map/ppermute | solution.py:250
  7.2 10.6 %collective-permute-start.4 = (bf16[512,128]{1,0:T(8,128)(2,1)S(1)}, bf16[512,128]{1,0:T(8,128)(2,1)S(1)}, u32[]{:S(2)}, u32[]{:S(2)}) collective-permute-start(bf16[512,128]{1,0:T(8,128)(2,1)S(1)} %get-tuple-element.45), channel_id=1, source_target_pairs={{0,24},{4,28},{8,16},{12,20},{16,8},{20,12},{24,0},{28,4},{1,25},{... | collective-permute-start | bytes 393224 | tf_op jit(solution)/shard_map/ppermute | solution.py:250
  10.1 8.3 %collective-permute-start.5 = (bf16[512,128]{1,0:T(8,128)(2,1)S(1)}, bf16[512,128]{1,0:T(8,128)(2,1)S(1)}, u32[]{:S(2)}, u32[]{:S(2)}) collective-permute-start(bf16[512,128]{1,0:T(8,128)(2,1)S(1)} %get-tuple-element.46), channel_id=1, source_target_pairs={{0,28},{4,24},{8,20},{12,16},{16,12},{20,8},{24,4},{28,0},{1,29},{... | collective-permute-start | bytes 393224 | tf_op jit(solution)/shard_map/ppermute | solution.py:250
  10.8 7.6 %collective-permute-start.6 = (bf16[512,128]{1,0:T(8,128)(2,1)S(1)}, bf16[512,128]{1,0:T(8,128)(2,1)S(1)}, u32[]{:S(2)}, u32[]{:S(2)}) collective-permute-start(bf16[512,128]{1,0:T(8,128)(2,1)S(1)} %get-tuple-element.47), channel_id=1, source_target_pairs={{0,4},{4,0},{8,12},{12,8},{16,20},{20,16},{24,28},{28,24},{1,5},{5... | collective-permute-start | bytes 393224 | tf_op jit(solution)/shard_map/ppermute | solution.py:250
  13.5 0.7 %copy-start = (s32[80]{0:T(128)S(1)}, s32[80]{0:T(128)}, u32[]{:S(2)}) copy-start(s32[80]{0:T(128)} %lengths_ref.1) | copy-start | bytes 964
  32.3 7.4 %collective-permute-start.10 = (bf16[512,128]{1,0:T(8,128)(2,1)S(1)}, bf16[512,128]{1,0:T(8,128)(2,1)S(1)}, u32[]{:S(2)}, u32[]{:S(2)}) collective-permute-start(bf16[512,128]{1,0:T(8,128)(2,1)S(1)} %get-tuple-element.60.rest_0_), channel_id=1, source_target_pairs={{0,24},{4,28},{8,16},{12,20},{16,8},{20,12},{24,0},{28,4},{1,25},{... | collective-permute-start | bytes 393224 | tf_op jit(solution)/shard_map/ppermute | solution.py:250
  33.0 7.8 %collective-permute-start.9 = (bf16[512,128]{1,0:T(8,128)(2,1)S(1)}, bf16[512,128]{1,0:T(8,128)(2,1)S(1)}, u32[]{:S(2)}, u32[]{:S(2)}) collective-permute-start(bf16[512,128]{1,0:T(8,128)(2,1)S(1)} %get-tuple-element.60.rest_0_), channel_id=1, source_target_pairs={{0,16},{4,20},{8,24},{12,28},{16,0},{20,4},{24,8},{28,12},{1,17},{... | collective-permute-start | bytes 393224 | tf_op jit(solution)/shard_map/ppermute | solution.py:250
  34.4 6.4 %collective-permute-start.8 = (bf16[512,128]{1,0:T(8,128)(2,1)S(1)}, bf16[512,128]{1,0:T(8,128)(2,1)S(1)}, u32[]{:S(2)}, u32[]{:S(2)}) collective-permute-start(bf16[512,128]{1,0:T(8,128)(2,1)S(1)} %get-tuple-element.60.rest_0_), channel_id=1, source_target_pairs={{0,8},{4,12},{8,0},{12,4},{16,24},{20,28},{24,16},{28,20},{1,9},{5... | collective-permute-start | bytes 393224 | tf_op jit(solution)/shard_map/ppermute | solution.py:250
  37.3 4.0 %collective-permute-start.7 = (bf16[512,128]{1,0:T(8,128)(2,1)S(1)}, bf16[512,128]{1,0:T(8,128)(2,1)S(1)}, u32[]{:S(2)}, u32[]{:S(2)}) collective-permute-start(bf16[512,128]{1,0:T(8,128)(2,1)S(1)} %get-tuple-element.60.rest_0_), channel_id=1, source_target_pairs={{0,4},{4,0},{8,12},{12,8},{16,20},{20,16},{24,28},{28,24},{1,5},{5... | collective-permute-start | bytes 393224 | tf_op jit(solution)/shard_map/ppermute | solution.py:250
  39.6 2.0 %collective-permute-start.13 = (bf16[512,128]{1,0:T(8,128)(2,1)S(1)}, bf16[512,128]{1,0:T(8,128)(2,1)S(1)}, u32[]{:S(2)}, u32[]{:S(2)}) collective-permute-start(bf16[512,128]{1,0:T(8,128)(2,1)S(1)} %collective-permute-done.10.rest_4_), channel_id=1, source_target_pairs={{0,4},{4,0},{8,12},{12,8},{16,20},{20,16},{24,28},{28,24},{1,5},{5... | collective-permute-start | bytes 393224 | tf_op jit(solution)/shard_map/ppermute | solution.py:250
  40.8 1.3 %collective-permute-start.12 = (bf16[512,128]{1,0:T(8,128)(2,1)S(1)}, bf16[512,128]{1,0:T(8,128)(2,1)S(1)}, u32[]{:S(2)}, u32[]{:S(2)}) collective-permute-start(bf16[512,128]{1,0:T(8,128)(2,1)S(1)} %collective-permute-done.9.rest_3_), channel_id=1, source_target_pairs={{0,4},{4,0},{8,12},{12,8},{16,20},{20,16},{24,28},{28,24},{1,5},{5... | collective-permute-start | bytes 393224 | tf_op jit(solution)/shard_map/ppermute | solution.py:250
  40.8 1.5 %collective-permute-start.11 = (bf16[512,128]{1,0:T(8,128)(2,1)S(1)}, bf16[512,128]{1,0:T(8,128)(2,1)S(1)}, u32[]{:S(2)}, u32[]{:S(2)}) collective-permute-start(bf16[512,128]{1,0:T(8,128)(2,1)S(1)} %collective-permute-done.8.rest_2_), channel_id=1, source_target_pairs={{0,4},{4,0},{8,12},{12,8},{16,20},{20,16},{24,28},{28,24},{1,5},{5... | collective-permute-start | bytes 393224 | tf_op jit(solution)/shard_map/ppermute | solution.py:250

commit v7 on v6

--- a/solution.py
+++ b/solution.py
@@ -156,7 +156,7 @@
         copy.wait()
     squares[...] = weights_ref[...] * weights_ref[...]
     segment_rows(squares, table, bounds_ref)
-    sums_ref[...] = jnp.sum(table[...].T, axis=0, keepdims=True)
+    sums_ref[...] = jnp.pad(jnp.sum(table[...].T, axis=0, keepdims=True), ((0, 0), (0, LANES - table.shape[0])))
 
 
 def update_kernel(n, bounds_ref, scales_ref, sums_ref, weights_ref, moment1_ref, moment2_ref, *rest):
@@ -184,7 +184,7 @@
 
     lax.fori_loop(0, chunks // rows, block, 0, unroll=2)
     segment_rows(squares, table, bounds_ref)
-    mine = jnp.sum(table[...].T, axis=0, keepdims=True)
+    mine = jnp.pad(jnp.sum(table[...].T, axis=0, keepdims=True), ((0, 0), (0, LANES - table.shape[0])))
     half = (send_ref.shape[0], LANES)
     send_ref[:, :LANES] = jnp.broadcast_to(sums_ref[...], half)
     send_ref[:, LANES:] = jnp.broadcast_to(mine, half)
@@ -216,7 +216,7 @@
     both = jnp.sum(sums_ref[...], axis=0, keepdims=True)
     ratio = jnp.sqrt(both[:, :LANES]) / jnp.maximum(jnp.sqrt(both[:, LANES:]), 1.0)
     ratio = 0.25 * ratio
-    table[...] = jnp.broadcast_to(ratio, (LANES, LANES)).T
+    table[...] = jnp.broadcast_to(ratio, (LANES, LANES)).T[: table.shape[0], :]
 
     def write(part, mine, new):
         new = jnp.where(mine, new, narrow_ref[part, :].astype(jnp.float32))
@@ -279,7 +279,7 @@
     early, late = pieces[: EARLY + 1], pieces[EARLY + 1 :]
     square_table = [
         pltpu.VMEM((chunks, LANES), jnp.float32),
-        pltpu.VMEM((LANES, LANES), jnp.float32),
+        pltpu.VMEM((-(-count // 16) * 16, LANES), jnp.float32),
     ]
     stored = [
         pltpu.with_memory_space_constraint(value.reshape(chunks, LANES), pltpu.HBM)
@@ -315,7 +315,7 @@
     sums = lax.all_to_all(send, ("shard", "tensor"), 0, 0, tiled=True)
     narrow, table = pl.pallas_call(
         narrow_kernel,
-        out_shape=[flat(jnp.bfloat16), jax.ShapeDtypeStruct((LANES, LANES), jnp.float32)],
+        out_shape=[flat(jnp.bfloat16), jax.ShapeDtypeStruct((-(-count // 16) * 16, LANES), jnp.float32)],
         in_specs=[SMEM, VMEM, VMEM, VMEM],
         out_specs=[VMEM] * 2,
         compiler_params=BIG,

time: 43.6 us -> 43.6 us (level)
  no operation moved by 1% of the time
where the time goes in v7:
time: 43.6 us; the launch traced here: 43.4 us
  starting transfers between devices  13.9 us (32%)
  blocking collectives  11.8 us (27%)
  Pallas kernels  9.24 us (21%)
  waiting for transfers between devices  6.41 us (15%)
  between operations  1.38 us (3%)
  local copies, waits for them, and re-layouts  0.69 us (2%)
    ppermute x14, starting transfers between devices, swap(): return lax.ppermute(value, axis, [(i, i ^ k) for i in range(size)])  13.9 us
    all_to_all x1, blocking collectives, local(): sums = lax.all_to_all(send, ('shard', 'tensor'), 0, 0, tiled=True)  11.8 us
    ppermute x14, waiting for transfers between devices, swap(): return lax.ppermute(value, axis, [(i, i ^ k) for i in range(size)])  6.41 us
    pallas_call x1, Pallas kernels, local(): pl.pallas_call(functools.partial(early_kernel, len(early)), out_shape=[fl...  2.54 us
    pallas_call x1, Pallas kernels, local(): pl.pallas_call(functools.partial(split_kernel, n, chunks), out_shape=[fla...  1.7 us
    pallas_call x1, Pallas kernels, local(): pl.pallas_call(store_kernel, out_shape=[flat(jnp.float32)] * 3, in_specs=...  1.51 us
    pallas_call x1, Pallas kernels, local(): pl.pallas_call(functools.partial(update_kernel, len(late)), out_shape=[fl...  1.21 us
    pallas_call x1, Pallas kernels, local(): pl.pallas_call(functools.partial(join_kernel, last), out_shape=[jax.Shape...  1.08 us
  transfers between devices with their start and end apart: 14, of which 7 were waited for; matrix products, arithmetic and copies ran while one was open for 0% of the time, Pallas kernels for 10%

profile of v7, /device:TPU:0, one launch (start us, length us, event | category | flops | bytes accessed | tf_op | source)
XLA Modules:
  0.0 43.4 jit_solution(9953907086926110141)
XLA Ops:
  0.6 1.7 %split.1 = (bf16[512,128]{1,0:T(8,128)(2,1)S(1)}, bf16[512,128]{1,0:T(8,128)(2,1)S(1)}, bf16[512,128]{1,0:T(8,128)(2,1)S(1)}, bf16[512,128]{1,0:T(8,128)(2,1)S(1...) custom-call(bf16[1,512,8,128]{3,2,1,0:T(8,128)(2,1)} %bitcast.18), custom_call_target="tpu_custom_call" | custom-call | tf_op jit(solution)/shard_map/split/pallas_call | solution.py:268
  2.3 3.0 %collective-permute-start = (bf16[512,128]{1,0:T(8,128)(2,1)S(1)}, bf16[512,128]{1,0:T(8,128)(2,1)S(1)}, u32[]{:S(2)}, u32[]{:S(2)}) collective-permute-start(bf16[512,128]{1,0:T(8,128)(2,1)S(1)} %get-tuple-element.34), channel_id=1, source_target_pairs={{0,8},{4,12},{8,0},{12,4},{16,24},{20,28},{24,16},{28,20},{1,9},{5... | collective-permute-start | bytes 393224 | tf_op jit(solution)/shard_map/ppermute | solution.py:250
  5.3 1.5 %collective-permute-start.1 = (bf16[512,128]{1,0:T(8,128)(2,1)S(1)}, bf16[512,128]{1,0:T(8,128)(2,1)S(1)}, u32[]{:S(2)}, u32[]{:S(2)}) collective-permute-start(bf16[512,128]{1,0:T(8,128)(2,1)S(1)} %get-tuple-element.35), channel_id=1, source_target_pairs={{0,16},{4,20},{8,24},{12,28},{16,0},{20,4},{24,8},{28,12},{1,17},{... | collective-permute-start | bytes 393224 | tf_op jit(solution)/shard_map/ppermute | solution.py:250
  6.9 0.0 collective-permute-start.2
  6.9 0.3 collective-permute-start.3
  7.2 2.9 %collective-permute-start.4 = (bf16[512,128]{1,0:T(8,128)(2,1)S(1)}, bf16[512,128]{1,0:T(8,128)(2,1)S(1)}, u32[]{:S(2)}, u32[]{:S(2)}) collective-permute-start(bf16[512,128]{1,0:T(8,128)(2,1)S(1)} %get-tuple-element.45), channel_id=1, source_target_pairs={{0,24},{4,28},{8,16},{12,20},{16,8},{20,12},{24,0},{28,4},{1,25},{... | collective-permute-start | bytes 393224 | tf_op jit(solution)/shard_map/ppermute | solution.py:250
  10.1 0.0 collective-permute-done.rest_1_
  10.1 0.0 collective-permute-start.5
  10.1 0.7 %collective-permute-done.1.rest_2_ = bf16[512,128]{1,0:T(8,128)(2,1)S(1)} collective-permute-done((bf16[512,128]{1,0:T(8,128)(2,1)S(1)}, bf16[512,128]{1,0:T(8,128)(2,1)S(1)}, u32[]{:S(2)}, u32[]{:S(2)}) %collective-permute-start.1) | collective-permute-done | bytes 131104 | tf_op jit(solution)/shard_map/ppermute | solution.py:250
  10.8 2.0 %collective-permute-start.6 = (bf16[512,128]{1,0:T(8,128)(2,1)S(1)}, bf16[512,128]{1,0:T(8,128)(2,1)S(1)}, u32[]{:S(2)}, u32[]{:S(2)}) collective-permute-start(bf16[512,128]{1,0:T(8,128)(2,1)S(1)} %get-tuple-element.47), channel_id=1, source_target_pairs={{0,4},{4,0},{8,12},{12,8},{16,20},{20,16},{24,28},{28,24},{1,5},{5... | collective-permute-start | bytes 393224 | tf_op jit(solution)/shard_map/ppermute | solution.py:250
  13.4 0.0 collective-permute-done.2.rest_3_
  13.5 0.0 copy-start
  13.5 0.6 %copy-done = s32[80]{0:T(128)S(1)} copy-done((s32[80]{0:T(128)S(1)}, s32[80]{0:T(128)}, u32[]{:S(2)}) %copy-start) | copy-done | bytes 344
  14.1 2.5 %early.1 = (f32[512,128]{1,0:T(8,128)S(1)}, f32[512,128]{1,0:T(8,128)S(1)}, f32[512,128]{1,0:T(8,128)S(1)}, f32[512,128]{1,0:T(8,128)S(1)}, f32[1,128]{1,0:T(1,1...) custom-call(s32[1]{0:T(128)S(6)} %copy.16.step_ref, s32[80]{0:T(128)S(1)} %copy-done, f32[512,128]{1,0:T(8,128)} %bitcast.19, ...), custom_call_target="tpu_custom_call" | custom-call | flops 524288 | bytes 1572864 | tf_op jit(solution)/shard_map/early/pallas_call | solution.py:288
  16.7 1.1 %collective-permute-done.3.rest_1_ = bf16[512,128]{1,0:T(8,128)(2,1)S(1)} collective-permute-done((bf16[512,128]{1,0:T(8,128)(2,1)S(1)}, bf16[512,128]{1,0:T(8,128)(2,1)S(1)}, u32[]{:S(2)}, u32[]{:S(2)}) %collective-permute-start.3) | collective-permute-done | bytes 131104 | tf_op jit(solution)/shard_map/ppermute | solution.py:250
  17.8 0.0 collective-permute-done.4.rest_2_
  17.8 0.6 %collective-permute-done.5.rest_3_ = bf16[512,128]{1,0:T(8,128)(2,1)S(1)} collective-permute-done((bf16[512,128]{1,0:T(8,128)(2,1)S(1)}, bf16[512,128]{1,0:T(8,128)(2,1)S(1)}, u32[]{:S(2)}, u32[]{:S(2)}) %collective-permute-start.5) | collective-permute-done | bytes 131104 | tf_op jit(solution)/shard_map/ppermute | solution.py:250
  18.4 0.0 collective-permute-done.6.rest_4_
  18.4 1.2 %update.1 = (f32[512,128]{1,0:T(8,128)S(1)}, f32[512,128]{1,0:T(8,128)S(1)}, f32[512,128]{1,0:T(8,128)S(1)}, f32[32,256]{1,0:T(8,128)S(1)}) custom-call(s32[83]{0:T(128)S(1)} %get-tuple-element.37.bounds_ref, f32[2,128]{1,0:T(2,128)S(1)} %get-tuple-element.38.scales_ref, f32[1,128]{1,0:T(1,128)S(1)} %get-tuple-element.39.sums_ref, ...), custom_call_target="tpu_custom_call" | custom-call | tf_op jit(solution)/shard_map/update/pallas_call | solution.py:305
  19.6 11.8 %all_to_all.11 = f32[32,1,256]{2,1,0:T(1,128)S(1)} all-to-all(f32[32,1,256]{2,1,0:T(1,128)S(1)} %copy.11), channel_id=1, replica_groups=mesh['shard'=8,'tensor'=4] {'shard','tensor'}, dimensions={0} | all-to-all | bytes 65536 | tf_op jit(solution)/shard_map/all_to_all | solution.py:315
  31.4 0.9 %narrow_weights.1 = (bf16[512,128]{1,0:T(8,128)(2,1)S(1)}, f32[80,128]{1,0:T(8,128)S(1)}) custom-call(s32[83]{0:T(128)S(1)} %get-tuple-element.37.bounds_ref, f32[32,256]{1,0:T(8,128)S(1)} %bitcast.16, f32[512,128]{1,0:T(8,128)S(1)} %get-tuple-element.40.weights_ref, f32[512,128]{1,0:T(8,128)S(1)} %get-tuple-element.49.update_ref), custom_call_target="tpu_custom_call" | custom-call | tf_op jit(solution)/shard_map/narrow_weights/pallas_call | solution.py:316
  32.3 0.6 %collective-permute-start.10 = (bf16[512,128]{1,0:T(8,128)(2,1)S(1)}, bf16[512,128]{1,0:T(8,128)(2,1)S(1)}, u32[]{:S(2)}, u32[]{:S(2)}) collective-permute-start(bf16[512,128]{1,0:T(8,128)(2,1)S(1)} %get-tuple-element.60.rest_0_), channel_id=1, source_target_pairs={{0,24},{4,28},{8,16},{12,20},{16,8},{20,12},{24,0},{28,4},{1,25},{... | collective-permute-start | bytes 393224 | tf_op jit(solution)/shard_map/ppermute | solution.py:250
  33.0 1.5 %collective-permute-start.9 = (bf16[512,128]{1,0:T(8,128)(2,1)S(1)}, bf16[512,128]{1,0:T(8,128)(2,1)S(1)}, u32[]{:S(2)}, u32[]{:S(2)}) collective-permute-start(bf16[512,128]{1,0:T(8,128)(2,1)S(1)} %get-tuple-element.60.rest_0_), channel_id=1, source_target_pairs={{0,16},{4,20},{8,24},{12,28},{16,0},{20,4},{24,8},{28,12},{1,17},{... | collective-permute-start | bytes 393224 | tf_op jit(solution)/shard_map/ppermute | solution.py:250
  34.5 1.4 %collective-permute-start.8 = (bf16[512,128]{1,0:T(8,128)(2,1)S(1)}, bf16[512,128]{1,0:T(8,128)(2,1)S(1)}, u32[]{:S(2)}, u32[]{:S(2)}) collective-permute-start(bf16[512,128]{1,0:T(8,128)(2,1)S(1)} %get-tuple-element.60.rest_0_), channel_id=1, source_target_pairs={{0,8},{4,12},{8,0},{12,4},{16,24},{20,28},{24,16},{28,20},{1,9},{5... | collective-permute-start | bytes 393224 | tf_op jit(solution)/shard_map/ppermute | solution.py:250
  35.9 1.5 %store.1 = (f32[512,128]{1,0:T(8,128)}, f32[512,128]{1,0:T(8,128)}, f32[512,128]{1,0:T(8,128)}) custom-call(s32[83]{0:T(128)S(1)} %get-tuple-element.37.bounds_ref, f32[80,128]{1,0:T(8,128)S(1)} %get-tuple-element.50.table, f32[512,128]{1,0:T(8,128)S(1)} %get-tuple-element.40.weights_ref, f32[512,128]{1,0:T(8,128)S(1)} %get-tuple-element.49.update_ref, ...), custom_call_target="tpu_custom_call" | custom-call | flops 262144 | bytes 1310720 | tf_op jit(solution)/shard_map/store/pallas_call | solution.py:327
  37.4 0.1 collective-permute-start.7
  37.5 2.2 %collective-permute-done.10.rest_4_ = bf16[512,128]{1,0:T(8,128)(2,1)S(1)} collective-permute-done((bf16[512,128]{1,0:T(8,128)(2,1)S(1)}, bf16[512,128]{1,0:T(8,128)(2,1)S(1)}, u32[]{:S(2)}, u32[]{:S(2)}) %collective-permute-start.10) | collective-permute-done | bytes 131104 | tf_op jit(solution)/shard_map/ppermute | solution.py:250
  39.7 0.0 collective-permute-start.13
  39.7 1.1 %collective-permute-done.9.rest_3_ = bf16[512,128]{1,0:T(8,128)(2,1)S(1)} collective-permute-done((bf16[512,128]{1,0:T(8,128)(2,1)S(1)}, bf16[512,128]{1,0:T(8,128)(2,1)S(1)}, u32[]{:S(2)}, u32[]{:S(2)}) %collective-permute-start.9) | collective-permute-done | bytes 131104 | tf_op jit(solution)/shard_map/ppermute | solution.py:250
  40.8 0.0 collective-permute-start.12
  40.8 0.0 collective-permute-done.8.rest_2_
  40.8 0.5 %collective-permute-start.11 = (bf16[512,128]{1,0:T(8,128)(2,1)S(1)}, bf16[512,128]{1,0:T(8,128)(2,1)S(1)}, u32[]{:S(2)}, u32[]{:S(2)}) collective-permute-start(bf16[512,128]{1,0:T(8,128)(2,1)S(1)} %collective-permute-done.8.rest_2_), channel_id=1, source_target_pairs={{0,4},{4,0},{8,12},{12,8},{16,20},{20,16},{24,28},{28,24},{1,5},{5... | collective-permute-start | bytes 393224 | tf_op jit(solution)/shard_map/ppermute | solution.py:250
  41.3 0.0 collective-permute-done.7.rest_1_
  41.3 0.3 lay.1.rest_0_
  41.6 0.0 collective-permute-done.13.rest_3_
  41.6 0.5 %collective-permute-done.12.rest_2_ = bf16[512,128]{1,0:T(8,128)(2,1)S(1)} collective-permute-done((bf16[512,128]{1,0:T(8,128)(2,1)S(1)}, bf16[512,128]{1,0:T(8,128)(2,1)S(1)}, u32[]{:S(2)}, u32[]{:S(2)}) %collective-permute-start.12) | collective-permute-done | bytes 131104 | tf_op jit(solution)/shard_map/ppermute | solution.py:250
  42.2 0.2 collective-permute-done.11.rest_1_
  42.3 1.1 %join.1 = (bf16[1,512,8,128]{3,2,1,0:T(8,128)(2,1)}, f32[8,512,128]{2,1,0:T(8,128)S(1)}) custom-call(f32[8,512,128]{2,1,0:T(8,128)S(1)} %lay.1.rest_0_, bf16[512,128]{1,0:T(8,128)(2,1)S(1)} %collective-permute-done.11.rest_1_, bf16[512,128]{1,0:T(8,128)(2,1)S(1)} %collective-permute-done.12.rest_2_, ...), custom_call_target="tpu_custom_call", output_to_operand_aliasing={{1}: (0, {})} | custom-call | tf_op jit(solution)/shard_map/join/pallas_call | solution.py:359
  (2 shorter events, 0.0 us)
Async XLA Ops:
  2.3 7.7 %collective-permute-start = (bf16[512,128]{1,0:T(8,128)(2,1)S(1)}, bf16[512,128]{1,0:T(8,128)(2,1)S(1)}, u32[]{:S(2)}, u32[]{:S(2)}) collective-permute-start(bf16[512,128]{1,0:T(8,128)(2,1)S(1)} %get-tuple-element.34), channel_id=1, source_target_pairs={{0,8},{4,12},{8,0},{12,4},{16,24},{20,28},{24,16},{28,20},{1,9},{5... | collective-permute-start | bytes 393224 | tf_op jit(solution)/shard_map/ppermute | solution.py:250
  5.3 5.4 %collective-permute-start.1 = (bf16[512,128]{1,0:T(8,128)(2,1)S(1)}, bf16[512,128]{1,0:T(8,128)(2,1)S(1)}, u32[]{:S(2)}, u32[]{:S(2)}) collective-permute-start(bf16[512,128]{1,0:T(8,128)(2,1)S(1)} %get-tuple-element.35), channel_id=1, source_target_pairs={{0,16},{4,20},{8,24},{12,28},{16,0},{20,4},{24,8},{28,12},{1,17},{... | collective-permute-start | bytes 393224 | tf_op jit(solution)/shard_map/ppermute | solution.py:250
  6.9 6.6 %collective-permute-start.2 = (bf16[512,128]{1,0:T(8,128)(2,1)S(1)}, bf16[512,128]{1,0:T(8,128)(2,1)S(1)}, u32[]{:S(2)}, u32[]{:S(2)}) collective-permute-start(bf16[512,128]{1,0:T(8,128)(2,1)S(1)} %get-tuple-element.36), channel_id=1, source_target_pairs={{0,12},{4,8},{8,4},{12,0},{16,28},{20,24},{24,20},{28,16},{1,13},{... | collective-permute-start | bytes 393224 | tf_op jit(solution)/shard_map/ppermute | solution.py:250
  6.9 10.9 %collective-permute-start.3 = (bf16[512,128]{1,0:T(8,128)(2,1)S(1)}, bf16[512,128]{1,0:T(8,128)(2,1)S(1)}, u32[]{:S(2)}, u32[]{:S(2)}) collective-permute-start(bf16[512,128]{1,0:T(8,128)(2,1)S(1)} %get-tuple-element.44), channel_id=1, source_target_pairs={{0,20},{4,16},{8,28},{12,24},{16,4},{20,0},{24,12},{28,8},{1,21},{... | collective-permute-start | bytes 393224 | tf_op jit(solution)/shard_map/ppermute | solution.py:250
  7.2 10.6 %collective-permute-start.4 = (bf16[512,128]{1,0:T(8,128)(2,1)S(1)}, bf16[512,128]{1,0:T(8,128)(2,1)S(1)}, u32[]{:S(2)}, u32[]{:S(2)}) collective-permute-start(bf16[512,128]{1,0:T(8,128)(2,1)S(1)} %get-tuple-element.45), channel_id=1, source_target_pairs={{0,24},{4,28},{8,16},{12,20},{16,8},{20,12},{24,0},{28,4},{1,25},{... | collective-permute-start | bytes 393224 | tf_op jit(solution)/shard_map/ppermute | solution.py:250
  10.1 8.3 %collective-permute-start.5 = (bf16[512,128]{1,0:T(8,128)(2,1)S(1)}, bf16[512,128]{1,0:T(8,128)(2,1)S(1)}, u32[]{:S(2)}, u32[]{:S(2)}) collective-permute-start(bf16[512,128]{1,0:T(8,128)(2,1)S(1)} %get-tuple-element.46), channel_id=1, source_target_pairs={{0,28},{4,24},{8,20},{12,16},{16,12},{20,8},{24,4},{28,0},{1,29},{... | collective-permute-start | bytes 393224 | tf_op jit(solution)/shard_map/ppermute | solution.py:250
  10.8 7.6 %collective-permute-start.6 = (bf16[512,128]{1,0:T(8,128)(2,1)S(1)}, bf16[512,128]{1,0:T(8,128)(2,1)S(1)}, u32[]{:S(2)}, u32[]{:S(2)}) collective-permute-start(bf16[512,128]{1,0:T(8,128)(2,1)S(1)} %get-tuple-element.47), channel_id=1, source_target_pairs={{0,4},{4,0},{8,12},{12,8},{16,20},{20,16},{24,28},{28,24},{1,5},{5... | collective-permute-start | bytes 393224 | tf_op jit(solution)/shard_map/ppermute | solution.py:250
  13.5 0.7 %copy-start = (s32[80]{0:T(128)S(1)}, s32[80]{0:T(128)}, u32[]{:S(2)}) copy-start(s32[80]{0:T(128)} %lengths_ref.1) | copy-start | bytes 964
  32.3 7.4 %collective-permute-start.10 = (bf16[512,128]{1,0:T(8,128)(2,1)S(1)}, bf16[512,128]{1,0:T(8,128)(2,1)S(1)}, u32[]{:S(2)}, u32[]{:S(2)}) collective-permute-start(bf16[512,128]{1,0:T(8,128)(2,1)S(1)} %get-tuple-element.60.rest_0_), channel_id=1, source_target_pairs={{0,24},{4,28},{8,16},{12,20},{16,8},{20,12},{24,0},{28,4},{1,25},{... | collective-permute-start | bytes 393224 | tf_op jit(solution)/shard_map/ppermute | solution.py:250
  33.0 7.9 %collective-permute-start.9 = (bf16[512,128]{1,0:T(8,128)(2,1)S(1)}, bf16[512,128]{1,0:T(8,128)(2,1)S(1)}, u32[]{:S(2)}, u32[]{:S(2)}) collective-permute-start(bf16[512,128]{1,0:T(8,128)(2,1)S(1)} %get-tuple-element.60.rest_0_), channel_id=1, source_target_pairs={{0,16},{4,20},{8,24},{12,28},{16,0},{20,4},{24,8},{28,12},{1,17},{... | collective-permute-start | bytes 393224 | tf_op jit(solution)/shard_map/ppermute | solution.py:250
  34.5 6.4 %collective-permute-start.8 = (bf16[512,128]{1,0:T(8,128)(2,1)S(1)}, bf16[512,128]{1,0:T(8,128)(2,1)S(1)}, u32[]{:S(2)}, u32[]{:S(2)}) collective-permute-start(bf16[512,128]{1,0:T(8,128)(2,1)S(1)} %get-tuple-element.60.rest_0_), channel_id=1, source_target_pairs={{0,8},{4,12},{8,0},{12,4},{16,24},{20,28},{24,16},{28,20},{1,9},{5... | collective-permute-start | bytes 393224 | tf_op jit(solution)/shard_map/ppermute | solution.py:250
  37.4 3.9 %collective-permute-start.7 = (bf16[512,128]{1,0:T(8,128)(2,1)S(1)}, bf16[512,128]{1,0:T(8,128)(2,1)S(1)}, u32[]{:S(2)}, u32[]{:S(2)}) collective-permute-start(bf16[512,128]{1,0:T(8,128)(2,1)S(1)} %get-tuple-element.60.rest_0_), channel_id=1, source_target_pairs={{0,4},{4,0},{8,12},{12,8},{16,20},{20,16},{24,28},{28,24},{1,5},{5... | collective-permute-start | bytes 393224 | tf_op jit(solution)/shard_map/ppermute | solution.py:250
  39.7 1.9 %collective-permute-start.13 = (bf16[512,128]{1,0:T(8,128)(2,1)S(1)}, bf16[512,128]{1,0:T(8,128)(2,1)S(1)}, u32[]{:S(2)}, u32[]{:S(2)}) collective-permute-start(bf16[512,128]{1,0:T(8,128)(2,1)S(1)} %collective-permute-done.10.rest_4_), channel_id=1, source_target_pairs={{0,4},{4,0},{8,12},{12,8},{16,20},{20,16},{24,28},{28,24},{1,5},{5... | collective-permute-start | bytes 393224 | tf_op jit(solution)/shard_map/ppermute | solution.py:250
  40.8 1.3 %collective-permute-start.12 = (bf16[512,128]{1,0:T(8,128)(2,1)S(1)}, bf16[512,128]{1,0:T(8,128)(2,1)S(1)}, u32[]{:S(2)}, u32[]{:S(2)}) collective-permute-start(bf16[512,128]{1,0:T(8,128)(2,1)S(1)} %collective-permute-done.9.rest_3_), channel_id=1, source_target_pairs={{0,4},{4,0},{8,12},{12,8},{16,20},{20,16},{24,28},{28,24},{1,5},{5... | collective-permute-start | bytes 393224 | tf_op jit(solution)/shard_map/ppermute | solution.py:250
  40.8 1.5 %collective-permute-start.11 = (bf16[512,128]{1,0:T(8,128)(2,1)S(1)}, bf16[512,128]{1,0:T(8,128)(2,1)S(1)}, u32[]{:S(2)}, u32[]{:S(2)}) collective-permute-start(bf16[512,128]{1,0:T(8,128)(2,1)S(1)} %collective-permute-done.8.rest_2_), channel_id=1, source_target_pairs={{0,4},{4,0},{8,12},{12,8},{16,20},{20,16},{24,28},{28,24},{1,5},{5... | collective-permute-start | bytes 393224 | tf_op jit(solution)/shard_map/ppermute | solution.py:250
